TPU v7x, 512 devices: a whole 4x8x8 slice. The times are simulated.
512 devices in a mesh: dp: 16 (over y, z_lo), tensor: 32 (over z_hi, x, core).
Axes of the slice: x: 4, y: 8, z: 8 (z_hi: 4, z_lo: 2; z = z_hi * 2 + z_lo), core: 2. Of those that a mesh axis runs over, the one named last changes fastest.
Arguments:
- hidden_in: bfloat16 [16, 32, 1, 64, 1536], P('dp', 'tensor'), may hold values from -6 to 6
- rotated_queries: bfloat16 [16, 32, 1, 64, 1536], P('dp', 'tensor'), may hold values from -8 to 8
- fresh_key_values: bfloat16 [16, 32, 1, 64, 1024], P('dp', 'tensor'), may hold values from -6 to 6
- cached_key_values: bfloat16 [16, 1024, 1024], P('dp', 'tensor'), may hold values from -8 to 8
- cached_len: int32 [16], P('dp'), may hold values from 8 to 1024, as said below
- expert_ids: int32 [16, 32, 1, 64, 8], P('dp', 'tensor'), may hold values from 0 to 31, all different within a row; in each aligned block of 64 rows (0 to 63, 64 to 127, ..., all dimensions but the last counted through in order) at most 17 rows name the same one
- route_gates: float32 [16, 32, 1, 64, 8], P('dp', 'tensor'), may hold values from 0.1 to 0.4
- output_weight: bfloat16 [1536, 1536], P('tensor'), may hold values from -3 to 3
- norm_gain: float32 [1536], replicated, may hold values from 0.1 to 1.9
- gate_up: bfloat16 [32, 1536, 1024], P('tensor', 'dp'), may hold values from -0.15625 to 0.15625
- down_weight: bfloat16 [32, 512, 1536], P('tensor', 'dp'), may hold values from -0.25 to 0.25
Outputs:
- hidden_out: bfloat16 [16, 32, 1, 64, 1536], P('dp', 'tensor')
- cache_out: bfloat16 [16, 3072, 1024], P('dp', None, 'tensor')
Inputs may be any that keep to these rules, and one draw needn't show every extreme that they name: `cached_len`: some request has exactly 1024 valid slots. `expert_ids`: among the 64 tokens of one device no expert is chosen more than 17 times, and on some device some expert is chosen exactly 17 times.
All inputs are finite; a program needn't handle non-finite values.
Results may differ from a plain program's by a relative error of at most 0.006.
Values may be sent and summed in bfloat16 or wider, within the bound.
No kernel may reach another device: no remote copies, remote signals or barrier semaphores. Data moves between devices by JAX's collectives and lax.ppermute only.
A program may use at most 64 MiB of HBM per device.

v0:
```python
import math

import jax
import jax.numpy as jnp
from jax import lax
from jax.sharding import PartitionSpec as P

MODEL_WIDTH = 1536
QUERY_HEADS = 24
KEY_VALUE_HEADS = 8
HEAD_WIDTH = 64
FFE = 512
TOPK = 8


epsilon = 1e-05


def partner_2(block, axis, stride):
    count = lax.axis_size(axis)
    route = []
    for low in range(count):
        high = low | 1 << stride
        if high != low and high < count:
            route += [(low, high), (high, low)]
    return lax.ppermute(block, axis, route)


def joined_rows(blocks, head_fourths, position):
    for which_bit in range(head_fourths.bit_length() - 1):
        partner = partner_2(blocks, "tensor", which_bit)
        low_side = position >> which_bit & 1 == 0
        blocks = jnp.where(
            low_side, jnp.concatenate([blocks, partner], 0), jnp.concatenate([partner, blocks], 0)
        )
    return blocks


def head_layout(local, head_fourths, sub_len):
    request_list, unused_len, heads, last_width = local.shape
    shaped = local.reshape(request_list, head_fourths, sub_len, heads, last_width)
    return jnp.transpose(shaped, (3, 1, 0, 2, 4)).reshape(
        heads * head_fourths, request_list, sub_len, last_width
    )


def attend_request(queries_req, pairs_req, cache_total, length, query_pos):
    row_count = queries_req.shape[0]
    block_rows = math.gcd(row_count, 512)
    block_count = row_count // block_rows
    key_pos = jnp.arange(pairs_req.shape[0], dtype=jnp.int32)
    keys_all = pairs_req[:, :HEAD_WIDTH]
    values_all = pairs_req[:, HEAD_WIDTH:]

    def one_block(packed):
        query_block, pos_block = packed
        scores = lax.dot_general(
            query_block, keys_all, (((1,), (1,)), ((), ())), preferred_element_type=jnp.float32
        ) * (1.0 / math.sqrt(HEAD_WIDTH))
        visible = jnp.where(
            key_pos[None, :] < cache_total,
            key_pos[None, :] < length,
            key_pos[None, :] - cache_total <= pos_block[:, None],
        )
        scores = jnp.where(visible, scores, -1e30)
        highest = jnp.max(scores, 1, keepdims=True)
        weights = jnp.where(visible, jnp.exp(scores - highest), 0.0)
        denoms = jnp.sum(weights, 1, keepdims=True)
        mixed_output = (
            jnp.dot(weights.astype(jnp.bfloat16), values_all, preferred_element_type=jnp.float32)
            / denoms
        )
        return mixed_output.astype(jnp.bfloat16)

    mixed_output = lax.map(
        one_block,
        (
            queries_req.reshape(block_count, block_rows, HEAD_WIDTH),
            query_pos.reshape(block_count, block_rows),
        ),
    )
    return mixed_output.reshape(row_count, HEAD_WIDTH)


def shards(
    hidden_in,
    rotated_queries,
    fresh_key_values,
    cached_key_values,
    cached_len,
    expert_ids,
    route_gates,
    output_weight,
    norm_gain,
    gate_up,
    down_weight,
):
    device_list = lax.axis_size("tensor")
    head_fourths = device_list // KEY_VALUE_HEADS
    query_groups = QUERY_HEADS // KEY_VALUE_HEADS
    request_list = rotated_queries.shape[2]
    request_results = rotated_queries.shape[3]
    cache_row_list = cached_key_values.shape[1]
    partial_rows = request_results // head_fourths
    key_value_width = 2 * HEAD_WIDTH
    cache_total = device_list * cache_row_list
    new_total = device_list * request_results
    position = lax.axis_index("tensor")
    quarter = position % head_fourths
    query_shard = rotated_queries[0, 0].reshape(
        request_list, request_results, KEY_VALUE_HEADS, query_groups * HEAD_WIDTH
    )
    query_send = head_layout(query_shard, head_fourths, partial_rows)
    fresh_shard = fresh_key_values[0, 0].reshape(
        request_list, request_results, KEY_VALUE_HEADS, key_value_width
    )
    cache_shard = cached_key_values.reshape(
        request_list, cache_row_list, KEY_VALUE_HEADS, key_value_width
    )
    fresh_copy = jnp.broadcast_to(
        jnp.transpose(fresh_shard, (2, 0, 1, 3))[:, None],
        (KEY_VALUE_HEADS, head_fourths, request_list, request_results, key_value_width),
    )
    cache_copy = jnp.broadcast_to(
        jnp.transpose(cache_shard, (2, 0, 1, 3))[:, None],
        (KEY_VALUE_HEADS, head_fourths, request_list, cache_row_list, key_value_width),
    )
    pairs_send = jnp.concatenate([cache_copy, fresh_copy], 3).reshape(
        device_list, request_list, cache_row_list + request_results, key_value_width
    )
    query_got, pairs_got = (
        lax.all_to_all(query_send, "tensor", split_axis=0, concat_axis=0, tiled=True),
        lax.all_to_all(pairs_send, "tensor", split_axis=0, concat_axis=0, tiled=True),
    )
    cache_head = jnp.transpose(pairs_got[:, :, :cache_row_list], (1, 0, 2, 3)).reshape(
        request_list, cache_total, key_value_width
    )
    fresh_head = jnp.transpose(pairs_got[:, :, cache_row_list:], (1, 0, 2, 3)).reshape(
        request_list, new_total, key_value_width
    )
    query_pos = (
        jnp.arange(device_list, dtype=jnp.int32)[:, None] * request_results
        + quarter * partial_rows
        + jnp.arange(partial_rows, dtype=jnp.int32)[None, :]
    )
    query_pos = jnp.broadcast_to(
        query_pos[:, :, None], (device_list, partial_rows, query_groups)
    ).reshape(-1)
    col_width = key_value_width // head_fourths
    context = jnp.arange(cache_total + new_total, dtype=jnp.int32)
    length = cached_len[0]
    pairs_req = jnp.concatenate([cache_head[0], fresh_head[0]], 0)
    queries_req = query_got[:, 0].reshape(device_list * partial_rows * query_groups, HEAD_WIDTH)
    attended_all = [
        attend_request(queries_req, pairs_req, cache_total, length, query_pos).reshape(
            device_list, partial_rows, query_groups * HEAD_WIDTH
        )
    ]
    old_cols = lax.dynamic_slice_in_dim(cache_head[0], quarter * col_width, col_width, 1)
    new_cols = lax.dynamic_slice_in_dim(fresh_head[0], quarter * col_width, col_width, 1)
    base_rows = jnp.concatenate([old_cols, jnp.zeros((new_total, col_width), old_cols.dtype)], 0)
    base_rows = jnp.where((context < length)[:, None], base_rows, jnp.zeros_like(base_rows))
    appended_all = [lax.dynamic_update_slice_in_dim(base_rows, new_cols, length, 0)]
    attention_result = jnp.stack(attended_all, 0)
    cache_out = jnp.stack(appended_all, 0)
    head_weight = joined_rows(output_weight[None], head_fourths, position).reshape(
        query_groups * HEAD_WIDTH, MODEL_WIDTH
    )
    head_sums = jnp.dot(
        attention_result.reshape(-1, query_groups * HEAD_WIDTH),
        head_weight,
        preferred_element_type=jnp.float32,
    ).astype(jnp.bfloat16)
    head_sums = jnp.transpose(
        head_sums.reshape(request_list, device_list, partial_rows, MODEL_WIDTH), (1, 0, 2, 3)
    )
    incoming_rows = lax.all_to_all(head_sums, "tensor", split_axis=0, concat_axis=0, tiled=True)
    total_output = jnp.sum(
        incoming_rows.reshape(
            KEY_VALUE_HEADS, head_fourths, request_list, partial_rows, MODEL_WIDTH
        ).astype(jnp.float32),
        0,
    )
    attention_sum = jnp.transpose(total_output, (1, 0, 2, 3)).reshape(
        request_list, request_results, MODEL_WIDTH
    )
    residual = hidden_in[0, 0].astype(jnp.float32) + attention_sum
    meansq = jnp.mean(residual * residual, -1, keepdims=True)
    tokens_dev = request_list * request_results
    normed = (
        (residual * lax.rsqrt(meansq + epsilon) * norm_gain)
        .astype(jnp.bfloat16)
        .reshape(tokens_dev, MODEL_WIDTH)
    )
    capacity = min(
        tokens_dev,
        tokens_dev * TOPK // device_list + max(1, tokens_dev * TOPK // (32 * device_list)),
    )
    ids_flat = expert_ids[0, 0].reshape(-1)
    onehot = (ids_flat[:, None] == jnp.arange(device_list, dtype=jnp.int32)[None, :]).astype(
        jnp.int32
    )
    slot_rank = jnp.sum(onehot * (jnp.cumsum(onehot, 0) - onehot), 1)
    slot_index = ids_flat * capacity + slot_rank
    token_index = jnp.arange(tokens_dev * TOPK, dtype=jnp.int32) // TOPK
    outbound_rows = (
        jnp.zeros((device_list * capacity, MODEL_WIDTH), jnp.bfloat16)
        .at[slot_index]
        .set(normed[token_index])
        .reshape(device_list, capacity, MODEL_WIDTH)
    )
    full_gate_up, full_down = (
        lax.all_gather(gate_up, "dp", axis=1, tiled=True),
        lax.all_gather(down_weight, "dp", axis=1, tiled=True),
    )
    slots_in = lax.all_to_all(outbound_rows, "tensor", split_axis=0, concat_axis=0, tiled=True)
    flat_rows = slots_in.reshape(-1, MODEL_WIDTH)
    hidden_units = jnp.dot(flat_rows, full_gate_up[0], preferred_element_type=jnp.float32)
    active = (jax.nn.silu(hidden_units[:, :FFE]) * hidden_units[:, FFE:]).astype(jnp.bfloat16)
    outputs = jnp.dot(active, full_down[0], preferred_element_type=jnp.float32).astype(jnp.bfloat16)
    computed = outputs.reshape(slots_in.shape)
    returned = lax.all_to_all(computed, "tensor", split_axis=0, concat_axis=0, tiled=True)
    picked = returned.reshape(device_list * capacity, MODEL_WIDTH)[slot_index].reshape(
        tokens_dev, TOPK, MODEL_WIDTH
    )
    gates_local = route_gates[0, 0].reshape(tokens_dev, TOPK)
    mixture = jnp.sum(gates_local[:, :, None] * picked.astype(jnp.float32), 1)
    hidden_out = (
        (residual.reshape(tokens_dev, MODEL_WIDTH) + mixture)
        .astype(jnp.bfloat16)
        .reshape(1, 1, request_list, request_results, MODEL_WIDTH)
    )
    return (hidden_out, cache_out)


def solution(mesh):
    return jax.shard_map(
        shards,
        mesh=mesh,
        in_specs=(
            P("dp", "tensor", None, None, None),
            P("dp", "tensor", None, None, None),
            P("dp", "tensor", None, None, None),
            P("dp", "tensor", None),
            P("dp"),
            P("dp", "tensor", None, None, None),
            P("dp", "tensor", None, None, None),
            P("tensor", None),
            P(),
            P("tensor", "dp", None),
            P("tensor", "dp", None),
        ),
        out_specs=(P("dp", "tensor", None, None, None), P("dp", None, "tensor")),
        check_vma=False,
    )
```

profile of v0, /device:TPU:1, one launch (start us, length us, event | category | flops | bytes accessed | tf_op | source)
XLA Modules:
  0.0 362.6 jit_solution(2532485472738883430)
XLA Ops:
  9.1 14.4 %all-to-all-start = ((bf16[32,1,16,192]{3,2,1,0:T(8,128)(2,1)}), bf16[32,1,16,192]{3,2,1,0:T(8,128)(2,1)S(1)}, u32[]{:S(2)}, u32[]{:S(2)}) async-start(bf16[32,1,16,192]{3,2,1,0:T(8,128)(2,1)} %bitcast.2), calls=%async_computation | async-start | bytes 524288 | tf_op jit(solution)/shard_map/all_to_all | solution.py:132
  25.7 11.5 %all-to-all-done = bf16[32,1,16,192]{3,2,1,0:T(8,128)(2,1)S(1)} async-done(((bf16[32,1,16,192]{3,2,1,0:T(8,128)(2,1)}), bf16[32,1,16,192]{3,2,1,0:T(8,128)(2,1)S(1)}, u32[]{:S(2)}, u32[]{:S(2)}) %all-to-all-start) | async-done | bytes 196640 | tf_op jit(solution)/shard_map/all_to_all | solution.py:132
  37.3 3.7 %all-to-all-start.1 = ((bf16[32,1,96,128]{3,2,1,0:T(8,128)(2,1)}), bf16[32,1,96,128]{3,2,1,0:T(8,128)(2,1)S(1)}, u32[]{:S(2)}, u32[]{:S(2)}) async-start(bf16[32,1,96,128]{3,2,1,0:T(8,128)(2,1)} %bitcast.7), calls=%async_computation.1 | async-start | bytes 1572864 | tf_op jit(solution)/shard_map/all_to_all | solution.py:133
  44.3 3.0 collective-permute-start.1
  48.0 11.3 %collective-permute-done.1 = bf16[2,48,1536]{2,1,0:T(8,128)(2,1)S(1)} collective-permute-done((bf16[2,48,1536]{2,1,0:T(8,128)(2,1)S(1)}, bf16[2,48,1536]{2,1,0:T(8,128)(2,1)S(1)}, u32[]{:S(2)}, u32[]{:S(2)}) %collective-permute-start.1) | collective-permute-done | bytes 294944 | tf_op jit(solution)/shard_map/ppermute | solution.py:26
  59.4 2.7 all-to-all-done.1
  62.5 20.9 %while.14 = (s32[]{:T(128)}, bf16[3,512,64]{1,2,0:T(8,128)(2,1)S(1)}, s32[]{:T(128)}, s32[3,512]{1,0:T(4,128)S(1)}, bf16[3,512,64]{2,1,0:T(8,128)(2,1)S(1)}, /*i...) while((s32[]{:T(128)}, bf16[3,512,64]{1,2,0:T(8,128)(2,1)S(1)}, ...), condition=%wide.region_3.4_spmd.clone.clone, body=%wide.region_0.3_spmd.clone.clone.sunk | while | flops 426319872 | bytes 20738148 | solution.py:75
  64.9 2.5 fusion.58
  67.5 2.0 fusion.59
  71.9 2.5 fusion.58
  78.9 2.5 fusion.58
  81.4 2.0 fusion.59
  85.7 6.6 %all-to-all-start.2 = ((bf16[32,1,16,1536]{3,2,1,0:T(8,128)(2,1)}), bf16[32,1,16,1536]{3,2,1,0:T(8,128)(2,1)S(1)}, u32[]{:S(2)}, u32[]{:S(2)}) async-start(bf16[32,1,16,1536]{3,2,1,0:T(8,128)(2,1)} %bitcast.14), calls=%async_computation.2 | async-start | bytes 3145728 | tf_op jit(solution)/shard_map/all_to_all | solution.py:177
  94.4 68.3 %all-to-all-done.2 = bf16[32,1,16,1536]{3,2,1,0:T(8,128)(2,1)S(1)} async-done(((bf16[32,1,16,1536]{3,2,1,0:T(8,128)(2,1)}), bf16[32,1,16,1536]{3,2,1,0:T(8,128)(2,1)S(1)}, u32[]{:S(2)}, u32[]{:S(2)}) %all-to-all-start.2) | async-done | bytes 1572896 | tf_op jit(solution)/shard_map/all_to_all | solution.py:177
  163.2 8.6 %scatter_custom_fusion = bf16[544,1536]{1,0:T(8,128)(2,1)S(1)} fusion(s32[512]{0:T(512)S(1)} %bitcast.148, bf16[64,1536]{1,0:T(8,128)(2,1)S(1)} %fusion.35, s32[1024]{0:T(1024)S(1)} %pad_clamp_fusion.1, bf16[]{:T(256)} %constant.101.clone.1), kind=kCustom, calls=%fused_computation.30 | custom fusion | bytes 1671170 | tf_op jit(solution)/shard_map/scatter | solution.py:209
  173.5 6.9 %all-to-all-start.3 = ((bf16[32,17,1536]{2,1,0:T(8,128)(2,1)}), bf16[32,17,1536]{2,1,0:T(8,128)(2,1)S(1)}, u32[]{:S(2)}, u32[]{:S(2)}) async-start(bf16[32,17,1536]{2,1,0:T(8,128)(2,1)} %reshape.282), calls=%async_computation.3 | async-start | bytes 4718592 | tf_op jit(solution)/shard_map/all_to_all | solution.py:216
  181.2 76.6 %all-to-all-done.3 = bf16[32,17,1536]{2,1,0:T(8,128)(2,1)S(1)} async-done(((bf16[32,17,1536]{2,1,0:T(8,128)(2,1)}), bf16[32,17,1536]{2,1,0:T(8,128)(2,1)S(1)}, u32[]{:S(2)}, u32[]{:S(2)}) %all-to-all-start.3) | async-done | bytes 1671200 | tf_op jit(solution)/shard_map/all_to_all | solution.py:216
  259.3 5.7 %fusion.23 = f32[544,1024]{1,0:T(8,128)} fusion(bf16[544,1536]{1,0:T(8,128)(2,1)} %reshape.283, bf16[1,1536,1024]{2,1,0:T(8,128)(2,1)} %all-gather.3.cloned.1.call-done), kind=kOutput, calls=%fused_computation.25 | convolution fusion | flops 1711276032 | bytes 7045120 | tf_op jit(solution)/shard_map/dot_general | solution.py:218
  265.0 6.5 %all-gather.5.cloned.1.call-done = bf16[1,512,1536]{2,1,0:T(8,128)(2,1)} async-done(((bf16[1,32,1536]{2,1,0:T(8,128)(2,1)}), bf16[1,512,1536]{2,1,0:T(8,128)(2,1)}) %all-gather.5.cloned.1.call-update) | async-done | bytes 1572880 | tf_op jit(solution)/shard_map/all_gather | solution.py:214
  271.5 3.1 convolution_convert_fusion
  276.4 14.2 %all-to-all-start.4 = ((bf16[32,17,1536]{2,1,0:T(8,128)(2,1)}), bf16[32,17,1536]{2,1,0:T(8,128)(2,1)}, u32[]{:S(2)}, u32[]{:S(2)}) async-start(bf16[32,17,1536]{2,1,0:T(8,128)(2,1)} %reshape.284), calls=%async_computation.4 | async-start | bytes 4718592 | tf_op jit(solution)/shard_map/all_to_all | solution.py:222
  295.8 51.4 %all-to-all-done.4 = bf16[32,17,1536]{2,1,0:T(8,128)(2,1)} async-done(((bf16[32,17,1536]{2,1,0:T(8,128)(2,1)}), bf16[32,17,1536]{2,1,0:T(8,128)(2,1)}, u32[]{:S(2)}, u32[]{:S(2)}) %all-to-all-start.4) | async-done | bytes 1671200 | tf_op jit(solution)/shard_map/all_to_all | solution.py:222
  349.2 3.0 gather_fusion
  352.1 2.9 fusion.22
  (91 shorter events, 35.4 us)
Async XLA Ops:
  7.2 17.4 %copy-start.3 = (bf16[1,32,1024]{2,1,0:T(8,128)(2,1)S(1)}, bf16[1,32,1024]{2,1,0:T(8,128)(2,1)}, u32[]{:S(2)}) copy-start(bf16[1,32,1024]{2,1,0:T(8,128)(2,1)} %param.16) | copy-start | bytes 196612
  9.1 28.1 %all-to-all-start = ((bf16[32,1,16,192]{3,2,1,0:T(8,128)(2,1)}), bf16[32,1,16,192]{3,2,1,0:T(8,128)(2,1)S(1)}, u32[]{:S(2)}, u32[]{:S(2)}) async-start(bf16[32,1,16,192]{3,2,1,0:T(8,128)(2,1)} %bitcast.2), calls=%async_computation | async-start | bytes 524288 | tf_op jit(solution)/shard_map/all_to_all | solution.py:132
  24.7 16.3 %copy-start.2 = (bf16[48,1536]{1,0:T(8,128)(2,1)S(1)}, bf16[48,1536]{1,0:T(8,128)(2,1)}, u32[]{:S(2)}) copy-start(bf16[48,1536]{1,0:T(8,128)(2,1)} %param.20) | copy-start | bytes 442372
  37.3 24.8 %all-to-all-start.1 = ((bf16[32,1,96,128]{3,2,1,0:T(8,128)(2,1)}), bf16[32,1,96,128]{3,2,1,0:T(8,128)(2,1)S(1)}, u32[]{:S(2)}, u32[]{:S(2)}) async-start(bf16[32,1,96,128]{3,2,1,0:T(8,128)(2,1)} %bitcast.7), calls=%async_computation.1 | async-start | bytes 1572864 | tf_op jit(solution)/shard_map/all_to_all | solution.py:133
  41.0 218.4 %all-gather.3.cloned.1.call-start = ((), (), s32[]{:S(2)}) async-start(), calls=%async_computation.5 | async-start | bytes 3342336 | tf_op jit(solution)/shard_map/all_gather | solution.py:213
  41.0 3.3 collective-permute-start
  44.3 15.0 %collective-permute-start.1 = (bf16[2,48,1536]{2,1,0:T(8,128)(2,1)S(1)}, bf16[2,48,1536]{2,1,0:T(8,128)(2,1)S(1)}, u32[]{:S(2)}, u32[]{:S(2)}) collective-permute-start(bf16[2,48,1536]{2,1,0:T(8,128)(2,1)S(1)} %maximum_select_fusion.1), channel_id=1, source_target_pairs={{0,2},{2,0},{1,3},{3,1},{4,6},{6,4},{5,7},{7,5},{8,10},{10,8},{9,1... | collective-permute-start | bytes 884744 | tf_op jit(solution)/shard_map/ppermute | solution.py:26
  85.7 6.6 %copy-start.4 = (s32[1,1,1,64,8]{3,4,2,1,0:T(8,128)S(1)}, s32[1,1,1,64,8]{3,4,2,1,0:T(8,128)}, u32[]{:S(2)}) copy-start(s32[1,1,1,64,8]{3,4,2,1,0:T(8,128)} %param.18) | copy-start | bytes 6148
  85.7 77.0 %all-to-all-start.2 = ((bf16[32,1,16,1536]{3,2,1,0:T(8,128)(2,1)}), bf16[32,1,16,1536]{3,2,1,0:T(8,128)(2,1)S(1)}, u32[]{:S(2)}, u32[]{:S(2)}) async-start(bf16[32,1,16,1536]{3,2,1,0:T(8,128)(2,1)} %bitcast.14), calls=%async_computation.2 | async-start | bytes 3145728 | tf_op jit(solution)/shard_map/all_to_all | solution.py:177
  92.3 70.6 %copy-start = (bf16[1,1,1,64,1536]{4,3,2,1,0:T(8,128)(2,1)S(1)}, bf16[1,1,1,64,1536]{4,3,2,1,0:T(8,128)(2,1)}, u32[]{:S(2)}) copy-start(bf16[1,1,1,64,1536]{4,3,2,1,0:T(8,128)(2,1)} %param.13) | copy-start | bytes 589828
  92.4 70.8 %copy-start.5 = (f32[1536]{0:T(1024)S(1)}, f32[1536]{0:T(1024)}, u32[]{:S(2)}) copy-start(f32[1536]{0:T(1024)} %param.21) | copy-start | bytes 18436
  173.5 84.2 %all-to-all-start.3 = ((bf16[32,17,1536]{2,1,0:T(8,128)(2,1)}), bf16[32,17,1536]{2,1,0:T(8,128)(2,1)S(1)}, u32[]{:S(2)}, u32[]{:S(2)}) async-start(bf16[32,17,1536]{2,1,0:T(8,128)(2,1)} %reshape.282), calls=%async_computation.3 | async-start | bytes 4718592 | tf_op jit(solution)/shard_map/all_to_all | solution.py:216
  180.4 91.1 %all-gather.5.cloned.1.call-start = ((), (), s32[]{:S(2)}) async-start(), calls=%async_computation.6 | async-start | bytes 1671168 | tf_op jit(solution)/shard_map/all_gather | solution.py:214
  276.4 14.9 %copy-start.6 = (f32[1,1,1,64,8]{3,4,2,1,0:T(8,128)S(1)}, f32[1,1,1,64,8]{3,4,2,1,0:T(8,128)}, u32[]{:S(2)}) copy-start(f32[1,1,1,64,8]{3,4,2,1,0:T(8,128)} %param.19) | copy-start | bytes 6148
  276.4 70.8 %all-to-all-start.4 = ((bf16[32,17,1536]{2,1,0:T(8,128)(2,1)}), bf16[32,17,1536]{2,1,0:T(8,128)(2,1)}, u32[]{:S(2)}, u32[]{:S(2)}) async-start(bf16[32,17,1536]{2,1,0:T(8,128)(2,1)} %reshape.284), calls=%async_computation.4 | async-start | bytes 4718592 | tf_op jit(solution)/shard_map/all_to_all | solution.py:222
  352.1 2.9 copy-start.1
Sparse Core Ops, SparseCore 0:
  43.9 115.4 all-gather.2
  183.3 88.1 all-gather.4
where the time goes:
time: 363 us
  waiting for transfers between devices  230 us (63%)
  starting transfers between devices  51 us (14%)
  local copies, waits for them, and re-layouts  26 us (7%)
  matrix products  21.7 us (6%)
  other arithmetic  18.4 us (5%)
  between operations  15.1 us (4%)
    all_to_all x1, waiting for transfers between devices, shards(): lax.all_to_all(outbound_rows, 'tensor', split_axis=0, concat_axis=0, tile...  76.6 us
    all_to_all x1, waiting for transfers between devices, shards(): lax.all_to_all(head_sums, 'tensor', split_axis=0, concat_axis=0, tiled=True)  68.3 us
    all_to_all x1, waiting for transfers between devices, shards(): lax.all_to_all(computed, 'tensor', split_axis=0, concat_axis=0, tiled=True)  51.4 us
    all_to_all x1, starting transfers between devices, shards(): lax.all_to_all(query_send, 'tensor', split_axis=0, concat_axis=0, tiled=T...  14.4 us
    all_to_all x1, starting transfers between devices, shards(): lax.all_to_all(computed, 'tensor', split_axis=0, concat_axis=0, tiled=True)  14.2 us
    ppermute x2, waiting for transfers between devices, partner_2(): return lax.ppermute(block, axis, route)  12.6 us
    all_to_all x1, waiting for transfers between devices, shards(): lax.all_to_all(query_send, 'tensor', split_axis=0, concat_axis=0, tiled=T...  11.5 us
    scatter x1, local copies, waits for them, and re-layouts, shards(): outbound_rows = jnp.zeros((device_list * capacity, MODEL_WIDTH), jnp.bflo...  8.56 us
  transfers between devices with their start and end apart: 9, of which 8 were waited for; matrix products, arithmetic and copies ran while one was open for 14% of the time, Pallas kernels for 0%

commit v1 on v0

v1 whole, which is shorter than its diff:
```python
import functools
import math

import jax
import jax.numpy as jnp
from jax import lax
from jax.experimental import pallas as pl
from jax.experimental.pallas import tpu as pltpu
from jax.sharding import Mesh
from jax.sharding import PartitionSpec as P

D = 1536
HQ = 24
HKV = 8
HD = 64
FFE = 512
TOPK = 8
EPS = 1e-05
NT = 32
TOK = 64
CROWS = 32
SLOT = 16
CH = D // 128
SROWS = SLOT * CH + 16
BF = jnp.bfloat16
F32 = jnp.float32
TEN = ("zhi", "x", "core")
NEG = -1e30
INTERPRET = False


def vmem():
    return pl.BlockSpec(memory_space=pltpu.VMEM)


def params(mib):
    return pltpu.CompilerParams(vmem_limit_bytes=mib << 20)


def dot(a, b):
    return lax.dot_general(a, b, (((1,), (0,)), ((), ())), preferred_element_type=F32)


def iota(shape, dim):
    return lax.broadcasted_iota(jnp.int32, shape, dim)


def pack_kernel(q_ref, f_ref, c_ref, o_ref):
    zeros = jnp.zeros((16, HD), BF)
    for g in range(HKV):
        cols = pl.ds(g * 128, 128)
        for quarter in range(4):
            t = g * 4 + quarter
            rows = q_ref[quarter * 16 : quarter * 16 + 16, g * 192 : g * 192 + 192]
            half = quarter % 2
            o_ref[t, 0:16, :] = rows[:, :128]
            o_ref[t, 16:32, :] = jnp.concatenate([rows[:, 128:], zeros], 1)
            o_ref[t, 32:48, :] = c_ref[half * 16 : half * 16 + 16, cols]
            o_ref[t, 48:80, :] = f_ref[half * 32 : half * 32 + 32, cols]


def pack(queries, fresh, cache):
    return pl.pallas_call(
        pack_kernel,
        out_shape=jax.ShapeDtypeStruct((NT, 80, 128), BF),
        in_specs=[vmem()] * 3,
        out_specs=vmem(),
        interpret=INTERPRET,
        name="pack",
    )(queries, fresh, cache)


def attention_kernel(info_ref, own_ref, oth_ref, o_ref, kv, sc, bias_c, bias_d):
    b = pl.program_id(0)
    length, core, quarter = info_ref[0], info_ref[1], info_ref[2]

    @pl.when(b == 0)
    def _():
        kv[0:512, :] = own_ref[:, 32:48, :].reshape(512, 128)
        kv[512:1024, :] = oth_ref[:, 0:16, :].reshape(512, 128)
        for j in range(4):
            base = 1024 + 512 * j
            kv[base : base + 256, :] = own_ref[8 * j : 8 * j + 8, 48:80, :].reshape(256, 128)
            kv[base + 256 : base + 512, :] = oth_ref[8 * j : 8 * j + 8, 16:48, :].reshape(256, 128)
        col = iota((8, 1024), 1)
        half = jnp.where(col < 512, core, 1 - core)
        inner = col % 512
        place = (inner // 16) * 32 + half * 16 + inner % 16
        bias_c[...] = jnp.where(place < length, 0.0, NEG)
        row = iota((128, 512), 0)
        col = iota((128, 512), 1)
        half = jnp.where(col < 256, core, 1 - core)
        inner = col % 256
        key_at = (inner // 32) * 64 + half * 32 + inner % 32
        query_at = (row // 16) * 64 + quarter * 16 + row % 16
        bias_d[...] = jnp.where(key_at <= query_at, 0.0, NEG)

    first = own_ref[pl.ds(b * 8, 8), 0:16, :].reshape(128, 128).astype(F32) * 0.125
    second = own_ref[pl.ds(b * 8, 8), 16:32, :].reshape(128, 128).astype(F32) * 0.125
    low = iota((128, 128), 1) < HD
    q = jnp.concatenate(
        [
            jnp.where(low, first, 0.0),
            jnp.where(low, pltpu.roll(first, HD, 1), 0.0),
            jnp.where(low, second, 0.0),
        ],
        0,
    ).astype(BF)

    def scores(k):
        keys = kv[pl.ds(pl.multiple_of(k * 512, 512), 512), :]
        return lax.dot_general(q, keys, (((1,), (1,)), ((), ())), preferred_element_type=F32)

    def fold(fn, top, s):
        for j in range(4):
            top = fn(top, s[:, j * 128 : j * 128 + 128])
        return top

    top = jnp.full((384, 128), NEG, F32)
    for k in range(2):
        s = scores(k) + bias_c[0:1, k * 512 : k * 512 + 512]
        sc[k] = s
        top = fold(jnp.maximum, top, s)
    s = scores(2 + b)
    s = s + jnp.concatenate([bias_d[...]] * 3, 0)
    sc[2 + b] = s
    top = fold(jnp.maximum, top, s)

    def middle(k, top):
        s = scores(k)
        sc[k] = s
        return fold(jnp.maximum, top, s)

    top = lax.fori_loop(2, 2 + b, middle, top)
    highest = jnp.max(top, 1, keepdims=True)

    def mix(k, carry):
        total, acc = carry
        p = jnp.exp(sc[k] - highest)
        values = kv[pl.ds(pl.multiple_of(k * 512, 512), 512), :]
        return fold(jnp.add, total, p), acc + dot(p.astype(BF), values)

    zero = jnp.zeros((384, 128), F32)
    total, acc = lax.fori_loop(0, 3 + b, mix, (zero, zero))
    out = acc / jnp.sum(total, 1, keepdims=True)
    a0, a1, a2 = out[0:128], out[128:256], out[256:384]
    pair = jnp.where(low, pltpu.roll(a0, HD, 1), a1).astype(BF)
    last = jnp.where(low, pltpu.roll(a2, HD, 1), 0.0).astype(BF)
    o_ref[pl.ds(b * 8, 8), 0:16, :] = pair.reshape(8, 16, 128)
    o_ref[pl.ds(b * 8, 8), 16:32, :] = last.reshape(8, 16, 128)


def attention(info, own, other):
    return pl.pallas_call(
        attention_kernel,
        out_shape=jax.ShapeDtypeStruct((NT, 32, 128), BF),
        grid=(4,),
        in_specs=[
            pl.BlockSpec(memory_space=pltpu.SMEM),
            vmem(),
            vmem(),
        ],
        out_specs=vmem(),
        scratch_shapes=[
            pltpu.VMEM((3072, 128), BF),
            pltpu.VMEM((6, 384, 512), F32),
            pltpu.VMEM((8, 1024), F32),
            pltpu.VMEM((128, 512), F32),
        ],
        compiler_params=params(32),
        cost_estimate=pl.CostEstimate(
            flops=2 * 2 * 1536 * 2304 * 128, bytes_accessed=3 << 20, transcendentals=1536 * 2304
        ),
        interpret=INTERPRET,
        name="attention",
    )(info, own, other)


def project_kernel(att_ref, w_ref, hid_ref, gain_ref, ids_ref, res_ref, disp_ref):
    g = pl.program_id(0)

    @pl.when(g == 0)
    def _():
        res_ref[...] = jnp.zeros_like(res_ref)

    pair = att_ref[pl.ds(g * 4, 4), 0:16, :].reshape(TOK, 128)
    last = att_ref[pl.ds(g * 4, 4), 16:32, :].reshape(TOK, 128)
    term = dot(pair, w_ref[0:128, :]) + dot(last[:, :HD], w_ref[128:192, :])
    res_ref[...] += term.astype(BF).astype(F32)

    @pl.when(g == HKV - 1)
    def _():
        residual = hid_ref[...].astype(F32) + res_ref[...]
        res_ref[...] = residual
        meansq = jnp.mean(residual * residual, 1, keepdims=True)
        normed = (residual * lax.rsqrt(meansq + EPS) * gain_ref[...]).astype(BF)
        experts = iota((NT, TOK), 0)
        named = jnp.zeros((NT, TOK), F32)
        for k in range(TOPK):
            named = named + jnp.where(ids_ref[k : k + 1, :] == experts, 1.0, 0.0)
        before = jnp.where(iota((TOK, TOK), 0) < iota((TOK, TOK), 1), 1.0, 0.0).astype(BF)
        rank = dot(named.astype(BF), before)
        rank = jnp.where(named > 0.5, rank, -1.0).astype(BF)
        spread = jnp.where(iota((512, NT), 0) // SLOT == iota((512, NT), 1), 1.0, 0.0).astype(BF)
        ranks = dot(spread, rank)
        place = iota((512, TOK), 0) % SLOT
        pick = jnp.where(ranks == place.astype(F32), 1.0, 0.0).astype(BF)
        late = jnp.where(ranks == float(SLOT), 1.0, 0.0)
        extra = jnp.zeros((512, 128), F32)
        for c in range(CH):
            chunk = normed[:, c * 128 : c * 128 + 128]
            disp_ref[:, c * SLOT : (c + 1) * SLOT, :] = (
                dot(pick, chunk).astype(BF).reshape(NT, SLOT, 128)
            )
            extra = extra + dot(jnp.where(place == c, late, 0.0).astype(BF), chunk)
        disp_ref[:, SLOT * CH : SROWS, :] = extra.astype(BF).reshape(NT, 16, 128)


def project(att, weight, hidden, gain, ids_t):
    return pl.pallas_call(
        project_kernel,
        out_shape=(
            jax.ShapeDtypeStruct((TOK, D), F32),
            jax.ShapeDtypeStruct((NT, SROWS, 128), BF),
        ),
        grid=(HKV,),
        in_specs=[
            vmem(),
            pl.BlockSpec((192, D), lambda g: (g, 0)),
            vmem(),
            vmem(),
            vmem(),
        ],
        out_specs=(vmem(), vmem()),
        compiler_params=params(32),
        cost_estimate=pl.CostEstimate(
            flops=2 * TOK * D * D, bytes_accessed=8 << 20, transcendentals=0
        ),
        interpret=INTERPRET,
        name="project",
    )(att, weight, hidden, gain, ids_t)


def gather_extra(block):
    rows = iota((CH * NT, 512), 0)
    cols = iota((CH * NT, 512), 1)
    match = (rows % NT == cols // 16) & (rows // NT == cols % 16)
    stacked = dot(jnp.where(match, 1.0, 0.0).astype(BF), block).astype(BF)
    return [stacked[c * NT : (c + 1) * NT, :] for c in range(CH)]


def spread_extra(rows):
    place = iota((512, NT), 0)
    owner = place // 16 == iota((512, NT), 1)
    out = jnp.zeros((512, 128), F32)
    for c in range(CH):
        match = jnp.where(owner & (place % 16 == c), 1.0, 0.0).astype(BF)
        out = out + dot(match, rows[:, c * 128 : c * 128 + 128])
    return out.astype(BF)


def expert_kernel(in_ref, w_ref, o_ref, x, w1, w2, sems):
    blocks = w_ref.shape[0]
    copies = []
    for d in range(blocks):
        pieces = (
            (w_ref.at[d, 0:64, 0:1024], w1.at[d * 96 : d * 96 + 64, :]),
            (w_ref.at[d, 0:32, 1024:1536], w1.at[d * 96 + 64 : d * 96 + 96, 0:512]),
            (w_ref.at[d, 32:64, 1024:1536], w1.at[d * 96 + 64 : d * 96 + 96, 512:1024]),
            (w_ref.at[d, 64:96, :], w2.at[d * 32 : d * 32 + 32, :]),
        )
        for n, (src, dst) in enumerate(pieces):
            copies.append(pltpu.make_async_copy(src, dst, sems.at[d, n]))
    for copy in copies:
        copy.start()
    for c in range(CH):
        x[0:512, c * 128 : c * 128 + 128] = in_ref[:, c * SLOT : (c + 1) * SLOT, :].reshape(512, 128)
    chunks = gather_extra(in_ref[:, SLOT * CH : SROWS, :].reshape(512, 128))
    for c in range(CH):
        x[512:544, c * 128 : c * 128 + 128] = chunks[c]
    for copy in copies:
        copy.wait()
    hidden = dot(x[...], w1[...])
    gate = hidden[:, :FFE]
    active = (gate / (1.0 + jnp.exp(-gate)) * hidden[:, FFE:]).astype(BF)
    out = dot(active, w2[...]).astype(BF)
    for c in range(CH):
        o_ref[:, c * SLOT : (c + 1) * SLOT, :] = out[0:512, c * 128 : c * 128 + 128].reshape(
            NT, SLOT, 128
        )
    o_ref[:, SLOT * CH : SROWS, :] = spread_extra(out[512:544, :]).reshape(NT, 16, 128)


def expert(slots, weights):
    blocks = weights.shape[0]
    return pl.pallas_call(
        expert_kernel,
        out_shape=jax.ShapeDtypeStruct((NT, SROWS, 128), BF),
        in_specs=[vmem(), pl.BlockSpec(memory_space=pl.ANY)],
        out_specs=vmem(),
        scratch_shapes=[
            pltpu.VMEM((544, D), BF),
            pltpu.VMEM((blocks * 96, 2 * FFE), BF),
            pltpu.VMEM((blocks * 32, D), BF),
            pltpu.SemaphoreType.DMA((blocks, 4)),
        ],
        compiler_params=params(40),
        cost_estimate=pl.CostEstimate(
            flops=2 * 544 * 1536 * 1536, bytes_accessed=9 << 20, transcendentals=544 * 512
        ),
        interpret=INTERPRET,
        name="expert",
    )(slots, weights)


def combine_kernel(in_ref, res_ref, ids_ref, gate_ref, o_ref):
    experts = iota((TOK, NT), 1)
    named = jnp.zeros((TOK, NT), F32)
    gates = jnp.zeros((TOK, NT), F32)
    for k in range(TOPK):
        match = ids_ref[:, k : k + 1] == experts
        named = named + jnp.where(match, 1.0, 0.0)
        gates = gates + jnp.where(match, gate_ref[:, k : k + 1], 0.0)
    before = jnp.where(iota((TOK, TOK), 1) < iota((TOK, TOK), 0), 1.0, 0.0).astype(BF)
    rank = dot(before, named.astype(BF))
    rank = jnp.where(named > 0.5, rank, -1.0)
    spread = jnp.where(iota((NT, 512), 0) == iota((NT, 512), 1) // SLOT, 1.0, 0.0).astype(BF)
    place = (iota((TOK, 512), 1) % SLOT).astype(F32)
    pick = dot(rank.astype(BF), spread) == place
    high = gates.astype(BF)
    low = (gates - high.astype(F32)).astype(BF)
    weights = jnp.concatenate(
        [jnp.where(pick, dot(part, spread), 0.0).astype(BF) for part in (high, low)], 0
    )
    late = rank == float(SLOT)
    late_weights = jnp.concatenate(
        [jnp.where(late, part.astype(F32), 0.0).astype(BF) for part in (high, low)], 0
    )
    chunks = gather_extra(in_ref[:, SLOT * CH : SROWS, :].reshape(512, 128))
    for c in range(CH):
        main = in_ref[:, c * SLOT : (c + 1) * SLOT, :].reshape(512, 128)
        both = dot(weights, main) + dot(late_weights, chunks[c])
        cols = slice(c * 128, c * 128 + 128)
        o_ref[:, cols] = (res_ref[:, cols] + (both[:TOK] + both[TOK:])).astype(BF)


def combine(returned, residual, ids, gates):
    return pl.pallas_call(
        combine_kernel,
        out_shape=jax.ShapeDtypeStruct((TOK, D), BF),
        in_specs=[vmem()] * 4,
        out_specs=vmem(),
        compiler_params=params(32),
        interpret=INTERPRET,
        name="combine",
    )(returned, residual, ids, gates)


def shards(
    hidden_in,
    rotated_queries,
    fresh_key_values,
    cached_key_values,
    cached_len,
    expert_ids,
    route_gates,
    output_weight,
    norm_gain,
    gate_up,
    down_weight,
):
    zlo = lax.axis_index("zlo")
    core = lax.axis_index("core")
    quarter = lax.axis_index(TEN) % 4
    length = cached_len[0]
    ids = expert_ids[0, 0, 0]
    gates = route_gates[0, 0, 0]

    send = pack(rotated_queries[0, 0, 0], fresh_key_values[0, 0, 0], cached_key_values[0])
    full_weight = lax.all_gather(output_weight, TEN, axis=0, tiled=True)
    up = gate_up[0]
    packed = jnp.concatenate(
        [jnp.concatenate([up[:64], jnp.concatenate([up[64:, :512], up[64:, 512:]], 0)], 1), down_weight[0]], 0
    )
    across = lax.ppermute(packed, "zlo", [(0, 1), (1, 0)])
    both = jnp.where(
        zlo == 0, jnp.stack([packed, across], 0), jnp.stack([across, packed], 0)
    )
    weights = lax.all_gather(both, "y", axis=0, tiled=True)

    own = lax.all_to_all(send, TEN, split_axis=0, concat_axis=0, tiled=True)
    other = lax.ppermute(own[:, 32:, :], "core", [(0, 1), (1, 0)])
    info = jnp.stack([length, core.astype(jnp.int32), quarter.astype(jnp.int32)])
    attended = attention(info, own, other)
    att = lax.all_to_all(attended, TEN, split_axis=0, concat_axis=0, tiled=True)
    residual, outbound = project(att, full_weight, hidden_in[0, 0, 0], norm_gain[None], ids.T)
    slots = lax.all_to_all(outbound, TEN, split_axis=0, concat_axis=0, tiled=True)
    computed = expert(slots, weights)
    returned = lax.all_to_all(computed, TEN, split_axis=0, concat_axis=0, tiled=True)
    hidden_out = combine(returned, residual, ids, gates)

    mine = lax.dynamic_slice_in_dim(own[:, 32:, :], quarter * 32, 32, 2)
    theirs = lax.dynamic_slice_in_dim(other, quarter * 32, 32, 2)
    halves = jnp.where(
        core == 0, jnp.stack([mine, theirs], 1), jnp.stack([theirs, mine], 1)
    )
    old_rows = halves[:, :, :16].reshape(NT * CROWS, 32)
    new_rows = halves[:, :, 16:].reshape(NT * TOK, 32)
    total = NT * CROWS + NT * TOK
    base = jnp.concatenate([old_rows, jnp.zeros((NT * TOK, 32), BF)], 0)
    base = jnp.where((jnp.arange(total, dtype=jnp.int32) < length)[:, None], base, jnp.zeros_like(base))
    cache_out = lax.dynamic_update_slice_in_dim(base, new_rows, length, 0)
    return hidden_out.reshape(1, 1, 1, TOK, D), cache_out[None]


def solution(mesh):
    dp, tensor = mesh.devices.shape
    fine = Mesh(mesh.devices.reshape(dp // 2, 2, 4, 4, 2), ("y", "zlo", "zhi", "x", "core"))
    ydp = ("y", "zlo")
    return jax.shard_map(
        shards,
        mesh=fine,
        in_specs=(
            P(ydp, TEN, None, None, None),
            P(ydp, TEN, None, None, None),
            P(ydp, TEN, None, None, None),
            P(ydp, TEN, None),
            P(ydp),
            P(ydp, TEN, None, None, None),
            P(ydp, TEN, None, None, None),
            P(TEN, None),
            P(),
            P(TEN, ydp, None),
            P(TEN, ydp, None),
        ),
        out_specs=(P(ydp, TEN, None, None, None), P(ydp, None, TEN)),
        check_vma=False,
    )
```

time: 363 us -> 232 us (0.64)
  waiting for transfers between devices: 230 us -> 98.6 us
  blocking collectives: 0 us -> 37.1 us
  Pallas kernels: 0 us -> 29.3 us
  matrix products: 21.7 us -> 0 us
  starting transfers between devices: 51 us -> 30.3 us
  other arithmetic: 18.4 us -> 5.08 us
  local copies, waits for them, and re-layouts: 26 us -> 15.9 us
    all_to_all x5 -> x3, waiting for transfers between devices: 211 us -> 45.5 us  [the longest x1 30 us: shards(): lax.all_to_all(computed, TEN, split_axis=0, concat_axis=0, tiled=True)]
    all_gather x2, waiting for transfers between devices: 6.52 us -> 47.8 us  [the longest x1 47.8 us: shards(): weights = lax.all_gather(both, 'y', axis=0, tiled=True)]
    all_to_all x0 -> x1, blocking collectives: none -> 37.1 us  [shards(): own = lax.all_to_all(send, TEN, split_axis=0, concat_axis=0, tiled=True)]
    pallas_call x0 -> x5, Pallas kernels: none -> 29.3 us  [the longest x1 11.8 us: attention(): pl.pallas_call(attention_kernel, out_shape=jax.ShapeDtypeStruct((NT, 32,...]
    all_to_all x5 -> x3, starting transfers between devices: 45.8 us -> 23.1 us  [the longest x1 10.6 us: shards(): lax.all_to_all(computed, TEN, split_axis=0, concat_axis=0, tiled=True)]
    dot_general x9 -> x0, matrix products: 21.7 us -> none  [the longest x3 5.9 us: one_block(): jnp.dot(weights.astype(jnp.bfloat16), values_all, preferred_element_type=...]
    reduce_sum x7 -> x0, other arithmetic: 10.9 us -> none  [the longest x3 7.58 us: one_block(): denoms = jnp.sum(weights, 1, keepdims=True)]
    scatter x1 -> x0, local copies, waits for them, and re-layouts: 8.56 us -> none  [shards(): outbound_rows = jnp.zeros((device_list * capacity, MODEL_WIDTH), jnp.bflo...]
  transfers between devices with their start and end apart: 9 -> 7, of which waited for: 8 -> 5; matrix products, arithmetic and copies ran while one was open for 14% -> 7% of each run, Pallas kernels for 0% -> 8%
where the time goes in v1:
time: 232 us; the launch traced here: 231 us
  waiting for transfers between devices  98.6 us (42%)
  blocking collectives  37.1 us (16%)
  starting transfers between devices  30.3 us (13%)
  Pallas kernels  29.3 us (13%)
  local copies, waits for them, and re-layouts  15.9 us (7%)
  between operations  14.8 us (6%)
  other arithmetic  5.08 us (2%)
    all_gather x1, waiting for transfers between devices, shards(): weights = lax.all_gather(both, 'y', axis=0, tiled=True)  47.8 us
    all_to_all x1, blocking collectives, shards(): own = lax.all_to_all(send, TEN, split_axis=0, concat_axis=0, tiled=True)  37.1 us
    all_to_all x1, waiting for transfers between devices, shards(): lax.all_to_all(computed, TEN, split_axis=0, concat_axis=0, tiled=True)  30 us
    all_to_all x1, waiting for transfers between devices, shards(): att = lax.all_to_all(attended, TEN, split_axis=0, concat_axis=0, tiled=True)  15.5 us
    pallas_call x1, Pallas kernels, attention(): pl.pallas_call(attention_kernel, out_shape=jax.ShapeDtypeStruct((NT, 32,...  11.8 us
    all_to_all x1, starting transfers between devices, shards(): lax.all_to_all(computed, TEN, split_axis=0, concat_axis=0, tiled=True)  10.6 us
    pallas_call x1, Pallas kernels, expert(): pl.pallas_call(expert_kernel, out_shape=jax.ShapeDtypeStruct((NT, SROWS,...  8.92 us
    all_to_all x1, starting transfers between devices, shards(): att = lax.all_to_all(attended, TEN, split_axis=0, concat_axis=0, tiled=True)  6.82 us
  transfers between devices with their start and end apart: 7, of which 5 were waited for; matrix products, arithmetic and copies ran while one was open for 7% of the time, Pallas kernels for 8%

profile of v1, /device:TPU:1, one launch (start us, length us, event | category | flops | bytes accessed | tf_op | source)
XLA Modules:
  0.0 231.1 jit_solution(7023238799182620829)
XLA Ops:
  9.6 0.9 fusion
  10.6 4.8 %collective-permute-start.1 = (bf16[96,1536]{1,0:T(8,128)(2,1)S(1)}, bf16[96,1536]{1,0:T(8,128)(2,1)S(1)}, u32[]{:S(2)}, u32[]{:S(2)}) collective-permute-start(bf16[96,1536]{1,0:T(8,128)(2,1)S(1)} %get-tuple-element.13), channel_id=1, source_target_pairs={{0,32},{32,0},{1,33},{33,1},{2,34},{34,2},{3,35},{35,3},{4,36},{36... | collective-permute-start | bytes 884744 | tf_op jit(solution)/shard_map/ppermute | solution.py:385
  15.4 4.1 %collective-permute-done.1 = bf16[96,1536]{1,0:T(8,128)(2,1)S(1)} collective-permute-done((bf16[96,1536]{1,0:T(8,128)(2,1)S(1)}, bf16[96,1536]{1,0:T(8,128)(2,1)S(1)}, u32[]{:S(2)}, u32[]{:S(2)}) %collective-permute-start.1) | collective-permute-done | bytes 294944 | tf_op jit(solution)/shard_map/ppermute | solution.py:385
  20.5 2.0 pack.1
  22.4 37.1 %all_to_all.20.own_ref = bf16[32,80,128]{2,1,0:T(8,128)(2,1)S(1)} all-to-all(bf16[32,80,128]{2,1,0:T(8,128)(2,1)} %pack.1), channel_id=1, replica_groups=mesh['y'=8,'zlo'=2,'zhi'=4,'x'=4,'core'=2] {'zhi','x','core'}, dimensions={0} | all-to-all | bytes 1310720 | tf_op jit(solution)/shard_map/all_to_all | solution.py:391
  59.5 2.3 collective-permute-start
  63.1 11.8 %attention.1 = bf16[32,32,128]{2,1,0:T(8,128)(2,1)} custom-call(s32[3]{0:T(128)S(1)} %pad_add_fusion.info_ref, bf16[32,80,128]{2,1,0:T(8,128)(2,1)S(1)} %all_to_all.20.own_ref, bf16[32,48,128]{2,1,0:T(8,128)(2,1)S(1)} %collective-permute-done.oth_ref), custom_call_target="tpu_custom_call" | custom-call | flops 1811939328 | bytes 3145728 | tf_op jit(solution)/shard_map/attention/pallas_call | solution.py:154
  74.9 6.8 %all-to-all-start.1 = ((bf16[32,32,128]{2,1,0:T(8,128)(2,1)}), bf16[32,32,128]{2,1,0:T(8,128)(2,1)S(1)}, u32[]{:S(2)}, u32[]{:S(2)}) async-start(bf16[32,32,128]{2,1,0:T(8,128)(2,1)} %attention.1), calls=%async_computation.1 | async-start | bytes 524288 | tf_op jit(solution)/shard_map/all_to_all | solution.py:395
  81.8 15.5 %all-to-all-done.1.att_ref = bf16[32,32,128]{2,1,0:T(8,128)(2,1)S(1)} async-done(((bf16[32,32,128]{2,1,0:T(8,128)(2,1)}), bf16[32,32,128]{2,1,0:T(8,128)(2,1)S(1)}, u32[]{:S(2)}, u32[]{:S(2)}) %all-to-all-start.1) | async-done | bytes 262176 | tf_op jit(solution)/shard_map/all_to_all | solution.py:395
  97.3 2.3 %copy-done = bf16[1536,1536]{1,0:T(8,128)(2,1)S(1)} copy-done((bf16[1536,1536]{1,0:T(8,128)(2,1)S(1)}, bf16[1536,1536]{1,0:T(8,128)(2,1)}, u32[]{:S(2)}) %copy-start) | copy-done | bytes 4718616
  99.6 4.5 %project.1 = (f32[64,1536]{1,0:T(8,128)S(1)}, bf16[32,208,128]{2,1,0:T(8,128)(2,1)}) custom-call(bf16[32,32,128]{2,1,0:T(8,128)(2,1)S(1)} %all-to-all-done.1.att_ref, bf16[1536,1536]{1,0:T(8,128)(2,1)S(1)} %copy-done, bf16[64,1536]{1,0:T(8,128)(2,1)S(1)} %bitcast.30, f32[1,1536]{1,0:T(1,128)S(1)} %broadcast_in_dim.21.gain_ref, s32[8,64]{1,0:T(8,128)S(1)} %bitcast.33), custom_call_target="tpu_custom_call" | custom-call | flops 301989888 | bytes 8388608 | tf_op jit(solution)/shard_map/project/pallas_call | solution.py:220
  104.2 5.6 %all-to-all-start.2 = ((bf16[32,208,128]{2,1,0:T(8,128)(2,1)}), bf16[32,208,128]{2,1,0:T(8,128)(2,1)S(1)}, u32[]{:S(2)}, u32[]{:S(2)}) async-start(bf16[32,208,128]{2,1,0:T(8,128)(2,1)} %get-tuple-element.4), calls=%async_computation.2 | async-start | bytes 3407872 | tf_op jit(solution)/shard_map/all_to_all | solution.py:397
  109.8 47.8 %all-gather.5.cloned.1.call-done.w_ref = bf16[16,96,1536]{2,1,0:T(8,128)(2,1)} async-done(((bf16[2,96,1536]{2,1,0:T(8,128)(2,1)}), bf16[16,96,1536]{2,1,0:T(8,128)(2,1)}) %all-gather.5.cloned.1.call-update) | async-done | bytes 4718608 | tf_op jit(solution)/shard_map/all_gather | solution.py:389
  157.6 2.3 %copy-done.3 = bf16[16,96,1536]{2,1,0:T(8,128)(2,1)S(1)} copy-done((bf16[16,96,1536]{2,1,0:T(8,128)(2,1)S(1)}, bf16[16,96,1536]{2,1,0:T(8,128)(2,1)}, u32[]{:S(2)}) %copy-start.3) | copy-done | bytes 4718616
  159.9 8.9 %expert.1 = bf16[32,208,128]{2,1,0:T(8,128)(2,1)} custom-call(bf16[32,208,128]{2,1,0:T(8,128)(2,1)S(1)} %all-to-all-done.2.in_ref, bf16[16,96,1536]{2,1,0:T(8,128)(2,1)S(1)} %copy-done.3), custom_call_target="tpu_custom_call" | custom-call | flops 2566914048 | bytes 9437184 | tf_op jit(solution)/shard_map/expert/pallas_call | solution.py:296
  168.9 10.6 %all-to-all-start.3 = ((bf16[32,208,128]{2,1,0:T(8,128)(2,1)}), bf16[32,208,128]{2,1,0:T(8,128)(2,1)S(1)}, u32[]{:S(2)}, u32[]{:S(2)}) async-start(bf16[32,208,128]{2,1,0:T(8,128)(2,1)} %expert.1), calls=%async_computation.3 | async-start | bytes 3407872 | tf_op jit(solution)/shard_map/all_to_all | solution.py:399
  181.2 1.2 maximum_select_fusion.1
  182.4 1.0 slice.33
  183.6 2.1 copy.44
  185.7 1.9 select_bitcast_fusion
  187.6 3.7 %dynamic_update_slice.4 = bf16[1,3072,32]{2,1,0:T(8,128)(2,1)S(1)} dynamic-update-slice(bf16[1,3072,32]{2,1,0:T(8,128)(2,1)S(1)} %select_bitcast_fusion, bf16[1,2048,32]{2,1,0:T(8,128)(2,1)} %bitcast.35, s32[]{:T(128)} %constant.35.clone.1, s32[]{:T(128)S(6)} %select_n.41, s32[]{:T(128)} %constant.35.clone.1) | dynamic-update-slice | bytes 262148 | tf_op jit(solution)/shard_map/dynamic_update_slice | solution.py:412
  191.3 0.9 copy.42
  192.2 30.0 %all-to-all-done.3.in_ref = bf16[32,208,128]{2,1,0:T(8,128)(2,1)S(1)} async-done(((bf16[32,208,128]{2,1,0:T(8,128)(2,1)}), bf16[32,208,128]{2,1,0:T(8,128)(2,1)S(1)}, u32[]{:S(2)}, u32[]{:S(2)}) %all-to-all-start.3) | async-done | bytes 1703968 | tf_op jit(solution)/shard_map/all_to_all | solution.py:399
  222.2 2.0 combine.1
  (31 shorter events, 6.0 us)
Async XLA Ops:
  7.2 90.1 %all-gather.3.cloned.1.call-start = ((), (), s32[]{:S(2)}) async-start(), calls=%async_computation.4 | async-start | bytes 4866048 | tf_op jit(solution)/shard_map/all_gather | solution.py:380
  7.9 149.7 %all-gather.5.cloned.1.call-start = ((), (), s32[]{:S(2)}) async-start(), calls=%async_computation.5 | async-start | bytes 5308416 | tf_op jit(solution)/shard_map/all_gather | solution.py:389
  10.6 8.9 %collective-permute-start.1 = (bf16[96,1536]{1,0:T(8,128)(2,1)S(1)}, bf16[96,1536]{1,0:T(8,128)(2,1)S(1)}, u32[]{:S(2)}, u32[]{:S(2)}) collective-permute-start(bf16[96,1536]{1,0:T(8,128)(2,1)S(1)} %get-tuple-element.13), channel_id=1, source_target_pairs={{0,32},{32,0},{1,33},{33,1},{2,34},{34,2},{3,35},{35,3},{4,36},{36... | collective-permute-start | bytes 884744 | tf_op jit(solution)/shard_map/ppermute | solution.py:385
  59.5 3.6 %collective-permute-start = (bf16[32,48,128]{2,1,0:T(8,128)(2,1)S(1)}, bf16[32,48,128]{2,1,0:T(8,128)(2,1)S(1)}, u32[]{:S(2)}, u32[]{:S(2)}) collective-permute-start(bf16[32,48,128]{2,1,0:T(8,128)(2,1)S(1)} %slice.29), channel_id=1, source_target_pairs={{0,1},{1,0},{2,3},{3,2},{4,5},{5,4},{6,7},{7,6},{8,9},{9,8},{10,11... | collective-permute-start | bytes 1179656 | tf_op jit(solution)/shard_map/ppermute | solution.py:392
  62.5 19.2 %copy-start.4 = (f32[1536]{0:T(1024)S(1)}, f32[1536]{0:T(1024)}, u32[]{:S(2)}) copy-start(f32[1536]{0:T(1024)} %param.19) | copy-start | bytes 18436
  62.5 34.7 %copy-start.1 = (bf16[1,1,1,64,1536]{4,3,2,1,0:T(8,128)(2,1)S(1)}, bf16[1,1,1,64,1536]{4,3,2,1,0:T(8,128)(2,1)}, u32[]{:S(2)}) copy-start(bf16[1,1,1,64,1536]{4,3,2,1,0:T(8,128)(2,1)} %param.11) | copy-start | bytes 589828
  62.6 34.7 %copy-start.2 = (s32[1,1,1,64,8]{3,4,2,1,0:T(8,128)S(1)}, s32[1,1,1,64,8]{3,4,2,1,0:T(8,128)}, u32[]{:S(2)}) copy-start(s32[1,1,1,64,8]{3,4,2,1,0:T(8,128)} %param.16) | copy-start | bytes 6148
  74.9 22.3 %all-to-all-start.1 = ((bf16[32,32,128]{2,1,0:T(8,128)(2,1)}), bf16[32,32,128]{2,1,0:T(8,128)(2,1)S(1)}, u32[]{:S(2)}, u32[]{:S(2)}) async-start(bf16[32,32,128]{2,1,0:T(8,128)(2,1)} %attention.1), calls=%async_computation.1 | async-start | bytes 524288 | tf_op jit(solution)/shard_map/all_to_all | solution.py:395
  97.3 2.3 %copy-start = (bf16[1536,1536]{1,0:T(8,128)(2,1)S(1)}, bf16[1536,1536]{1,0:T(8,128)(2,1)}, u32[]{:S(2)}) copy-start(bf16[1536,1536]{1,0:T(8,128)(2,1)} %all-gather.3.cloned.1.call-done.w_ref) | copy-start | bytes 14155780
  104.2 53.4 %all-to-all-start.2 = ((bf16[32,208,128]{2,1,0:T(8,128)(2,1)}), bf16[32,208,128]{2,1,0:T(8,128)(2,1)S(1)}, u32[]{:S(2)}, u32[]{:S(2)}) async-start(bf16[32,208,128]{2,1,0:T(8,128)(2,1)} %get-tuple-element.4), calls=%async_computation.2 | async-start | bytes 3407872 | tf_op jit(solution)/shard_map/all_to_all | solution.py:397
  157.6 2.3 %copy-start.3 = (bf16[16,96,1536]{2,1,0:T(8,128)(2,1)S(1)}, bf16[16,96,1536]{2,1,0:T(8,128)(2,1)}, u32[]{:S(2)}) copy-start(bf16[16,96,1536]{2,1,0:T(8,128)(2,1)} %all-gather.5.cloned.1.call-done.w_ref) | copy-start | bytes 14155780
  168.8 10.7 %copy-start.5 = (f32[1,1,1,64,8]{3,4,2,1,0:T(8,128)S(1)}, f32[1,1,1,64,8]{3,4,2,1,0:T(8,128)}, u32[]{:S(2)}) copy-start(f32[1,1,1,64,8]{3,4,2,1,0:T(8,128)} %param.17) | copy-start | bytes 6148
  168.9 53.3 %all-to-all-start.3 = ((bf16[32,208,128]{2,1,0:T(8,128)(2,1)}), bf16[32,208,128]{2,1,0:T(8,128)(2,1)S(1)}, u32[]{:S(2)}, u32[]{:S(2)}) async-start(bf16[32,208,128]{2,1,0:T(8,128)(2,1)} %expert.1), calls=%async_computation.3 | async-start | bytes 3407872 | tf_op jit(solution)/shard_map/all_to_all | solution.py:399
Sparse Core Ops, SparseCore 0:
  11.1 82.9 all-gather.2
  96.2 61.3 all-gather.4

commit v2 on v1

--- a/solution.py
+++ b/solution.py
@@ -34,7 +34,7 @@
 
 
 def params(mib):
-    return pltpu.CompilerParams(vmem_limit_bytes=mib << 20)
+    return pltpu.CompilerParams(vmem_limit_bytes=int(mib * (1 << 20)))
 
 
 def dot(a, b):
@@ -176,69 +176,95 @@
     )(info, own, other)
 
 
-def project_kernel(att_ref, w_ref, hid_ref, gain_ref, ids_ref, res_ref, disp_ref):
-    g = pl.program_id(0)
-
-    @pl.when(g == 0)
-    def _():
-        res_ref[...] = jnp.zeros_like(res_ref)
-
-    pair = att_ref[pl.ds(g * 4, 4), 0:16, :].reshape(TOK, 128)
-    last = att_ref[pl.ds(g * 4, 4), 16:32, :].reshape(TOK, 128)
-    term = dot(pair, w_ref[0:128, :]) + dot(last[:, :HD], w_ref[128:192, :])
-    res_ref[...] += term.astype(BF).astype(F32)
-
-    @pl.when(g == HKV - 1)
-    def _():
-        residual = hid_ref[...].astype(F32) + res_ref[...]
-        res_ref[...] = residual
-        meansq = jnp.mean(residual * residual, 1, keepdims=True)
-        normed = (residual * lax.rsqrt(meansq + EPS) * gain_ref[...]).astype(BF)
-        experts = iota((NT, TOK), 0)
-        named = jnp.zeros((NT, TOK), F32)
-        for k in range(TOPK):
-            named = named + jnp.where(ids_ref[k : k + 1, :] == experts, 1.0, 0.0)
-        before = jnp.where(iota((TOK, TOK), 0) < iota((TOK, TOK), 1), 1.0, 0.0).astype(BF)
-        rank = dot(named.astype(BF), before)
-        rank = jnp.where(named > 0.5, rank, -1.0).astype(BF)
-        spread = jnp.where(iota((512, NT), 0) // SLOT == iota((512, NT), 1), 1.0, 0.0).astype(BF)
-        ranks = dot(spread, rank)
-        place = iota((512, TOK), 0) % SLOT
-        pick = jnp.where(ranks == place.astype(F32), 1.0, 0.0).astype(BF)
-        late = jnp.where(ranks == float(SLOT), 1.0, 0.0)
-        extra = jnp.zeros((512, 128), F32)
-        for c in range(CH):
-            chunk = normed[:, c * 128 : c * 128 + 128]
-            disp_ref[:, c * SLOT : (c + 1) * SLOT, :] = (
-                dot(pick, chunk).astype(BF).reshape(NT, SLOT, 128)
-            )
-            extra = extra + dot(jnp.where(place == c, late, 0.0).astype(BF), chunk)
-        disp_ref[:, SLOT * CH : SROWS, :] = extra.astype(BF).reshape(NT, 16, 128)
-
-
-def project(att, weight, hidden, gain, ids_t):
+def merge_kernel(info_ref, own_ref, oth_ref, after_ref, o_ref):
+    zlo = info_ref[3]
+    o_ref[zlo] = own_ref[...]
+    o_ref[1 - zlo] = oth_ref[...]
+
+
+def merge(info, own, other, after):
+    return pl.pallas_call(
+        merge_kernel,
+        out_shape=jax.ShapeDtypeStruct((2,) + own.shape, BF),
+        in_specs=[
+            pl.BlockSpec(memory_space=pltpu.SMEM),
+            vmem(),
+            vmem(),
+            pl.BlockSpec(memory_space=pltpu.HBM),
+        ],
+        out_specs=vmem(),
+        cost_estimate=pl.CostEstimate(flops=1 << 33, bytes_accessed=1 << 20, transcendentals=0),
+        interpret=INTERPRET,
+        name="merge",
+    )(info, own, other, after)
+
+
+def project_kernel(info_ref, att_ref, wo_ref, wx_ref, hid_ref, gain_ref, ids_ref, res_ref, disp_ref, w, sems):
+    core = info_ref[1]
+    copies = []
+    for j in range(NT // 2):
+        for n, (src, side) in enumerate(((wo_ref, core), (wx_ref, 1 - core))):
+            at = pl.multiple_of((2 * j + side) * 48, 16)
+            copies.append(pltpu.make_async_copy(src.at[j], w.at[pl.ds(at, 48), :], sems.at[j, n]))
+    for copy in copies:
+        copy.start()
+
+    experts = iota((NT, TOK), 0)
+    named = jnp.zeros((NT, TOK), F32)
+    for k in range(TOPK):
+        named = named + jnp.where(ids_ref[k : k + 1, :] == experts, 1.0, 0.0)
+    before = jnp.where(iota((TOK, TOK), 0) < iota((TOK, TOK), 1), 1.0, 0.0).astype(BF)
+    rank = dot(named.astype(BF), before)
+    rank = jnp.where(named > 0.5, rank, -1.0).astype(BF)
+    spread = jnp.where(iota((512, NT), 0) // SLOT == iota((512, NT), 1), 1.0, 0.0).astype(BF)
+    ranks = dot(spread, rank)
+    place = iota((512, TOK), 0) % SLOT
+    pick = jnp.where(ranks == place.astype(F32), 1.0, 0.0).astype(BF)
+    late = jnp.where(ranks == float(SLOT), 1.0, 0.0)
+
+    total = hid_ref[...].astype(F32)
+    for g in range(HKV):
+        for copy in copies[4 * g : 4 * g + 4]:
+            copy.wait()
+        pair = att_ref[g * 4 : g * 4 + 4, 0:16, :].reshape(TOK, 128)
+        last = att_ref[g * 4 : g * 4 + 4, 16:32, :].reshape(TOK, 128)
+        row = g * 192
+        term = dot(pair, w[row : row + 128, :]) + dot(last[:, :HD], w[row + 128 : row + 192, :])
+        total = total + term.astype(BF).astype(F32)
+    res_ref[...] = total
+    meansq = jnp.mean(total * total, 1, keepdims=True)
+    normed = (total * lax.rsqrt(meansq + EPS) * gain_ref[...]).astype(BF)
+    extra = jnp.zeros((512, 128), F32)
+    for c in range(CH):
+        chunk = normed[:, c * 128 : c * 128 + 128]
+        disp_ref[:, c * SLOT : (c + 1) * SLOT, :] = (
+            dot(pick, chunk).astype(BF).reshape(NT, SLOT, 128)
+        )
+        extra = extra + dot(jnp.where(place == c, late, 0.0).astype(BF), chunk)
+    disp_ref[:, SLOT * CH : SROWS, :] = extra.astype(BF).reshape(NT, 16, 128)
+
+
+def project(info, att, own_weight, other_weight, hidden, gain, ids_t):
+    hbm = pl.BlockSpec(memory_space=pltpu.HBM)
     return pl.pallas_call(
         project_kernel,
         out_shape=(
             jax.ShapeDtypeStruct((TOK, D), F32),
             jax.ShapeDtypeStruct((NT, SROWS, 128), BF),
         ),
-        grid=(HKV,),
-        in_specs=[
-            vmem(),
-            pl.BlockSpec((192, D), lambda g: (g, 0)),
-            vmem(),
-            vmem(),
-            vmem(),
-        ],
+        in_specs=[pl.BlockSpec(memory_space=pltpu.SMEM), vmem(), hbm, hbm, vmem(), vmem(), vmem()],
         out_specs=(vmem(), vmem()),
-        compiler_params=params(32),
+        scratch_shapes=[
+            pltpu.VMEM((D, D), BF),
+            pltpu.SemaphoreType.DMA((NT // 2, 2)),
+        ],
+        compiler_params=params(61.7),
         cost_estimate=pl.CostEstimate(
             flops=2 * TOK * D * D, bytes_accessed=8 << 20, transcendentals=0
         ),
         interpret=INTERPRET,
         name="project",
-    )(att, weight, hidden, gain, ids_t)
+    )(info, att, own_weight, other_weight, hidden, gain, ids_t)
 
 
 def gather_extra(block):
@@ -271,18 +297,22 @@
         )
         for n, (src, dst) in enumerate(pieces):
             copies.append(pltpu.make_async_copy(src, dst, sems.at[d, n]))
-    for copy in copies:
+    firsts = [copy for i, copy in enumerate(copies) if i % 4 < 3]
+    lasts = copies[3::4]
+    for copy in firsts + lasts:
         copy.start()
     for c in range(CH):
         x[0:512, c * 128 : c * 128 + 128] = in_ref[:, c * SLOT : (c + 1) * SLOT, :].reshape(512, 128)
     chunks = gather_extra(in_ref[:, SLOT * CH : SROWS, :].reshape(512, 128))
     for c in range(CH):
         x[512:544, c * 128 : c * 128 + 128] = chunks[c]
-    for copy in copies:
+    for copy in firsts:
         copy.wait()
     hidden = dot(x[...], w1[...])
     gate = hidden[:, :FFE]
     active = (gate / (1.0 + jnp.exp(-gate)) * hidden[:, FFE:]).astype(BF)
+    for copy in lasts:
+        copy.wait()
     out = dot(active, w2[...]).astype(BF)
     for c in range(CH):
         o_ref[:, c * SLOT : (c + 1) * SLOT, :] = out[0:512, c * 128 : c * 128 + 128].reshape(
@@ -296,7 +326,7 @@
     return pl.pallas_call(
         expert_kernel,
         out_shape=jax.ShapeDtypeStruct((NT, SROWS, 128), BF),
-        in_specs=[vmem(), pl.BlockSpec(memory_space=pl.ANY)],
+        in_specs=[vmem(), pl.BlockSpec(memory_space=pltpu.HBM)],
         out_specs=vmem(),
         scratch_shapes=[
             pltpu.VMEM((544, D), BF),
@@ -304,7 +334,7 @@
             pltpu.VMEM((blocks * 32, D), BF),
             pltpu.SemaphoreType.DMA((blocks, 4)),
         ],
-        compiler_params=params(40),
+        compiler_params=params(59.5),
         cost_estimate=pl.CostEstimate(
             flops=2 * 544 * 1536 * 1536, bytes_accessed=9 << 20, transcendentals=544 * 512
         ),
@@ -377,23 +407,25 @@
     gates = route_gates[0, 0, 0]
 
     send = pack(rotated_queries[0, 0, 0], fresh_key_values[0, 0, 0], cached_key_values[0])
-    full_weight = lax.all_gather(output_weight, TEN, axis=0, tiled=True)
-    up = gate_up[0]
+    own_weight = lax.all_gather(output_weight, ("zhi", "x"), axis=0)
+    up, down, _ = lax.optimization_barrier((gate_up[0], down_weight[0], send))
     packed = jnp.concatenate(
-        [jnp.concatenate([up[:64], jnp.concatenate([up[64:, :512], up[64:, 512:]], 0)], 1), down_weight[0]], 0
+        [jnp.concatenate([up[:64], jnp.concatenate([up[64:, :512], up[64:, 512:]], 0)], 1), down], 0
     )
-    across = lax.ppermute(packed, "zlo", [(0, 1), (1, 0)])
-    both = jnp.where(
-        zlo == 0, jnp.stack([packed, across], 0), jnp.stack([across, packed], 0)
-    )
-    weights = lax.all_gather(both, "y", axis=0, tiled=True)
 
     own = lax.all_to_all(send, TEN, split_axis=0, concat_axis=0, tiled=True)
     other = lax.ppermute(own[:, 32:, :], "core", [(0, 1), (1, 0)])
-    info = jnp.stack([length, core.astype(jnp.int32), quarter.astype(jnp.int32)])
+    packed, _ = lax.optimization_barrier((packed, own))
+    across = lax.ppermute(packed, "zlo", [(0, 1), (1, 0)])
+    info = jnp.stack([length, core.astype(jnp.int32), quarter.astype(jnp.int32), zlo.astype(jnp.int32)])
     attended = attention(info, own, other)
+    both = merge(info, packed, across, attended)
+    weights = lax.all_gather(both, "y", axis=0, tiled=True)
+    swapping, _ = lax.optimization_barrier((own_weight, both))
+    other_weight = lax.ppermute(swapping, "core", [(0, 1), (1, 0)])
     att = lax.all_to_all(attended, TEN, split_axis=0, concat_axis=0, tiled=True)
-    residual, outbound = project(att, full_weight, hidden_in[0, 0, 0], norm_gain[None], ids.T)
+    residual, outbound = project(
+        info, att, own_weight, other_weight, hidden_in[0, 0, 0], norm_gain[None], ids.T)
     slots = lax.all_to_all(outbound, TEN, split_axis=0, concat_axis=0, tiled=True)
     computed = expert(slots, weights)
     returned = lax.all_to_all(computed, TEN, split_axis=0, concat_axis=0, tiled=True)

time: 232 us -> 235 us (1.013)
  blocking collectives: 37.1 us -> 0 us
  waiting for transfers between devices: 98.6 us -> 127 us
  starting transfers between devices: 30.3 us -> 46.1 us
  local copies, waits for them, and re-layouts: 15.9 us -> 7.95 us
  Pallas kernels: 29.3 us -> 34.4 us
  other arithmetic: 5.08 us -> 2.5 us
    all_to_all x1 -> x0, blocking collectives: 37.1 us -> none  [shards(): own = lax.all_to_all(send, TEN, split_axis=0, concat_axis=0, tiled=True)]
    all_gather x1, waiting for transfers between devices: 47.8 us -> 27.3 us  [shards(): weights = lax.all_gather(both, 'y', axis=0, tiled=True)]
    all_gather x1, waiting for transfers between devices: 0.01 us -> 19.3 us  [shards(): own_weight = lax.all_gather(output_weight, ('zhi', 'x'), axis=0)]
    all_to_all x0 -> x1, waiting for transfers between devices: none -> 18.9 us  [shards(): own = lax.all_to_all(send, TEN, split_axis=0, concat_axis=0, tiled=True)]
    all_to_all x1, waiting for transfers between devices: 0.01 us -> 15.3 us  [shards(): lax.all_to_all(outbound, TEN, split_axis=0, concat_axis=0, tiled=True)]
    all_to_all x0 -> x1, starting transfers between devices: none -> 14.4 us  [shards(): own = lax.all_to_all(send, TEN, split_axis=0, concat_axis=0, tiled=True)]
    all_to_all x1, starting transfers between devices: 10.6 us -> 5.95 us  [shards(): lax.all_to_all(computed, TEN, split_axis=0, concat_axis=0, tiled=True)]
    ppermute x1, waiting for transfers between devices: 4.09 us -> 0.01 us  [shards(): across = lax.ppermute(packed, 'zlo', [(0, 1), (1, 0)])]
  transfers between devices with their start and end apart: 7 -> 9, of which waited for: 5 -> 6; matrix products, arithmetic and copies ran while one was open for 7% -> 3% of each run, Pallas kernels for 8% -> 10%
where the time goes in v2:
time: 235 us; the launch traced here: 233 us
  waiting for transfers between devices  127 us (54%)
  starting transfers between devices  46.1 us (20%)
  Pallas kernels  34.4 us (15%)
  between operations  15 us (6%)
  local copies, waits for them, and re-layouts  7.95 us (3%)
  other arithmetic  2.5 us (1%)
    all_to_all x1, waiting for transfers between devices, shards(): lax.all_to_all(computed, TEN, split_axis=0, concat_axis=0, tiled=True)  33.5 us
    all_gather x1, waiting for transfers between devices, shards(): weights = lax.all_gather(both, 'y', axis=0, tiled=True)  27.3 us
    all_gather x1, waiting for transfers between devices, shards(): own_weight = lax.all_gather(output_weight, ('zhi', 'x'), axis=0)  19.3 us
    all_to_all x1, waiting for transfers between devices, shards(): own = lax.all_to_all(send, TEN, split_axis=0, concat_axis=0, tiled=True)  18.9 us
    all_to_all x1, waiting for transfers between devices, shards(): lax.all_to_all(outbound, TEN, split_axis=0, concat_axis=0, tiled=True)  15.3 us
    all_to_all x1, starting transfers between devices, shards(): own = lax.all_to_all(send, TEN, split_axis=0, concat_axis=0, tiled=True)  14.4 us
    all_to_all x1, waiting for transfers between devices, shards(): att = lax.all_to_all(attended, TEN, split_axis=0, concat_axis=0, tiled=True)  12.4 us
    pallas_call x1, Pallas kernels, attention(): pl.pallas_call(attention_kernel, out_shape=jax.ShapeDtypeStruct((NT, 32,...  11.8 us
  transfers between devices with their start and end apart: 9, of which 6 were waited for; matrix products, arithmetic and copies ran while one was open for 3% of the time, Pallas kernels for 10%

profile of v2, /device:TPU:1, one launch (start us, length us, event | category | flops | bytes accessed | tf_op | source)
XLA Modules:
  0.0 233.2 jit_solution(16313702448825609955)
XLA Ops:
  7.9 2.0 pack.1
  9.9 14.4 %all-to-all-start = ((bf16[32,80,128]{2,1,0:T(8,128)(2,1)}), bf16[32,80,128]{2,1,0:T(8,128)(2,1)S(1)}, u32[]{:S(2)}, u32[]{:S(2)}) async-start(bf16[32,80,128]{2,1,0:T(8,128)(2,1)} %pack.1), calls=%async_computation | async-start | bytes 1310720 | tf_op jit(solution)/shard_map/all_to_all | solution.py:416
  24.4 18.9 %all-to-all-done.own_ref = bf16[32,80,128]{2,1,0:T(8,128)(2,1)S(1)} async-done(((bf16[32,80,128]{2,1,0:T(8,128)(2,1)}), bf16[32,80,128]{2,1,0:T(8,128)(2,1)S(1)}, u32[]{:S(2)}, u32[]{:S(2)}) %all-to-all-start) | async-done | bytes 655392 | tf_op jit(solution)/shard_map/all_to_all | solution.py:416
  43.3 2.4 %collective-permute-start = (bf16[32,48,128]{2,1,0:T(8,128)(2,1)S(1)}, bf16[32,48,128]{2,1,0:T(8,128)(2,1)S(1)}, u32[]{:S(2)}, u32[]{:S(2)}) collective-permute-start(bf16[32,48,128]{2,1,0:T(8,128)(2,1)S(1)} %slice.25), channel_id=1, source_target_pairs={{0,1},{1,0},{2,3},{3,2},{4,5},{5,4},{6,7},{7,6},{8,9},{9,8},{10,11... | collective-permute-start | bytes 1179656 | tf_op jit(solution)/shard_map/ppermute | solution.py:417
  45.8 8.4 %collective-permute-start.1 = (bf16[96,1536]{1,0:T(8,128)(2,1)S(1)}, bf16[96,1536]{1,0:T(8,128)(2,1)S(1)}, u32[]{:S(2)}, u32[]{:S(2)}) collective-permute-start(bf16[96,1536]{1,0:T(8,128)(2,1)S(1)} %pad_maximum_fusion.own_ref), channel_id=1, source_target_pairs={{0,32},{32,0},{1,33},{33,1},{2,34},{34,2},{3,35},{35,3},{4,36},{36... | collective-permute-start | bytes 884744 | tf_op jit(solution)/shard_map/ppermute | solution.py:419
  55.0 11.8 %attention.1.after_ref = bf16[32,32,128]{2,1,0:T(8,128)(2,1)} custom-call(s32[4]{0:T(128)S(1)} %pad_add_fusion.info_ref, bf16[32,80,128]{2,1,0:T(8,128)(2,1)S(1)} %all-to-all-done.own_ref, bf16[32,48,128]{2,1,0:T(8,128)(2,1)S(1)} %collective-permute-done.oth_ref), custom_call_target="tpu_custom_call" | custom-call | flops 1811939328 | bytes 3145728 | tf_op jit(solution)/shard_map/attention/pallas_call | solution.py:154
  67.5 1.9 merge.1
  69.5 19.3 %all-gather.6.cloned.1.call-done = bf16[768,1536]{1,0:T(8,128)(2,1)} async-done(((bf16[48,1536]{1,0:T(8,128)(2,1)}), bf16[768,1536]{1,0:T(8,128)(2,1)}) %all-gather.6.cloned.1.call-update) | async-done | bytes 2359312 | tf_op jit(solution)/shard_map/all_gather | solution.py:410
  88.8 3.3 %collective-permute-start.2 = (bf16[16,48,1536]{2,1,0:T(8,128)(2,1)}, bf16[16,48,1536]{2,1,0:T(8,128)(2,1)}, u32[]{:S(2)}, u32[]{:S(2)}) collective-permute-start(bf16[16,48,1536]{2,1,0:T(8,128)(2,1)} %bitcast.30), channel_id=1, source_target_pairs={{0,1},{1,0},{2,3},{3,2},{4,5},{5,4},{6,7},{7,6},{8,9},{9,8},{10,11... | collective-permute-start | bytes 7077896 | tf_op jit(solution)/shard_map/ppermute | solution.py:425
  92.1 6.9 %all-to-all-start.1 = ((bf16[32,32,128]{2,1,0:T(8,128)(2,1)}), bf16[32,32,128]{2,1,0:T(8,128)(2,1)S(1)}, u32[]{:S(2)}, u32[]{:S(2)}) async-start(bf16[32,32,128]{2,1,0:T(8,128)(2,1)} %attention.1.after_ref), calls=%async_computation.1 | async-start | bytes 524288 | tf_op jit(solution)/shard_map/all_to_all | solution.py:426
  99.6 12.4 %all-to-all-done.1.att_ref = bf16[32,32,128]{2,1,0:T(8,128)(2,1)S(1)} async-done(((bf16[32,32,128]{2,1,0:T(8,128)(2,1)}), bf16[32,32,128]{2,1,0:T(8,128)(2,1)S(1)}, u32[]{:S(2)}, u32[]{:S(2)}) %all-to-all-start.1) | async-done | bytes 262176 | tf_op jit(solution)/shard_map/all_to_all | solution.py:426
  112.7 7.2 %project.1 = (f32[64,1536]{1,0:T(8,128)}, bf16[32,208,128]{2,1,0:T(8,128)(2,1)}) custom-call(s32[4]{0:T(128)} %copy-done.1, bf16[32,32,128]{2,1,0:T(8,128)(2,1)} %copy-done.3, bf16[16,48,1536]{2,1,0:T(8,128)(2,1)} %bitcast.31, bf16[16,48,1536]{2,1,0:T(8,128)(2,1)} %collective-permute-done.2.wx_ref, bf16[64,1536]{1,0:T(8,128)(2,1)} %bitcast.36, ...), custom_call_target="tpu_custom_call" | custom-call | flops 301989888 | bytes 8388608 | tf_op jit(solution)/shard_map/project/pallas_call | solution.py:249
  119.8 4.6 %all-to-all-start.2 = ((bf16[32,208,128]{2,1,0:T(8,128)(2,1)}), bf16[32,208,128]{2,1,0:T(8,128)(2,1)S(1)}, u32[]{:S(2)}, u32[]{:S(2)}) async-start(bf16[32,208,128]{2,1,0:T(8,128)(2,1)} %get-tuple-element.12), calls=%async_computation.2 | async-start | bytes 3407872 | tf_op jit(solution)/shard_map/all_to_all | solution.py:429
  124.4 27.3 %all-gather.4.cloned.1.call-done.w_ref = bf16[16,96,1536]{2,1,0:T(8,128)(2,1)} async-done(((bf16[2,96,1536]{2,1,0:T(8,128)(2,1)}), bf16[16,96,1536]{2,1,0:T(8,128)(2,1)}) %all-gather.4.cloned.1.call-update) | async-done | bytes 4718608 | tf_op jit(solution)/shard_map/all_gather | solution.py:423
  151.7 15.3 %all-to-all-done.2.in_ref = bf16[32,208,128]{2,1,0:T(8,128)(2,1)S(1)} async-done(((bf16[32,208,128]{2,1,0:T(8,128)(2,1)}), bf16[32,208,128]{2,1,0:T(8,128)(2,1)S(1)}, u32[]{:S(2)}, u32[]{:S(2)}) %all-to-all-start.2) | async-done | bytes 1703968 | tf_op jit(solution)/shard_map/all_to_all | solution.py:429
  167.0 1.2 copy-done.2
  168.2 9.5 %expert.1 = bf16[32,208,128]{2,1,0:T(8,128)(2,1)} custom-call(bf16[32,208,128]{2,1,0:T(8,128)(2,1)} %copy-done.2, bf16[16,96,1536]{2,1,0:T(8,128)(2,1)} %all-gather.4.cloned.1.call-done.w_ref), custom_call_target="tpu_custom_call" | custom-call | flops 2566914048 | bytes 9437184 | tf_op jit(solution)/shard_map/expert/pallas_call | solution.py:326
  177.8 6.0 %all-to-all-start.3 = ((bf16[32,208,128]{2,1,0:T(8,128)(2,1)}), bf16[32,208,128]{2,1,0:T(8,128)(2,1)S(1)}, u32[]{:S(2)}, u32[]{:S(2)}) async-start(bf16[32,208,128]{2,1,0:T(8,128)(2,1)} %expert.1), calls=%async_computation.3 | async-start | bytes 3407872 | tf_op jit(solution)/shard_map/all_to_all | solution.py:431
  185.1 0.9 copy.39
  186.3 2.2 select_bitcast_fusion
  188.5 1.4 dynamic_update_slice.4
  189.9 0.9 copy.42
  190.9 33.5 %all-to-all-done.3.in_ref = bf16[32,208,128]{2,1,0:T(8,128)(2,1)S(1)} async-done(((bf16[32,208,128]{2,1,0:T(8,128)(2,1)}), bf16[32,208,128]{2,1,0:T(8,128)(2,1)S(1)}, u32[]{:S(2)}, u32[]{:S(2)}) %all-to-all-start.3) | async-done | bytes 1703968 | tf_op jit(solution)/shard_map/all_to_all | solution.py:431
  224.4 2.0 combine.1
  (44 shorter events, 4.6 us)
Async XLA Ops:
  7.2 38.6 %copy-start.5 = (bf16[1,96,1024]{2,1,0:T(8,128)(2,1)S(1)}, bf16[1,96,1024]{2,1,0:T(8,128)(2,1)}, u32[]{:S(2)}) copy-start(bf16[1,96,1024]{2,1,0:T(8,128)(2,1)} %param.20) | copy-start | bytes 589828
  7.2 81.6 %all-gather.6.cloned.1.call-start = ((), (), s32[]{:S(2)}) async-start(), calls=%async_computation.5 | async-start | bytes 2506752 | tf_op jit(solution)/shard_map/all_gather | solution.py:410
  7.9 37.9 %copy-start.6 = (bf16[1,32,1536]{2,1,0:T(8,128)(2,1)S(1)}, bf16[1,32,1536]{2,1,0:T(8,128)(2,1)}, u32[]{:S(2)}) copy-start(bf16[1,32,1536]{2,1,0:T(8,128)(2,1)} %param.21) | copy-start | bytes 294916
  9.9 33.4 %all-to-all-start = ((bf16[32,80,128]{2,1,0:T(8,128)(2,1)}), bf16[32,80,128]{2,1,0:T(8,128)(2,1)S(1)}, u32[]{:S(2)}, u32[]{:S(2)}) async-start(bf16[32,80,128]{2,1,0:T(8,128)(2,1)} %pack.1), calls=%async_computation | async-start | bytes 1310720 | tf_op jit(solution)/shard_map/all_to_all | solution.py:416
  24.3 127.4 %all-gather.4.cloned.1.call-start = ((), (), s32[]{:S(2)}) async-start(), calls=%async_computation.4 | async-start | bytes 5308416 | tf_op jit(solution)/shard_map/all_gather | solution.py:423
  43.3 11.7 %collective-permute-start = (bf16[32,48,128]{2,1,0:T(8,128)(2,1)S(1)}, bf16[32,48,128]{2,1,0:T(8,128)(2,1)S(1)}, u32[]{:S(2)}, u32[]{:S(2)}) collective-permute-start(bf16[32,48,128]{2,1,0:T(8,128)(2,1)S(1)} %slice.25), channel_id=1, source_target_pairs={{0,1},{1,0},{2,3},{3,2},{4,5},{5,4},{6,7},{7,6},{8,9},{9,8},{10,11... | collective-permute-start | bytes 1179656 | tf_op jit(solution)/shard_map/ppermute | solution.py:417
  45.8 21.0 %copy-start.4 = (bf16[96,1536]{1,0:T(8,128)(2,1)}, bf16[96,1536]{1,0:T(8,128)(2,1)S(1)}, u32[]{:S(2)}) copy-start(bf16[96,1536]{1,0:T(8,128)(2,1)S(1)} %pad_maximum_fusion.own_ref) | copy-start | bytes 884740
  45.8 21.0 %collective-permute-start.1 = (bf16[96,1536]{1,0:T(8,128)(2,1)S(1)}, bf16[96,1536]{1,0:T(8,128)(2,1)S(1)}, u32[]{:S(2)}, u32[]{:S(2)}) collective-permute-start(bf16[96,1536]{1,0:T(8,128)(2,1)S(1)} %pad_maximum_fusion.own_ref), channel_id=1, source_target_pairs={{0,32},{32,0},{1,33},{33,1},{2,34},{34,2},{3,35},{35,3},{4,36},{36... | collective-permute-start | bytes 884744 | tf_op jit(solution)/shard_map/ppermute | solution.py:419
  55.0 11.8 %copy-start.1 = (s32[4]{0:T(128)}, s32[4]{0:T(128)S(1)}, u32[]{:S(2)}) copy-start(s32[4]{0:T(128)S(1)} %pad_add_fusion.info_ref) | copy-start | bytes 52
  66.8 32.2 %copy-start.8 = (f32[1536]{0:T(1024)S(1)}, f32[1536]{0:T(1024)}, u32[]{:S(2)}) copy-start(f32[1536]{0:T(1024)} %param.19) | copy-start | bytes 18436
  66.8 0.7 copy-start.10
  88.8 23.2 %collective-permute-start.2 = (bf16[16,48,1536]{2,1,0:T(8,128)(2,1)}, bf16[16,48,1536]{2,1,0:T(8,128)(2,1)}, u32[]{:S(2)}, u32[]{:S(2)}) collective-permute-start(bf16[16,48,1536]{2,1,0:T(8,128)(2,1)} %bitcast.30), channel_id=1, source_target_pairs={{0,1},{1,0},{2,3},{3,2},{4,5},{5,4},{6,7},{7,6},{8,9},{9,8},{10,11... | collective-permute-start | bytes 7077896 | tf_op jit(solution)/shard_map/ppermute | solution.py:425
  92.1 19.8 %all-to-all-start.1 = ((bf16[32,32,128]{2,1,0:T(8,128)(2,1)}), bf16[32,32,128]{2,1,0:T(8,128)(2,1)S(1)}, u32[]{:S(2)}, u32[]{:S(2)}) async-start(bf16[32,32,128]{2,1,0:T(8,128)(2,1)} %attention.1.after_ref), calls=%async_computation.1 | async-start | bytes 524288 | tf_op jit(solution)/shard_map/all_to_all | solution.py:426
  112.0 0.7 copy-start.3
  119.8 47.2 %all-to-all-start.2 = ((bf16[32,208,128]{2,1,0:T(8,128)(2,1)}), bf16[32,208,128]{2,1,0:T(8,128)(2,1)S(1)}, u32[]{:S(2)}, u32[]{:S(2)}) async-start(bf16[32,208,128]{2,1,0:T(8,128)(2,1)} %get-tuple-element.12), calls=%async_computation.2 | async-start | bytes 3407872 | tf_op jit(solution)/shard_map/all_to_all | solution.py:429
  167.0 1.2 copy-start.2
  177.8 6.0 %copy-start.7 = (s32[1,1,1,64,8]{3,4,2,1,0:T(8,128)S(1)}, s32[1,1,1,64,8]{3,4,2,1,0:T(8,128)}, u32[]{:S(2)}) copy-start(s32[1,1,1,64,8]{3,4,2,1,0:T(8,128)} %param.16) | copy-start | bytes 6148
  177.8 6.1 %copy-start.9 = (f32[1,1,1,64,8]{3,4,2,1,0:T(8,128)S(1)}, f32[1,1,1,64,8]{3,4,2,1,0:T(8,128)}, u32[]{:S(2)}) copy-start(f32[1,1,1,64,8]{3,4,2,1,0:T(8,128)} %param.17) | copy-start | bytes 6148
  177.8 46.6 %all-to-all-start.3 = ((bf16[32,208,128]{2,1,0:T(8,128)(2,1)}), bf16[32,208,128]{2,1,0:T(8,128)(2,1)S(1)}, u32[]{:S(2)}, u32[]{:S(2)}) async-start(bf16[32,208,128]{2,1,0:T(8,128)(2,1)} %expert.1), calls=%async_computation.3 | async-start | bytes 3407872 | tf_op jit(solution)/shard_map/all_to_all | solution.py:431
  186.3 38.1 %copy-start = (f32[64,1536]{1,0:T(8,128)S(1)}, f32[64,1536]{1,0:T(8,128)}, u32[]{:S(2)}) copy-start(f32[64,1536]{1,0:T(8,128)} %get-tuple-element.13.res_ref) | copy-start | bytes 1179652
Sparse Core Ops, SparseCore 0:
  11.0 77.7 all-gather.5
  90.9 60.7 all-gather.3

commit v3 on v2

--- a/solution.py
+++ b/solution.py
@@ -190,7 +190,7 @@
             pl.BlockSpec(memory_space=pltpu.SMEM),
             vmem(),
             vmem(),
-            pl.BlockSpec(memory_space=pltpu.HBM),
+            pl.BlockSpec(memory_space=pl.ANY),
         ],
         out_specs=vmem(),
         cost_estimate=pl.CostEstimate(flops=1 << 33, bytes_accessed=1 << 20, transcendentals=0),
@@ -199,15 +199,78 @@
     )(info, own, other, after)
 
 
-def project_kernel(info_ref, att_ref, wo_ref, wx_ref, hid_ref, gain_ref, ids_ref, res_ref, disp_ref, w, sems):
-    core = info_ref[1]
+def prepare_kernel(up_ref, down_ref, w_ref, after_ref, o_ref, wo_ref):
+    o_ref[0:64, 0:1024] = up_ref[0:64, :]
+    o_ref[0:32, 1024:1536] = up_ref[64:96, 0:512]
+    o_ref[32:64, 1024:1536] = up_ref[64:96, 512:1024]
+    o_ref[64:96, :] = down_ref[...]
+    wo_ref[...] = w_ref[...]
+
+
+def prepare(up, down, weight, after):
+    return pl.pallas_call(
+        prepare_kernel,
+        out_shape=(jax.ShapeDtypeStruct((96, D), BF), jax.ShapeDtypeStruct(weight.shape, BF)),
+        in_specs=[vmem()] * 3 + [pl.BlockSpec(memory_space=pl.ANY)],
+        out_specs=(vmem(), vmem()),
+        cost_estimate=pl.CostEstimate(flops=1 << 33, bytes_accessed=1 << 20, transcendentals=0),
+        interpret=INTERPRET,
+        name="prepare",
+    )(up, down, weight, after)
+
+
+def load_weight(src_ref, zhi, w, sems):
     copies = []
     for j in range(NT // 2):
-        for n, (src, side) in enumerate(((wo_ref, core), (wx_ref, 1 - core))):
-            at = pl.multiple_of((2 * j + side) * 48, 16)
-            copies.append(pltpu.make_async_copy(src.at[j], w.at[pl.ds(at, 48), :], sems.at[j, n]))
+        turn = (zhi + 4 - j // 4) % 4
+        copies.append(
+            pltpu.make_async_copy(src_ref.at[j % 4, turn], w.at[j * 48 : j * 48 + 48, :], sems.at[j])
+        )
+        copies[-1].start()
+    return copies
+
+
+def columns(att_ref, side):
+    pieces = []
+    for g in range(HKV):
+        pair = att_ref[g * 4 : g * 4 + 4, 0:16, :].reshape(TOK, 128).astype(F32)
+        last = att_ref[g * 4 : g * 4 + 4, 16:32, :].reshape(TOK, 128).astype(F32)
+        every = jnp.concatenate([pair, last[:, :HD]], 1)
+        for x in range(2):
+            at = x * 96
+            pieces.append(jnp.where(side == 0, every[:, at : at + 48], every[:, at + 48 : at + 96]))
+    return jnp.concatenate(pieces, 1).astype(BF)
+
+
+def own_part_kernel(info_ref, att_ref, w_ref, o_ref, w, sems):
+    copies = load_weight(w_ref, info_ref[4], w, sems)
+    cols = columns(att_ref, info_ref[1])
     for copy in copies:
-        copy.start()
+        copy.wait()
+    o_ref[...] = dot(cols, w[...])
+
+
+def own_part(info, att, weight):
+    return pl.pallas_call(
+        own_part_kernel,
+        out_shape=jax.ShapeDtypeStruct((TOK, D), F32),
+        in_specs=[
+            pl.BlockSpec(memory_space=pltpu.SMEM),
+            vmem(),
+            pl.BlockSpec(memory_space=pltpu.HBM),
+        ],
+        out_specs=vmem(),
+        scratch_shapes=[pltpu.VMEM((D // 2, D), BF), pltpu.SemaphoreType.DMA((NT // 2,))],
+        compiler_params=params(61.7),
+        cost_estimate=pl.CostEstimate(flops=1 << 34, bytes_accessed=3 << 20, transcendentals=0),
+        interpret=INTERPRET,
+        name="own_part",
+    )(info, att, weight)
+
+
+def project_kernel(info_ref, att_ref, part_ref, w_ref, hid_ref, gain_ref, ids_ref, res_ref, disp_ref, w, sems):
+    copies = load_weight(w_ref, info_ref[4], w, sems)
+    cols = columns(att_ref, 1 - info_ref[1])
 
     experts = iota((NT, TOK), 0)
     named = jnp.zeros((NT, TOK), F32)
@@ -222,15 +285,10 @@
     pick = jnp.where(ranks == place.astype(F32), 1.0, 0.0).astype(BF)
     late = jnp.where(ranks == float(SLOT), 1.0, 0.0)
 
-    total = hid_ref[...].astype(F32)
-    for g in range(HKV):
-        for copy in copies[4 * g : 4 * g + 4]:
-            copy.wait()
-        pair = att_ref[g * 4 : g * 4 + 4, 0:16, :].reshape(TOK, 128)
-        last = att_ref[g * 4 : g * 4 + 4, 16:32, :].reshape(TOK, 128)
-        row = g * 192
-        term = dot(pair, w[row : row + 128, :]) + dot(last[:, :HD], w[row + 128 : row + 192, :])
-        total = total + term.astype(BF).astype(F32)
+    base = hid_ref[...].astype(F32) + part_ref[...]
+    for copy in copies:
+        copy.wait()
+    total = base + dot(cols, w[...])
     res_ref[...] = total
     meansq = jnp.mean(total * total, 1, keepdims=True)
     normed = (total * lax.rsqrt(meansq + EPS) * gain_ref[...]).astype(BF)
@@ -244,27 +302,31 @@
     disp_ref[:, SLOT * CH : SROWS, :] = extra.astype(BF).reshape(NT, 16, 128)
 
 
-def project(info, att, own_weight, other_weight, hidden, gain, ids_t):
-    hbm = pl.BlockSpec(memory_space=pltpu.HBM)
+def project(info, att, part, weight, hidden, gain, ids_t):
     return pl.pallas_call(
         project_kernel,
         out_shape=(
             jax.ShapeDtypeStruct((TOK, D), F32),
             jax.ShapeDtypeStruct((NT, SROWS, 128), BF),
         ),
-        in_specs=[pl.BlockSpec(memory_space=pltpu.SMEM), vmem(), hbm, hbm, vmem(), vmem(), vmem()],
+        in_specs=[
+            pl.BlockSpec(memory_space=pltpu.SMEM),
+            vmem(),
+            vmem(),
+            pl.BlockSpec(memory_space=pltpu.HBM),
+            vmem(),
+            vmem(),
+            vmem(),
+        ],
         out_specs=(vmem(), vmem()),
-        scratch_shapes=[
-            pltpu.VMEM((D, D), BF),
-            pltpu.SemaphoreType.DMA((NT // 2, 2)),
-        ],
+        scratch_shapes=[pltpu.VMEM((D // 2, D), BF), pltpu.SemaphoreType.DMA((NT // 2,))],
         compiler_params=params(61.7),
         cost_estimate=pl.CostEstimate(
             flops=2 * TOK * D * D, bytes_accessed=8 << 20, transcendentals=0
         ),
         interpret=INTERPRET,
         name="project",
-    )(info, att, own_weight, other_weight, hidden, gain, ids_t)
+    )(info, att, part, weight, hidden, gain, ids_t)
 
 
 def gather_extra(block):
@@ -400,6 +462,7 @@
     down_weight,
 ):
     zlo = lax.axis_index("zlo")
+    zhi = lax.axis_index("zhi")
     core = lax.axis_index("core")
     quarter = lax.axis_index(TEN) % 4
     length = cached_len[0]
@@ -407,25 +470,29 @@
     gates = route_gates[0, 0, 0]
 
     send = pack(rotated_queries[0, 0, 0], fresh_key_values[0, 0, 0], cached_key_values[0])
-    own_weight = lax.all_gather(output_weight, ("zhi", "x"), axis=0)
-    up, down, _ = lax.optimization_barrier((gate_up[0], down_weight[0], send))
-    packed = jnp.concatenate(
-        [jnp.concatenate([up[:64], jnp.concatenate([up[64:, :512], up[64:, 512:]], 0)], 1), down], 0
+    packed, shard = prepare(gate_up[0], down_weight[0], output_weight, send)
+    across = lax.ppermute(packed, "zlo", [(0, 1), (1, 0)])
+    turns = [
+        lax.ppermute(shard, "zhi", [(z, (z + step) % 4) for z in range(4)]) for step in (1, 3, 2)
+    ]
+    own = lax.all_to_all(send, TEN, split_axis=0, concat_axis=0, tiled=True)
+    (shard, back1, back3, back2, across), _ = lax.optimization_barrier(
+        ((shard, *turns, across), own)
     )
-
-    own = lax.all_to_all(send, TEN, split_axis=0, concat_axis=0, tiled=True)
+    column = jnp.stack([shard, back1, back2, back3], 0)
+    own_weight = lax.all_gather(column, "x", axis=0)
     other = lax.ppermute(own[:, 32:, :], "core", [(0, 1), (1, 0)])
-    packed, _ = lax.optimization_barrier((packed, own))
-    across = lax.ppermute(packed, "zlo", [(0, 1), (1, 0)])
-    info = jnp.stack([length, core.astype(jnp.int32), quarter.astype(jnp.int32), zlo.astype(jnp.int32)])
+    info = jnp.stack([length, core.astype(jnp.int32), quarter.astype(jnp.int32), zlo.astype(jnp.int32), zhi.astype(jnp.int32)])
     attended = attention(info, own, other)
     both = merge(info, packed, across, attended)
     weights = lax.all_gather(both, "y", axis=0, tiled=True)
-    swapping, _ = lax.optimization_barrier((own_weight, both))
+    att = lax.all_to_all(attended, TEN, split_axis=0, concat_axis=0, tiled=True)
+    swapping, _ = lax.optimization_barrier((own_weight, att))
     other_weight = lax.ppermute(swapping, "core", [(0, 1), (1, 0)])
-    att = lax.all_to_all(attended, TEN, split_axis=0, concat_axis=0, tiled=True)
+    part = own_part(info, att, own_weight)
     residual, outbound = project(
-        info, att, own_weight, other_weight, hidden_in[0, 0, 0], norm_gain[None], ids.T)
+        info, att, part, other_weight, hidden_in[0, 0, 0], norm_gain[None], ids.T
+    )
     slots = lax.all_to_all(outbound, TEN, split_axis=0, concat_axis=0, tiled=True)
     computed = expert(slots, weights)
     returned = lax.all_to_all(computed, TEN, split_axis=0, concat_axis=0, tiled=True)

time: 235 us -> 241 us (1.026)
  waiting for transfers between devices: 127 us -> 96.4 us
  blocking collectives: 0 us -> 21.6 us
  starting transfers between devices: 46.1 us -> 56.5 us
  Pallas kernels: 34.4 us -> 38.5 us
    all_to_all x0 -> x1, blocking collectives: none -> 21.6 us  [shards(): att = lax.all_to_all(attended, TEN, split_axis=0, concat_axis=0, tiled=True)]
    all_to_all x1, waiting for transfers between devices: 18.9 us -> 0.01 us  [shards(): own = lax.all_to_all(send, TEN, split_axis=0, concat_axis=0, tiled=True)]
    all_gather x1, waiting for transfers between devices: 19.3 us -> 0.94 us  [shards(): own_weight = lax.all_gather(column, 'x', axis=0)]
    ppermute x0 -> x3, waiting for transfers between devices: none -> 16.6 us  [shards(): lax.ppermute(shard, 'zhi', [(z, (z + step) % 4) for z in range(4)])]
    all_gather x1, waiting for transfers between devices: 27.3 us -> 42 us  [shards(): weights = lax.all_gather(both, 'y', axis=0, tiled=True)]
    all_to_all x1, waiting for transfers between devices: 15.3 us -> 0.7 us  [shards(): lax.all_to_all(outbound, TEN, split_axis=0, concat_axis=0, tiled=True)]
    ppermute x0 -> x3, starting transfers between devices: none -> 14.6 us  [shards(): lax.ppermute(shard, 'zhi', [(z, (z + step) % 4) for z in range(4)])]
    all_to_all x1 -> x0, waiting for transfers between devices: 12.4 us -> none  [shards(): att = lax.all_to_all(attended, TEN, split_axis=0, concat_axis=0, tiled=True)]
  transfers between devices with their start and end apart: 9 -> 11, of which waited for: 6 -> 7; matrix products, arithmetic and copies ran while one was open for 3% -> 3% of each run, Pallas kernels for 10% -> 10%
where the time goes in v3:
time: 241 us; the launch traced here: 240 us
  waiting for transfers between devices  96.4 us (40%)
  starting transfers between devices  56.5 us (23%)
  Pallas kernels  38.5 us (16%)
  blocking collectives  21.6 us (9%)
  between operations  15 us (6%)
  local copies, waits for them, and re-layouts  7.45 us (3%)
  other arithmetic  4.36 us (2%)
    all_gather x1, waiting for transfers between devices, shards(): weights = lax.all_gather(both, 'y', axis=0, tiled=True)  42 us
    all_to_all x1, waiting for transfers between devices, shards(): lax.all_to_all(computed, TEN, split_axis=0, concat_axis=0, tiled=True)  35.5 us
    all_to_all x1, blocking collectives, shards(): att = lax.all_to_all(attended, TEN, split_axis=0, concat_axis=0, tiled=True)  21.6 us
    ppermute x3, waiting for transfers between devices, shards(): lax.ppermute(shard, 'zhi', [(z, (z + step) % 4) for z in range(4)])  16.6 us
    ppermute x3, starting transfers between devices, shards(): lax.ppermute(shard, 'zhi', [(z, (z + step) % 4) for z in range(4)])  14.6 us
    all_to_all x1, starting transfers between devices, shards(): own = lax.all_to_all(send, TEN, split_axis=0, concat_axis=0, tiled=True)  14.4 us
    pallas_call x1, Pallas kernels, attention(): pl.pallas_call(attention_kernel, out_shape=jax.ShapeDtypeStruct((NT, 32,...  11.1 us
    all_to_all x1, starting transfers between devices, shards(): lax.all_to_all(computed, TEN, split_axis=0, concat_axis=0, tiled=True)  9.95 us
  transfers between devices with their start and end apart: 11, of which 7 were waited for; matrix products, arithmetic and copies ran while one was open for 3% of the time, Pallas kernels for 10%

profile of v3, /device:TPU:1, one launch (start us, length us, event | category | flops | bytes accessed | tf_op | source)
XLA Modules:
  0.0 239.8 jit_solution(17683172194024036151)
XLA Ops:
  7.2 2.0 pack.1.after_ref
  9.1 14.4 %all-to-all-start = ((bf16[32,80,128]{2,1,0:T(8,128)(2,1)}), bf16[32,80,128]{2,1,0:T(8,128)(2,1)S(1)}, u32[]{:S(2)}, u32[]{:S(2)}) async-start(bf16[32,80,128]{2,1,0:T(8,128)(2,1)} %pack.1.after_ref), calls=%async_computation | async-start | bytes 1310720 | tf_op jit(solution)/shard_map/all_to_all | solution.py:478
  23.6 1.8 prepare.1
  25.5 3.1 %collective-permute-start.4 = (bf16[96,1536]{1,0:T(8,128)(2,1)}, bf16[96,1536]{1,0:T(8,128)(2,1)S(1)}, u32[]{:S(2)}, u32[]{:S(2)}) collective-permute-start(bf16[96,1536]{1,0:T(8,128)(2,1)} %get-tuple-element.13.own_ref), channel_id=1, source_target_pairs={{0,32},{32,0},{1,33},{33,1},{2,34},{34,2},{3,35},{35,3},{4,36},{36... | collective-permute-start | bytes 884744 | tf_op jit(solution)/shard_map/ppermute | solution.py:474
  28.6 4.2 %collective-permute-start.1 = (bf16[48,1536]{1,0:T(8,128)(2,1)}, bf16[48,1536]{1,0:T(8,128)(2,1)S(1)}, u32[]{:S(2)}, u32[]{:S(2)}) collective-permute-start(bf16[48,1536]{1,0:T(8,128)(2,1)} %get-tuple-element.14), channel_id=1, source_target_pairs={{0,8},{8,16},{16,24},{24,0},{1,9},{9,17},{17,25},{25,1},{2,10},{10... | collective-permute-start | bytes 442376 | tf_op jit(solution)/shard_map/ppermute | solution.py:476
  32.8 3.2 %collective-permute-start.2 = (bf16[48,1536]{1,0:T(8,128)(2,1)}, bf16[48,1536]{1,0:T(8,128)(2,1)S(1)}, u32[]{:S(2)}, u32[]{:S(2)}) collective-permute-start(bf16[48,1536]{1,0:T(8,128)(2,1)} %get-tuple-element.14), channel_id=1, source_target_pairs={{0,24},{8,0},{16,8},{24,16},{1,25},{9,1},{17,9},{25,17},{2,26},{10... | collective-permute-start | bytes 442376 | tf_op jit(solution)/shard_map/ppermute | solution.py:476
  36.0 7.2 %collective-permute-start.3 = (bf16[48,1536]{1,0:T(8,128)(2,1)}, bf16[48,1536]{1,0:T(8,128)(2,1)S(1)}, u32[]{:S(2)}, u32[]{:S(2)}) collective-permute-start(bf16[48,1536]{1,0:T(8,128)(2,1)} %get-tuple-element.14), channel_id=1, source_target_pairs={{0,16},{8,24},{16,0},{24,8},{1,17},{9,25},{17,1},{25,9},{2,18},{10... | collective-permute-start | bytes 442376 | tf_op jit(solution)/shard_map/ppermute | solution.py:476
  43.2 11.5 %collective-permute-done.1 = bf16[48,1536]{1,0:T(8,128)(2,1)S(1)} collective-permute-done((bf16[48,1536]{1,0:T(8,128)(2,1)}, bf16[48,1536]{1,0:T(8,128)(2,1)S(1)}, u32[]{:S(2)}, u32[]{:S(2)}) %collective-permute-start.1) | collective-permute-done | bytes 147488 | tf_op jit(solution)/shard_map/ppermute | solution.py:476
  54.7 5.1 %collective-permute-done.3 = bf16[48,1536]{1,0:T(8,128)(2,1)S(1)} collective-permute-done((bf16[48,1536]{1,0:T(8,128)(2,1)}, bf16[48,1536]{1,0:T(8,128)(2,1)S(1)}, u32[]{:S(2)}, u32[]{:S(2)}) %collective-permute-start.3) | collective-permute-done | bytes 147488 | tf_op jit(solution)/shard_map/ppermute | solution.py:476
  59.8 2.0 pad_maximum_fusion
  61.9 2.9 %collective-permute-start = (bf16[32,48,128]{2,1,0:T(8,128)(2,1)S(1)}, bf16[32,48,128]{2,1,0:T(8,128)(2,1)S(1)}, u32[]{:S(2)}, u32[]{:S(2)}) collective-permute-start(bf16[32,48,128]{2,1,0:T(8,128)(2,1)S(1)} %slice.13), channel_id=1, source_target_pairs={{0,1},{1,0},{2,3},{3,2},{4,5},{5,4},{6,7},{7,6},{8,9},{9,8},{10,11... | collective-permute-start | bytes 1179656 | tf_op jit(solution)/shard_map/ppermute | solution.py:484
  66.1 11.1 %attention.1.after_ref = bf16[32,32,128]{2,1,0:T(8,128)(2,1)S(1)} custom-call(s32[5]{0:T(128)S(1)} %stack.48.info_ref, bf16[32,80,128]{2,1,0:T(8,128)(2,1)S(1)} %all-to-all-done.own_ref, bf16[32,48,128]{2,1,0:T(8,128)(2,1)S(1)} %collective-permute-done.oth_ref), custom_call_target="tpu_custom_call" | custom-call | flops 1811939328 | bytes 3145728 | tf_op jit(solution)/shard_map/attention/pallas_call | solution.py:154
  78.0 1.9 merge.1
  80.0 21.6 %all_to_all.20.att_ref = bf16[32,32,128]{2,1,0:T(8,128)(2,1)} all-to-all(bf16[32,32,128]{2,1,0:T(8,128)(2,1)} %copy-done.1), channel_id=1, replica_groups=mesh['y'=8,'zlo'=2,'zhi'=4,'x'=4,'core'=2] {'zhi','x','core'}, dimensions={0} | all-to-all | bytes 524288 | tf_op jit(solution)/shard_map/all_to_all | solution.py:489
  102.5 2.6 %collective-permute-start.5 = (bf16[4,4,48,1536]{3,2,1,0:T(8,128)(2,1)}, bf16[4,4,48,1536]{3,2,1,0:T(8,128)(2,1)}, u32[]{:S(2)}, u32[]{:S(2)}) collective-permute-start(bf16[4,4,48,1536]{3,2,1,0:T(8,128)(2,1)} %bitcast.49), channel_id=1, source_target_pairs={{0,1},{1,0},{2,3},{3,2},{4,5},{5,4},{6,7},{7,6},{8,9},{9,8},{10,11... | collective-permute-start | bytes 7077896 | tf_op jit(solution)/shard_map/ppermute | solution.py:491
  105.7 4.3 %own_part.1.part_ref = f32[64,1536]{1,0:T(8,128)} custom-call(s32[5]{0:T(128)} %copy-done.2, bf16[32,32,128]{2,1,0:T(8,128)(2,1)} %all_to_all.20.att_ref, bf16[4,4,48,1536]{3,2,1,0:T(8,128)(2,1)} %bitcast.50), custom_call_target="tpu_custom_call" | custom-call | flops 17179869184 | bytes 3145728 | tf_op jit(solution)/shard_map/own_part/pallas_call | solution.py:254
  109.9 5.9 %project.1 = (f32[64,1536]{1,0:T(8,128)}, bf16[32,208,128]{2,1,0:T(8,128)(2,1)}) custom-call(s32[5]{0:T(128)} %copy-done.2, bf16[32,32,128]{2,1,0:T(8,128)(2,1)} %all_to_all.20.att_ref, f32[64,1536]{1,0:T(8,128)} %own_part.1.part_ref, bf16[4,4,48,1536]{3,2,1,0:T(8,128)(2,1)} %collective-permute-done.5.w_ref, bf16[64,1536]{1,0:T(8,128)(2,1)} %bitcast.40, ...), custom_call_target="tpu_custom_call" | custom-call | flops 301989888 | bytes 8388608 | tf_op jit(solution)/shard_map/project/pallas_call | solution.py:306
  115.9 8.9 %all-to-all-start.2 = ((bf16[32,208,128]{2,1,0:T(8,128)(2,1)}), bf16[32,208,128]{2,1,0:T(8,128)(2,1)S(1)}, u32[]{:S(2)}, u32[]{:S(2)}) async-start(bf16[32,208,128]{2,1,0:T(8,128)(2,1)} %get-tuple-element.19), calls=%async_computation.2 | async-start | bytes 3407872 | tf_op jit(solution)/shard_map/all_to_all | solution.py:496
  124.8 42.0 %all-gather.4.cloned.1.call-done.w_ref = bf16[16,96,1536]{2,1,0:T(8,128)(2,1)} async-done(((bf16[2,96,1536]{2,1,0:T(8,128)(2,1)}), bf16[16,96,1536]{2,1,0:T(8,128)(2,1)}) %all-gather.4.cloned.1.call-update) | async-done | bytes 4718608 | tf_op jit(solution)/shard_map/all_gather | solution.py:488
  168.7 9.5 %expert.1 = bf16[32,208,128]{2,1,0:T(8,128)(2,1)} custom-call(bf16[32,208,128]{2,1,0:T(8,128)(2,1)} %copy-done.3, bf16[16,96,1536]{2,1,0:T(8,128)(2,1)} %all-gather.4.cloned.1.call-done.w_ref), custom_call_target="tpu_custom_call" | custom-call | flops 2566914048 | bytes 9437184 | tf_op jit(solution)/shard_map/expert/pallas_call | solution.py:388
  178.3 9.9 %all-to-all-start.3 = ((bf16[32,208,128]{2,1,0:T(8,128)(2,1)}), bf16[32,208,128]{2,1,0:T(8,128)(2,1)S(1)}, u32[]{:S(2)}, u32[]{:S(2)}) async-start(bf16[32,208,128]{2,1,0:T(8,128)(2,1)} %expert.1), calls=%async_computation.3 | async-start | bytes 3407872 | tf_op jit(solution)/shard_map/all_to_all | solution.py:498
  190.8 2.2 select_bitcast_fusion
  195.4 35.5 %all-to-all-done.3.in_ref = bf16[32,208,128]{2,1,0:T(8,128)(2,1)S(1)} async-done(((bf16[32,208,128]{2,1,0:T(8,128)(2,1)}), bf16[32,208,128]{2,1,0:T(8,128)(2,1)S(1)}, u32[]{:S(2)}, u32[]{:S(2)}) %all-to-all-start.3) | async-done | bytes 1703968 | tf_op jit(solution)/shard_map/all_to_all | solution.py:498
  230.9 2.0 combine.1
  (43 shorter events, 10.0 us)
Async XLA Ops:
  9.1 50.6 %all-to-all-start = ((bf16[32,80,128]{2,1,0:T(8,128)(2,1)}), bf16[32,80,128]{2,1,0:T(8,128)(2,1)S(1)}, u32[]{:S(2)}, u32[]{:S(2)}) async-start(bf16[32,80,128]{2,1,0:T(8,128)(2,1)} %pack.1.after_ref), calls=%async_computation | async-start | bytes 1310720 | tf_op jit(solution)/shard_map/all_to_all | solution.py:478
  23.6 78.9 %all-gather.6.cloned.1.call-start = ((), (), s32[]{:S(2)}) async-start(), calls=%async_computation.5 | async-start | bytes 2949120 | tf_op jit(solution)/shard_map/all_gather | solution.py:483
  25.5 34.3 %collective-permute-start.4 = (bf16[96,1536]{1,0:T(8,128)(2,1)}, bf16[96,1536]{1,0:T(8,128)(2,1)S(1)}, u32[]{:S(2)}, u32[]{:S(2)}) collective-permute-start(bf16[96,1536]{1,0:T(8,128)(2,1)} %get-tuple-element.13.own_ref), channel_id=1, source_target_pairs={{0,32},{32,0},{1,33},{33,1},{2,34},{34,2},{3,35},{35,3},{4,36},{36... | collective-permute-start | bytes 884744 | tf_op jit(solution)/shard_map/ppermute | solution.py:474
  28.6 26.1 %collective-permute-start.1 = (bf16[48,1536]{1,0:T(8,128)(2,1)}, bf16[48,1536]{1,0:T(8,128)(2,1)S(1)}, u32[]{:S(2)}, u32[]{:S(2)}) collective-permute-start(bf16[48,1536]{1,0:T(8,128)(2,1)} %get-tuple-element.14), channel_id=1, source_target_pairs={{0,8},{8,16},{16,24},{24,0},{1,9},{9,17},{17,25},{25,1},{2,10},{10... | collective-permute-start | bytes 442376 | tf_op jit(solution)/shard_map/ppermute | solution.py:476
  32.8 21.9 %collective-permute-start.2 = (bf16[48,1536]{1,0:T(8,128)(2,1)}, bf16[48,1536]{1,0:T(8,128)(2,1)S(1)}, u32[]{:S(2)}, u32[]{:S(2)}) collective-permute-start(bf16[48,1536]{1,0:T(8,128)(2,1)} %get-tuple-element.14), channel_id=1, source_target_pairs={{0,24},{8,0},{16,8},{24,16},{1,25},{9,1},{17,9},{25,17},{2,26},{10... | collective-permute-start | bytes 442376 | tf_op jit(solution)/shard_map/ppermute | solution.py:476
  36.0 23.8 %collective-permute-start.3 = (bf16[48,1536]{1,0:T(8,128)(2,1)}, bf16[48,1536]{1,0:T(8,128)(2,1)S(1)}, u32[]{:S(2)}, u32[]{:S(2)}) collective-permute-start(bf16[48,1536]{1,0:T(8,128)(2,1)} %get-tuple-element.14), channel_id=1, source_target_pairs={{0,16},{8,24},{16,0},{24,8},{1,17},{9,25},{17,1},{25,9},{2,18},{10... | collective-permute-start | bytes 442376 | tf_op jit(solution)/shard_map/ppermute | solution.py:476
  59.8 17.5 %copy-start.7 = (bf16[96,1536]{1,0:T(8,128)(2,1)}, bf16[96,1536]{1,0:T(8,128)(2,1)S(1)}, u32[]{:S(2)}) copy-start(bf16[96,1536]{1,0:T(8,128)(2,1)S(1)} %collective-permute-done.4.oth_ref) | copy-start | bytes 884740
  61.8 105.0 %all-gather.4.cloned.1.call-start = ((), (), s32[]{:S(2)}) async-start(), calls=%async_computation.4 | async-start | bytes 5308416 | tf_op jit(solution)/shard_map/all_gather | solution.py:488
  61.9 4.3 %collective-permute-start = (bf16[32,48,128]{2,1,0:T(8,128)(2,1)S(1)}, bf16[32,48,128]{2,1,0:T(8,128)(2,1)S(1)}, u32[]{:S(2)}, u32[]{:S(2)}) collective-permute-start(bf16[32,48,128]{2,1,0:T(8,128)(2,1)S(1)} %slice.13), channel_id=1, source_target_pairs={{0,1},{1,0},{2,3},{3,2},{4,5},{5,4},{6,7},{7,6},{8,9},{9,8},{10,11... | collective-permute-start | bytes 1179656 | tf_op jit(solution)/shard_map/ppermute | solution.py:484
  65.6 11.7 %copy-start.2 = (s32[5]{0:T(128)}, s32[5]{0:T(128)S(1)}, u32[]{:S(2)}) copy-start(s32[5]{0:T(128)S(1)} %stack.48.info_ref) | copy-start | bytes 64
  77.3 0.7 copy-start.1
  78.0 27.0 %copy-start.5 = (f32[1536]{0:T(1024)S(1)}, f32[1536]{0:T(1024)}, u32[]{:S(2)}) copy-start(f32[1536]{0:T(1024)} %param.19) | copy-start | bytes 18436
  102.5 7.5 %collective-permute-start.5 = (bf16[4,4,48,1536]{3,2,1,0:T(8,128)(2,1)}, bf16[4,4,48,1536]{3,2,1,0:T(8,128)(2,1)}, u32[]{:S(2)}, u32[]{:S(2)}) collective-permute-start(bf16[4,4,48,1536]{3,2,1,0:T(8,128)(2,1)} %bitcast.49), channel_id=1, source_target_pairs={{0,1},{1,0},{2,3},{3,2},{4,5},{5,4},{6,7},{7,6},{8,9},{9,8},{10,11... | collective-permute-start | bytes 7077896 | tf_op jit(solution)/shard_map/ppermute | solution.py:491
  115.9 51.6 %all-to-all-start.2 = ((bf16[32,208,128]{2,1,0:T(8,128)(2,1)}), bf16[32,208,128]{2,1,0:T(8,128)(2,1)S(1)}, u32[]{:S(2)}, u32[]{:S(2)}) async-start(bf16[32,208,128]{2,1,0:T(8,128)(2,1)} %get-tuple-element.19), calls=%async_computation.2 | async-start | bytes 3407872 | tf_op jit(solution)/shard_map/all_to_all | solution.py:496
  167.5 1.3 copy-start.3
  178.2 10.0 %copy-start.4 = (s32[1,1,1,64,8]{3,4,2,1,0:T(8,128)S(1)}, s32[1,1,1,64,8]{3,4,2,1,0:T(8,128)}, u32[]{:S(2)}) copy-start(s32[1,1,1,64,8]{3,4,2,1,0:T(8,128)} %param.16) | copy-start | bytes 6148
  178.3 10.1 %copy-start.6 = (f32[1,1,1,64,8]{3,4,2,1,0:T(8,128)S(1)}, f32[1,1,1,64,8]{3,4,2,1,0:T(8,128)}, u32[]{:S(2)}) copy-start(f32[1,1,1,64,8]{3,4,2,1,0:T(8,128)} %param.17) | copy-start | bytes 6148
  178.3 52.7 %all-to-all-start.3 = ((bf16[32,208,128]{2,1,0:T(8,128)(2,1)}), bf16[32,208,128]{2,1,0:T(8,128)(2,1)S(1)}, u32[]{:S(2)}, u32[]{:S(2)}) async-start(bf16[32,208,128]{2,1,0:T(8,128)(2,1)} %expert.1), calls=%async_computation.3 | async-start | bytes 3407872 | tf_op jit(solution)/shard_map/all_to_all | solution.py:498
  190.8 40.2 %copy-start = (f32[64,1536]{1,0:T(8,128)S(1)}, f32[64,1536]{1,0:T(8,128)}, u32[]{:S(2)}) copy-start(f32[64,1536]{1,0:T(8,128)} %get-tuple-element.21.res_ref) | copy-start | bytes 1179652
Sparse Core Ops, SparseCore 0:
  61.9 40.5 all-gather.5
  104.5 62.1 all-gather.3

commit v4 on v2

--- a/solution.py
+++ b/solution.py
@@ -46,23 +46,22 @@
 
 
 def pack_kernel(q_ref, f_ref, c_ref, o_ref):
-    zeros = jnp.zeros((16, HD), BF)
-    for g in range(HKV):
+    for t in range(NT):
+        g = t // 8 * 2 + t % 2
+        x = t // 2 % 4
         cols = pl.ds(g * 128, 128)
-        for quarter in range(4):
-            t = g * 4 + quarter
-            rows = q_ref[quarter * 16 : quarter * 16 + 16, g * 192 : g * 192 + 192]
-            half = quarter % 2
-            o_ref[t, 0:16, :] = rows[:, :128]
-            o_ref[t, 16:32, :] = jnp.concatenate([rows[:, 128:], zeros], 1)
-            o_ref[t, 32:48, :] = c_ref[half * 16 : half * 16 + 16, cols]
-            o_ref[t, 48:80, :] = f_ref[half * 32 : half * 32 + 32, cols]
+        rows = q_ref[x * 16 : x * 16 + 16, g * 192 : g * 192 + 192]
+        o_ref[t, 0:16, :] = rows[:, :128]
+        o_ref[t, 16:48, :] = c_ref[:, cols]
+        o_ref[t, 48:112, :] = f_ref[:, cols]
+        last = rows[:, 128:].astype(F32)
+        o_ref[t, 112:120, :] = jnp.concatenate([last[0:8], last[8:16]], 1).astype(BF)
 
 
 def pack(queries, fresh, cache):
     return pl.pallas_call(
         pack_kernel,
-        out_shape=jax.ShapeDtypeStruct((NT, 80, 128), BF),
+        out_shape=jax.ShapeDtypeStruct((NT, 120, 128), BF),
         in_specs=[vmem()] * 3,
         out_specs=vmem(),
         interpret=INTERPRET,
@@ -70,41 +69,32 @@
     )(queries, fresh, cache)
 
 
-def attention_kernel(info_ref, own_ref, oth_ref, o_ref, kv, sc, bias_c, bias_d):
+def attention_kernel(info_ref, own_ref, keep_ref, send_ref, kv, sc, bias_c, bias_d):
     b = pl.program_id(0)
-    length, core, quarter = info_ref[0], info_ref[1], info_ref[2]
+    length, core, x = info_ref[0], info_ref[1], info_ref[2]
 
     @pl.when(b == 0)
     def _():
-        kv[0:512, :] = own_ref[:, 32:48, :].reshape(512, 128)
-        kv[512:1024, :] = oth_ref[:, 0:16, :].reshape(512, 128)
-        for j in range(4):
-            base = 1024 + 512 * j
-            kv[base : base + 256, :] = own_ref[8 * j : 8 * j + 8, 48:80, :].reshape(256, 128)
-            kv[base + 256 : base + 512, :] = oth_ref[8 * j : 8 * j + 8, 16:48, :].reshape(256, 128)
-        col = iota((8, 1024), 1)
-        half = jnp.where(col < 512, core, 1 - core)
-        inner = col % 512
-        place = (inner // 16) * 32 + half * 16 + inner % 16
-        bias_c[...] = jnp.where(place < length, 0.0, NEG)
+        kv[0:1024, :] = own_ref[:, 16:48, :].reshape(1024, 128)
+        kv[1024:3072, :] = own_ref[:, 48:112, :].reshape(2048, 128)
+        bias_c[...] = jnp.where(iota((8, 1024), 1) < length, 0.0, NEG)
         row = iota((128, 512), 0)
-        col = iota((128, 512), 1)
-        half = jnp.where(col < 256, core, 1 - core)
-        inner = col % 256
-        key_at = (inner // 32) * 64 + half * 32 + inner % 32
-        query_at = (row // 16) * 64 + quarter * 16 + row % 16
-        bias_d[...] = jnp.where(key_at <= query_at, 0.0, NEG)
+        query_at = (row // 16) * 64 + x * 16 + row % 16
+        bias_d[...] = jnp.where(iota((128, 512), 1) <= query_at, 0.0, NEG)
 
     first = own_ref[pl.ds(b * 8, 8), 0:16, :].reshape(128, 128).astype(F32) * 0.125
-    second = own_ref[pl.ds(b * 8, 8), 16:32, :].reshape(128, 128).astype(F32) * 0.125
+    last = own_ref[pl.ds(b * 8, 8), 112:120, :].astype(F32).reshape(64, 128) * 0.125
     low = iota((128, 128), 1) < HD
+    low2 = iota((64, 128), 1) < HD
+    third = jnp.concatenate(
+        [
+            jnp.where(low2, last, 0.0).reshape(8, 8, 128),
+            jnp.where(low2, pltpu.roll(last, HD, 1), 0.0).reshape(8, 8, 128),
+        ],
+        1,
+    ).reshape(128, 128)
     q = jnp.concatenate(
-        [
-            jnp.where(low, first, 0.0),
-            jnp.where(low, pltpu.roll(first, HD, 1), 0.0),
-            jnp.where(low, second, 0.0),
-        ],
-        0,
+        [jnp.where(low, first, 0.0), jnp.where(low, pltpu.roll(first, HD, 1), 0.0), third], 0
     ).astype(BF)
 
     def scores(k):
@@ -144,23 +134,23 @@
     total, acc = lax.fori_loop(0, 3 + b, mix, (zero, zero))
     out = acc / jnp.sum(total, 1, keepdims=True)
     a0, a1, a2 = out[0:128], out[128:256], out[256:384]
-    pair = jnp.where(low, pltpu.roll(a0, HD, 1), a1).astype(BF)
-    last = jnp.where(low, pltpu.roll(a2, HD, 1), 0.0).astype(BF)
-    o_ref[pl.ds(b * 8, 8), 0:16, :] = pair.reshape(8, 16, 128)
-    o_ref[pl.ds(b * 8, 8), 16:32, :] = last.reshape(8, 16, 128)
-
-
-def attention(info, own, other):
+    tiles = (jnp.where(low, pltpu.roll(a0, HD, 1), a1), jnp.where(low, pltpu.roll(a2, HD, 1), 0.0))
+    for n, tile in enumerate(tiles):
+        halves = tile.reshape(4, 2, 16, 128)
+        even, odd = halves[:, 0], halves[:, 1]
+        rows = slice(n * 16, n * 16 + 16)
+        keep_ref[pl.ds(b * 4, 4), rows, :] = jnp.where(core == 0, even, odd).astype(BF)
+        send_ref[pl.ds(b * 4, 4), rows, :] = jnp.where(core == 0, odd, even).astype(BF)
+
+
+def attention(info, own):
+    shape = jax.ShapeDtypeStruct((NT // 2, 32, 128), BF)
     return pl.pallas_call(
         attention_kernel,
-        out_shape=jax.ShapeDtypeStruct((NT, 32, 128), BF),
+        out_shape=(shape, shape),
         grid=(4,),
-        in_specs=[
-            pl.BlockSpec(memory_space=pltpu.SMEM),
-            vmem(),
-            vmem(),
-        ],
-        out_specs=vmem(),
+        in_specs=[pl.BlockSpec(memory_space=pltpu.SMEM), vmem()],
+        out_specs=(vmem(), vmem()),
         scratch_shapes=[
             pltpu.VMEM((3072, 128), BF),
             pltpu.VMEM((6, 384, 512), F32),
@@ -173,7 +163,32 @@
         ),
         interpret=INTERPRET,
         name="attention",
-    )(info, own, other)
+    )(info, own)
+
+
+def group_sums_kernel(info_ref, own_ref, oth_ref, w_ref, o_ref):
+    core = info_ref[1]
+    total = jnp.zeros((256, D), F32)
+    for src, side in ((own_ref, core), (oth_ref, 1 - core)):
+        pair = src[:, 0:16, :].reshape(256, 128)
+        last = src[:, 16:32, :].reshape(256, 128)[:, :HD]
+        at = pl.multiple_of(side * 192, 64)
+        total = total + dot(pair, w_ref[pl.ds(at, 128), :])
+        total = total + dot(last, w_ref[pl.ds(pl.multiple_of(at + 128, 64), HD), :])
+    o_ref[...] = total.astype(BF).reshape(NT // 2, 16, D)
+
+
+def group_sums(info, own, other, weight):
+    return pl.pallas_call(
+        group_sums_kernel,
+        out_shape=jax.ShapeDtypeStruct((NT // 2, 16, D), BF),
+        in_specs=[pl.BlockSpec(memory_space=pltpu.SMEM)] + [vmem()] * 3,
+        out_specs=vmem(),
+        compiler_params=params(24),
+        cost_estimate=pl.CostEstimate(flops=2 * 256 * 384 * D, bytes_accessed=2 << 20, transcendentals=0),
+        interpret=INTERPRET,
+        name="group_sums",
+    )(info, own, other, weight)
 
 
 def merge_kernel(info_ref, own_ref, oth_ref, after_ref, o_ref):
@@ -190,7 +205,7 @@
             pl.BlockSpec(memory_space=pltpu.SMEM),
             vmem(),
             vmem(),
-            pl.BlockSpec(memory_space=pltpu.HBM),
+            pl.BlockSpec(memory_space=pl.ANY),
         ],
         out_specs=vmem(),
         cost_estimate=pl.CostEstimate(flops=1 << 33, bytes_accessed=1 << 20, transcendentals=0),
@@ -199,16 +214,26 @@
     )(info, own, other, after)
 
 
-def project_kernel(info_ref, att_ref, wo_ref, wx_ref, hid_ref, gain_ref, ids_ref, res_ref, disp_ref, w, sems):
-    core = info_ref[1]
-    copies = []
-    for j in range(NT // 2):
-        for n, (src, side) in enumerate(((wo_ref, core), (wx_ref, 1 - core))):
-            at = pl.multiple_of((2 * j + side) * 48, 16)
-            copies.append(pltpu.make_async_copy(src.at[j], w.at[pl.ds(at, 48), :], sems.at[j, n]))
-    for copy in copies:
-        copy.start()
-
+def prepare_kernel(up_ref, down_ref, after_ref, o_ref):
+    o_ref[0:64, 0:1024] = up_ref[0:64, :]
+    o_ref[0:32, 1024:1536] = up_ref[64:96, 0:512]
+    o_ref[32:64, 1024:1536] = up_ref[64:96, 512:1024]
+    o_ref[64:96, :] = down_ref[...]
+
+
+def prepare(up, down, after):
+    return pl.pallas_call(
+        prepare_kernel,
+        out_shape=jax.ShapeDtypeStruct((96, D), BF),
+        in_specs=[vmem()] * 2 + [pl.BlockSpec(memory_space=pl.ANY)],
+        out_specs=vmem(),
+        cost_estimate=pl.CostEstimate(flops=1 << 33, bytes_accessed=1 << 20, transcendentals=0),
+        interpret=INTERPRET,
+        name="prepare",
+    )(up, down, after)
+
+
+def norm_dispatch_kernel(sum_ref, hid_ref, gain_ref, ids_ref, res_ref, disp_ref):
     experts = iota((NT, TOK), 0)
     named = jnp.zeros((NT, TOK), F32)
     for k in range(TOPK):
@@ -223,14 +248,8 @@
     late = jnp.where(ranks == float(SLOT), 1.0, 0.0)
 
     total = hid_ref[...].astype(F32)
-    for g in range(HKV):
-        for copy in copies[4 * g : 4 * g + 4]:
-            copy.wait()
-        pair = att_ref[g * 4 : g * 4 + 4, 0:16, :].reshape(TOK, 128)
-        last = att_ref[g * 4 : g * 4 + 4, 16:32, :].reshape(TOK, 128)
-        row = g * 192
-        term = dot(pair, w[row : row + 128, :]) + dot(last[:, :HD], w[row + 128 : row + 192, :])
-        total = total + term.astype(BF).astype(F32)
+    for z in range(4):
+        total = total + sum_ref[z * 4 : z * 4 + 4].reshape(TOK, D).astype(F32)
     res_ref[...] = total
     meansq = jnp.mean(total * total, 1, keepdims=True)
     normed = (total * lax.rsqrt(meansq + EPS) * gain_ref[...]).astype(BF)
@@ -244,27 +263,20 @@
     disp_ref[:, SLOT * CH : SROWS, :] = extra.astype(BF).reshape(NT, 16, 128)
 
 
-def project(info, att, own_weight, other_weight, hidden, gain, ids_t):
-    hbm = pl.BlockSpec(memory_space=pltpu.HBM)
-    return pl.pallas_call(
-        project_kernel,
+def norm_dispatch(sums, hidden, gain, ids_t):
+    return pl.pallas_call(
+        norm_dispatch_kernel,
         out_shape=(
             jax.ShapeDtypeStruct((TOK, D), F32),
             jax.ShapeDtypeStruct((NT, SROWS, 128), BF),
         ),
-        in_specs=[pl.BlockSpec(memory_space=pltpu.SMEM), vmem(), hbm, hbm, vmem(), vmem(), vmem()],
+        in_specs=[vmem()] * 4,
         out_specs=(vmem(), vmem()),
-        scratch_shapes=[
-            pltpu.VMEM((D, D), BF),
-            pltpu.SemaphoreType.DMA((NT // 2, 2)),
-        ],
-        compiler_params=params(61.7),
-        cost_estimate=pl.CostEstimate(
-            flops=2 * TOK * D * D, bytes_accessed=8 << 20, transcendentals=0
-        ),
-        interpret=INTERPRET,
-        name="project",
-    )(info, att, own_weight, other_weight, hidden, gain, ids_t)
+        compiler_params=params(32),
+        cost_estimate=pl.CostEstimate(flops=1 << 30, bytes_accessed=4 << 20, transcendentals=0),
+        interpret=INTERPRET,
+        name="norm_dispatch",
+    )(sums, hidden, gain, ids_t)
 
 
 def gather_extra(block):
@@ -334,7 +346,7 @@
             pltpu.VMEM((blocks * 32, D), BF),
             pltpu.SemaphoreType.DMA((blocks, 4)),
         ],
-        compiler_params=params(59.5),
+        compiler_params=params(58),
         cost_estimate=pl.CostEstimate(
             flops=2 * 544 * 1536 * 1536, bytes_accessed=9 << 20, transcendentals=544 * 512
         ),
@@ -399,45 +411,40 @@
     gate_up,
     down_weight,
 ):
-    zlo = lax.axis_index("zlo")
-    core = lax.axis_index("core")
-    quarter = lax.axis_index(TEN) % 4
+    zlo = lax.axis_index("zlo").astype(jnp.int32)
+    x = lax.axis_index("x").astype(jnp.int32)
+    core = lax.axis_index("core").astype(jnp.int32)
     length = cached_len[0]
+    info = jnp.stack([length, core, x, zlo])
     ids = expert_ids[0, 0, 0]
     gates = route_gates[0, 0, 0]
 
+    plane_weight = lax.all_gather(output_weight, ("x", "core"), axis=0, tiled=True)
     send = pack(rotated_queries[0, 0, 0], fresh_key_values[0, 0, 0], cached_key_values[0])
-    own_weight = lax.all_gather(output_weight, ("zhi", "x"), axis=0)
-    up, down, _ = lax.optimization_barrier((gate_up[0], down_weight[0], send))
-    packed = jnp.concatenate(
-        [jnp.concatenate([up[:64], jnp.concatenate([up[64:, :512], up[64:, 512:]], 0)], 1), down], 0
-    )
-
+    packed = prepare(gate_up[0], down_weight[0], send)
+    across = lax.ppermute(packed, "zlo", [(0, 1), (1, 0)])
     own = lax.all_to_all(send, TEN, split_axis=0, concat_axis=0, tiled=True)
-    other = lax.ppermute(own[:, 32:, :], "core", [(0, 1), (1, 0)])
-    packed, _ = lax.optimization_barrier((packed, own))
-    across = lax.ppermute(packed, "zlo", [(0, 1), (1, 0)])
-    info = jnp.stack([length, core.astype(jnp.int32), quarter.astype(jnp.int32), zlo.astype(jnp.int32)])
-    attended = attention(info, own, other)
-    both = merge(info, packed, across, attended)
+    own, across = lax.optimization_barrier((own, across))
+    kept, sent = attention(info, own)
+    swapped = lax.ppermute(sent, "core", [(0, 1), (1, 0)])
+    terms = group_sums(info, kept, swapped, plane_weight)
+    both = merge(info, packed, across, terms)
     weights = lax.all_gather(both, "y", axis=0, tiled=True)
-    swapping, _ = lax.optimization_barrier((own_weight, both))
-    other_weight = lax.ppermute(swapping, "core", [(0, 1), (1, 0)])
-    att = lax.all_to_all(attended, TEN, split_axis=0, concat_axis=0, tiled=True)
-    residual, outbound = project(
-        info, att, own_weight, other_weight, hidden_in[0, 0, 0], norm_gain[None], ids.T)
+    sums = lax.all_to_all(terms, ("zhi", "x"), split_axis=0, concat_axis=0, tiled=True)
+    residual, outbound = norm_dispatch(sums, hidden_in[0, 0, 0], norm_gain[None], ids.T)
     slots = lax.all_to_all(outbound, TEN, split_axis=0, concat_axis=0, tiled=True)
     computed = expert(slots, weights)
     returned = lax.all_to_all(computed, TEN, split_axis=0, concat_axis=0, tiled=True)
     hidden_out = combine(returned, residual, ids, gates)
 
-    mine = lax.dynamic_slice_in_dim(own[:, 32:, :], quarter * 32, 32, 2)
-    theirs = lax.dynamic_slice_in_dim(other, quarter * 32, 32, 2)
-    halves = jnp.where(
-        core == 0, jnp.stack([mine, theirs], 1), jnp.stack([theirs, mine], 1)
-    )
-    old_rows = halves[:, :, :16].reshape(NT * CROWS, 32)
-    new_rows = halves[:, :, 16:].reshape(NT * TOK, 32)
+    pairs = own[:, 16:112, :]
+    low_x = x % 2
+    mine = lax.dynamic_slice_in_dim(pairs, (low_x * 2 + core) * 32, 32, 2)
+    for_other = lax.dynamic_slice_in_dim(pairs, (low_x * 2 + 1 - core) * 32, 32, 2)
+    theirs = lax.ppermute(for_other, "core", [(0, 1), (1, 0)])
+    chosen = jnp.where(core == x // 2, mine, theirs)
+    old_rows = chosen[:, :CROWS].reshape(NT * CROWS, 32)
+    new_rows = chosen[:, CROWS:].reshape(NT * TOK, 32)
     total = NT * CROWS + NT * TOK
     base = jnp.concatenate([old_rows, jnp.zeros((NT * TOK, 32), BF)], 0)
     base = jnp.where((jnp.arange(total, dtype=jnp.int32) < length)[:, None], base, jnp.zeros_like(base))

time: 235 us -> 221 us (0.940)
  the two profiles are of different devices: /device:TPU:1 before, /device:TPU:36 now
where the time goes in v4:
time: 221 us; the launch traced here: 220 us
  waiting for transfers between devices  77.7 us (35%)
  blocking collectives  49.8 us (23%)
  starting transfers between devices  34.9 us (16%)
  Pallas kernels  31.2 us (14%)
  between operations  14.9 us (7%)
  local copies, waits for them, and re-layouts  9.78 us (4%)
    all_to_all x1, blocking collectives, shards(): lax.all_to_all(outbound, TEN, split_axis=0, concat_axis=0, tiled=True)  49.8 us
    all_to_all x1, waiting for transfers between devices, shards(): lax.all_to_all(computed, TEN, split_axis=0, concat_axis=0, tiled=True)  30.4 us
    ppermute x1, waiting for transfers between devices, shards(): across = lax.ppermute(packed, 'zlo', [(0, 1), (1, 0)])  23.3 us
    all_to_all x1, waiting for transfers between devices, shards(): lax.all_to_all(terms, ('zhi', 'x'), split_axis=0, concat_axis=0, tiled=True)  20.8 us
    all_to_all x1, starting transfers between devices, shards(): own = lax.all_to_all(send, TEN, split_axis=0, concat_axis=0, tiled=True)  13.4 us
    pallas_call x1, Pallas kernels, attention(): pl.pallas_call(attention_kernel, out_shape=(shape, shape), grid=(4,), in_...  11.1 us
    pallas_call x1, Pallas kernels, expert(): pl.pallas_call(expert_kernel, out_shape=jax.ShapeDtypeStruct((NT, SROWS,...  9.52 us
    all_to_all x1, starting transfers between devices, shards(): lax.all_to_all(terms, ('zhi', 'x'), split_axis=0, concat_axis=0, tiled=True)  8.94 us
  transfers between devices with their start and end apart: 8, of which 5 were waited for; matrix products, arithmetic and copies ran while one was open for 4% of the time, Pallas kernels for 6%

profile of v4, /device:TPU:36, one launch (start us, length us, event | category | flops | bytes accessed | tf_op | source)
XLA Modules:
  0.0 219.9 jit_solution(827008506208603988)
XLA Ops:
  7.2 2.1 pack.1.after_ref
  9.3 13.4 %all-to-all-start = ((bf16[32,120,128]{2,1,0:T(8,128)(2,1)}), bf16[32,120,128]{2,1,0:T(8,128)(2,1)S(1)}, u32[]{:S(2)}, u32[]{:S(2)}) async-start(bf16[32,120,128]{2,1,0:T(8,128)(2,1)} %pack.1.after_ref), calls=%async_computation | async-start | bytes 1966080 | tf_op jit(solution)/shard_map/all_to_all | solution.py:426
  23.5 1.7 prepare.1.own_ref
  25.3 3.4 %collective-permute-start = (bf16[96,1536]{1,0:T(8,128)(2,1)}, bf16[96,1536]{1,0:T(8,128)(2,1)S(1)}, u32[]{:S(2)}, u32[]{:S(2)}) collective-permute-start(bf16[96,1536]{1,0:T(8,128)(2,1)} %prepare.1.own_ref), channel_id=1, source_target_pairs={{0,32},{32,0},{1,33},{33,1},{2,34},{34,2},{3,35},{35,3},{4,36},{36... | collective-permute-start | bytes 884744 | tf_op jit(solution)/shard_map/ppermute | solution.py:425
  29.4 23.3 %collective-permute-done.oth_ref = bf16[96,1536]{1,0:T(8,128)(2,1)S(1)} collective-permute-done((bf16[96,1536]{1,0:T(8,128)(2,1)}, bf16[96,1536]{1,0:T(8,128)(2,1)S(1)}, u32[]{:S(2)}, u32[]{:S(2)}) %collective-permute-start) | collective-permute-done | bytes 294944 | tf_op jit(solution)/shard_map/ppermute | solution.py:425
  52.7 11.1 %attention.1 = (bf16[16,32,128]{2,1,0:T(8,128)(2,1)S(1)}, bf16[16,32,128]{2,1,0:T(8,128)(2,1)S(1)}) custom-call(s32[4]{0:T(128)S(1)} %pad_add_fusion.info_ref, bf16[32,120,128]{2,1,0:T(8,128)(2,1)S(1)} %all-to-all-done.own_ref), custom_call_target="tpu_custom_call" | custom-call | flops 1811939328 | bytes 3145728 | tf_op jit(solution)/shard_map/attention/pallas_call | solution.py:148
  63.8 1.9 collective-permute-start.1
  65.7 1.3 collective-permute-done.1.oth_ref
  67.1 1.3 copy-done.1
  68.3 1.5 group_sums.1.after_ref
  70.7 1.9 merge.1
  72.7 8.9 %all-to-all-start.1 = ((bf16[16,16,1536]{2,1,0:T(8,128)(2,1)}), bf16[16,16,1536]{2,1,0:T(8,128)(2,1)S(1)}, u32[]{:S(2)}, u32[]{:S(2)}) async-start(bf16[16,16,1536]{2,1,0:T(8,128)(2,1)} %copy-done), calls=%async_computation.1 | async-start | bytes 1572864 | tf_op jit(solution)/shard_map/all_to_all | solution.py:433
  81.7 20.8 %all-to-all-done.1.sum_ref = bf16[16,16,1536]{2,1,0:T(8,128)(2,1)S(1)} async-done(((bf16[16,16,1536]{2,1,0:T(8,128)(2,1)}), bf16[16,16,1536]{2,1,0:T(8,128)(2,1)S(1)}, u32[]{:S(2)}, u32[]{:S(2)}) %all-to-all-start.1) | async-done | bytes 786464 | tf_op jit(solution)/shard_map/all_to_all | solution.py:433
  102.4 1.3 norm_dispatch.1
  103.7 49.8 %all_to_all.20.in_ref = bf16[32,208,128]{2,1,0:T(8,128)(2,1)} all-to-all(bf16[32,208,128]{2,1,0:T(8,128)(2,1)S(1)} %get-tuple-element.11), channel_id=1, replica_groups=mesh['y'=8,'zlo'=2,'zhi'=4,'x'=4,'core'=2] {'zhi','x','core'}, dimensions={0} | all-to-all | bytes 3407872 | tf_op jit(solution)/shard_map/all_to_all | solution.py:435
  153.5 9.5 %expert.1 = bf16[32,208,128]{2,1,0:T(8,128)(2,1)} custom-call(bf16[32,208,128]{2,1,0:T(8,128)(2,1)} %all_to_all.20.in_ref, bf16[16,96,1536]{2,1,0:T(8,128)(2,1)} %all-gather.5.cloned.1.call-done.w_ref), custom_call_target="tpu_custom_call" | custom-call | flops 2566914048 | bytes 9437184 | tf_op jit(solution)/shard_map/expert/pallas_call | solution.py:338
  163.1 5.0 %all-to-all-start.3 = ((bf16[32,208,128]{2,1,0:T(8,128)(2,1)}), bf16[32,208,128]{2,1,0:T(8,128)(2,1)S(1)}, u32[]{:S(2)}, u32[]{:S(2)}) async-start(bf16[32,208,128]{2,1,0:T(8,128)(2,1)} %expert.1), calls=%async_computation.3 | async-start | bytes 3407872 | tf_op jit(solution)/shard_map/all_to_all | solution.py:437
  170.2 1.5 copy.21
  171.7 2.2 %collective-permute-start.2 = (bf16[32,96,32]{1,2,0:T(8,128)(2,1)S(1)}, bf16[32,96,32]{1,2,0:T(8,128)(2,1)}, u32[]{:S(2)}, u32[]{:S(2)}) collective-permute-start(bf16[32,96,32]{1,2,0:T(8,128)(2,1)S(1)} %copy.21), channel_id=1, source_target_pairs={{0,1},{1,0},{2,3},{3,2},{4,5},{5,4},{6,7},{7,6},{8,9},{9,8},{10,11... | collective-permute-start | bytes 589832 | tf_op jit(solution)/shard_map/ppermute | solution.py:444
  175.3 2.2 copy.22
  177.4 1.5 dynamic-slice_select_fusion
  179.4 1.2 dynamic_update_slice.4
  180.6 30.4 %all-to-all-done.3.in_ref = bf16[32,208,128]{2,1,0:T(8,128)(2,1)S(1)} async-done(((bf16[32,208,128]{2,1,0:T(8,128)(2,1)}), bf16[32,208,128]{2,1,0:T(8,128)(2,1)S(1)}, u32[]{:S(2)}, u32[]{:S(2)}) %all-to-all-start.3) | async-done | bytes 1703968 | tf_op jit(solution)/shard_map/all_to_all | solution.py:437
  211.0 2.0 combine.1
  (41 shorter events, 5.6 us)
Async XLA Ops:
  9.3 43.4 %all-to-all-start = ((bf16[32,120,128]{2,1,0:T(8,128)(2,1)}), bf16[32,120,128]{2,1,0:T(8,128)(2,1)S(1)}, u32[]{:S(2)}, u32[]{:S(2)}) async-start(bf16[32,120,128]{2,1,0:T(8,128)(2,1)} %pack.1.after_ref), calls=%async_computation | async-start | bytes 1966080 | tf_op jit(solution)/shard_map/all_to_all | solution.py:426
  22.7 44.3 %all-gather.3.cloned.1.call-start = ((), (), s32[]{:S(2)}) async-start(), calls=%async_computation.4 | async-start | bytes 1327104 | tf_op jit(solution)/shard_map/all_gather | solution.py:422
  23.5 130.1 %all-gather.5.cloned.1.call-start = ((), (), s32[]{:S(2)}) async-start(), calls=%async_computation.5 | async-start | bytes 5308416 | tf_op jit(solution)/shard_map/all_gather | solution.py:432
  25.3 27.4 %collective-permute-start = (bf16[96,1536]{1,0:T(8,128)(2,1)}, bf16[96,1536]{1,0:T(8,128)(2,1)S(1)}, u32[]{:S(2)}, u32[]{:S(2)}) collective-permute-start(bf16[96,1536]{1,0:T(8,128)(2,1)} %prepare.1.own_ref), channel_id=1, source_target_pairs={{0,32},{32,0},{1,33},{33,1},{2,34},{34,2},{3,35},{35,3},{4,36},{36... | collective-permute-start | bytes 884744 | tf_op jit(solution)/shard_map/ppermute | solution.py:425
  29.4 37.7 %copy-start.3 = (s32[4]{0:T(128)}, s32[4]{0:T(128)S(1)}, u32[]{:S(2)}) copy-start(s32[4]{0:T(128)S(1)} %pad_add_fusion.info_ref) | copy-start | bytes 52
  52.7 11.1 %copy-start.10 = (bf16[96,1536]{1,0:T(8,128)(2,1)}, bf16[96,1536]{1,0:T(8,128)(2,1)S(1)}, u32[]{:S(2)}) copy-start(bf16[96,1536]{1,0:T(8,128)(2,1)S(1)} %collective-permute-done.oth_ref) | copy-start | bytes 884740
  63.8 3.2 %collective-permute-start.1 = (bf16[16,32,128]{2,1,0:T(8,128)(2,1)S(1)}, bf16[16,32,128]{2,1,0:T(8,128)(2,1)S(1)}, u32[]{:S(2)}, u32[]{:S(2)}) collective-permute-start(bf16[16,32,128]{2,1,0:T(8,128)(2,1)S(1)} %get-tuple-element.10), channel_id=1, source_target_pairs={{0,1},{1,0},{2,3},{3,2},{4,5},{5,4},{6,7},{7,6},{8,9},{9,8},{10,11... | collective-permute-start | bytes 393224 | tf_op jit(solution)/shard_map/ppermute | solution.py:429
  67.1 1.3 copy-start.1
  69.8 0.9 copy-start
  72.7 9.0 %copy-start.8 = (f32[1536]{0:T(1024)S(1)}, f32[1536]{0:T(1024)}, u32[]{:S(2)}) copy-start(f32[1536]{0:T(1024)} %param.19) | copy-start | bytes 18436
  72.7 29.8 %copy-start.2 = (s32[1,1,1,64,8]{3,4,2,1,0:T(8,128)S(1)}, s32[1,1,1,64,8]{3,4,2,1,0:T(8,128)}, u32[]{:S(2)}) copy-start(s32[1,1,1,64,8]{3,4,2,1,0:T(8,128)} %param.16) | copy-start | bytes 6148
  72.7 29.8 %copy-start.4 = (bf16[1,1,1,64,1536]{4,3,2,1,0:T(8,128)(2,1)S(1)}, bf16[1,1,1,64,1536]{4,3,2,1,0:T(8,128)(2,1)}, u32[]{:S(2)}) copy-start(bf16[1,1,1,64,1536]{4,3,2,1,0:T(8,128)(2,1)} %param.11) | copy-start | bytes 589828
  72.7 29.7 %all-to-all-start.1 = ((bf16[16,16,1536]{2,1,0:T(8,128)(2,1)}), bf16[16,16,1536]{2,1,0:T(8,128)(2,1)S(1)}, u32[]{:S(2)}, u32[]{:S(2)}) async-start(bf16[16,16,1536]{2,1,0:T(8,128)(2,1)} %copy-done), calls=%async_computation.1 | async-start | bytes 1572864 | tf_op jit(solution)/shard_map/all_to_all | solution.py:433
  163.1 48.0 %all-to-all-start.3 = ((bf16[32,208,128]{2,1,0:T(8,128)(2,1)}), bf16[32,208,128]{2,1,0:T(8,128)(2,1)S(1)}, u32[]{:S(2)}, u32[]{:S(2)}) async-start(bf16[32,208,128]{2,1,0:T(8,128)(2,1)} %expert.1), calls=%async_computation.3 | async-start | bytes 3407872 | tf_op jit(solution)/shard_map/all_to_all | solution.py:437
  168.1 0.9 copy-start.5
  169.0 5.0 %copy-start.9 = (f32[1,1,1,64,8]{3,4,2,1,0:T(8,128)S(1)}, f32[1,1,1,64,8]{3,4,2,1,0:T(8,128)}, u32[]{:S(2)}) copy-start(f32[1,1,1,64,8]{3,4,2,1,0:T(8,128)} %param.17) | copy-start | bytes 6148
  170.2 7.2 %copy-start.6 = (bf16[32,96,128]{2,1,0:T(8,128)(2,1)S(1)}, bf16[32,96,128]{2,1,0:T(8,128)(2,1)}, u32[]{:S(2)}) copy-start(bf16[32,96,128]{2,1,0:T(8,128)(2,1)} %copy-done.5) | copy-start | bytes 2359300
  171.7 3.6 %collective-permute-start.2 = (bf16[32,96,32]{1,2,0:T(8,128)(2,1)S(1)}, bf16[32,96,32]{1,2,0:T(8,128)(2,1)}, u32[]{:S(2)}, u32[]{:S(2)}) collective-permute-start(bf16[32,96,32]{1,2,0:T(8,128)(2,1)S(1)} %copy.21), channel_id=1, source_target_pairs={{0,1},{1,0},{2,3},{3,2},{4,5},{5,4},{6,7},{7,6},{8,9},{9,8},{10,11... | collective-permute-start | bytes 589832 | tf_op jit(solution)/shard_map/ppermute | solution.py:444
  180.6 32.5 %copy-start.7 = (bf16[1,3072,32]{1,2,0:T(8,128)(2,1)}, bf16[1,3072,32]{1,2,0:T(8,128)(2,1)S(1)}, u32[]{:S(2)}) copy-start(bf16[1,3072,32]{1,2,0:T(8,128)(2,1)S(1)} %dynamic_update_slice.4) | copy-start | bytes 589828
Sparse Core Ops, SparseCore 0:
  25.7 28.6 all-gather.2
  72.8 59.5 all-gather.4

commit v5 on v4

--- a/solution.py
+++ b/solution.py
@@ -46,22 +46,19 @@
 
 
 def pack_kernel(q_ref, f_ref, c_ref, o_ref):
-    for t in range(NT):
-        g = t // 8 * 2 + t % 2
-        x = t // 2 % 4
+    for g in range(HKV):
         cols = pl.ds(g * 128, 128)
-        rows = q_ref[x * 16 : x * 16 + 16, g * 192 : g * 192 + 192]
-        o_ref[t, 0:16, :] = rows[:, :128]
-        o_ref[t, 16:48, :] = c_ref[:, cols]
-        o_ref[t, 48:112, :] = f_ref[:, cols]
-        last = rows[:, 128:].astype(F32)
-        o_ref[t, 112:120, :] = jnp.concatenate([last[0:8], last[8:16]], 1).astype(BF)
+        rows = q_ref[:, g * 192 : g * 192 + 192]
+        o_ref[g, 0:64, :] = rows[:, :128]
+        o_ref[g, 64:96, :] = jnp.concatenate([rows[0:32, 128:], rows[32:64, 128:]], 1)
+        o_ref[g, 96:128, :] = c_ref[:, cols]
+        o_ref[g, 128:192, :] = f_ref[:, cols]
 
 
 def pack(queries, fresh, cache):
     return pl.pallas_call(
         pack_kernel,
-        out_shape=jax.ShapeDtypeStruct((NT, 120, 128), BF),
+        out_shape=jax.ShapeDtypeStruct((HKV, 192, 128), BF),
         in_specs=[vmem()] * 3,
         out_specs=vmem(),
         interpret=INTERPRET,
@@ -69,32 +66,32 @@
     )(queries, fresh, cache)
 
 
-def attention_kernel(info_ref, own_ref, keep_ref, send_ref, kv, sc, bias_c, bias_d):
+def attention_kernel(info_ref, own_ref, pair_ref, keep_ref, send_ref, kv, sc, bias_c, bias_d):
     b = pl.program_id(0)
     length, core, x = info_ref[0], info_ref[1], info_ref[2]
 
     @pl.when(b == 0)
     def _():
-        kv[0:1024, :] = own_ref[:, 16:48, :].reshape(1024, 128)
-        kv[1024:3072, :] = own_ref[:, 48:112, :].reshape(2048, 128)
+        for t in range(NT):
+            src = pair_ref.at[t // 2 % 4, t // 8 * 2 + t % 2]
+            kv[t * 32 : t * 32 + 32, :] = src[0:32, :]
+            kv[1024 + t * 64 : 1088 + t * 64, :] = src[32:96, :]
         bias_c[...] = jnp.where(iota((8, 1024), 1) < length, 0.0, NEG)
-        row = iota((128, 512), 0)
-        query_at = (row // 16) * 64 + x * 16 + row % 16
+        query_at = x * 128 + iota((128, 512), 0)
         bias_d[...] = jnp.where(iota((128, 512), 1) <= query_at, 0.0, NEG)
 
-    first = own_ref[pl.ds(b * 8, 8), 0:16, :].reshape(128, 128).astype(F32) * 0.125
-    last = own_ref[pl.ds(b * 8, 8), 112:120, :].astype(F32).reshape(64, 128) * 0.125
+    first = own_ref[pl.ds(b * 2, 2), 0:64, :].reshape(128, 128).astype(F32) * 0.125
+    last = own_ref[pl.ds(b * 2, 2), 64:96, :].reshape(64, 128).astype(F32) * 0.125
     low = iota((128, 128), 1) < HD
-    low2 = iota((64, 128), 1) < HD
-    third = jnp.concatenate(
+    turned = pltpu.roll(last, HD, 1)
+    third = jnp.concatenate([last[0:32], turned[0:32], last[32:64], turned[32:64]], 0)
+    q = jnp.concatenate(
         [
-            jnp.where(low2, last, 0.0).reshape(8, 8, 128),
-            jnp.where(low2, pltpu.roll(last, HD, 1), 0.0).reshape(8, 8, 128),
+            jnp.where(low, first, 0.0),
+            jnp.where(low, pltpu.roll(first, HD, 1), 0.0),
+            jnp.where(low, third, 0.0),
         ],
-        1,
-    ).reshape(128, 128)
-    q = jnp.concatenate(
-        [jnp.where(low, first, 0.0), jnp.where(low, pltpu.roll(first, HD, 1), 0.0), third], 0
+        0,
     ).astype(BF)
 
     def scores(k):
@@ -136,20 +133,19 @@
     a0, a1, a2 = out[0:128], out[128:256], out[256:384]
     tiles = (jnp.where(low, pltpu.roll(a0, HD, 1), a1), jnp.where(low, pltpu.roll(a2, HD, 1), 0.0))
     for n, tile in enumerate(tiles):
-        halves = tile.reshape(4, 2, 16, 128)
-        even, odd = halves[:, 0], halves[:, 1]
-        rows = slice(n * 16, n * 16 + 16)
-        keep_ref[pl.ds(b * 4, 4), rows, :] = jnp.where(core == 0, even, odd).astype(BF)
-        send_ref[pl.ds(b * 4, 4), rows, :] = jnp.where(core == 0, odd, even).astype(BF)
-
-
-def attention(info, own):
-    shape = jax.ShapeDtypeStruct((NT // 2, 32, 128), BF)
+        even, odd = tile[0:64], tile[64:128]
+        rows = slice(n * 64, n * 64 + 64)
+        keep_ref[b, rows, :] = jnp.where(core == 0, even, odd).astype(BF)
+        send_ref[b, rows, :] = jnp.where(core == 0, odd, even).astype(BF)
+
+
+def attention(info, own, pairs):
+    shape = jax.ShapeDtypeStruct((4, 128, 128), BF)
     return pl.pallas_call(
         attention_kernel,
         out_shape=(shape, shape),
         grid=(4,),
-        in_specs=[pl.BlockSpec(memory_space=pltpu.SMEM), vmem()],
+        in_specs=[pl.BlockSpec(memory_space=pltpu.SMEM), vmem(), vmem()],
         out_specs=(vmem(), vmem()),
         scratch_shapes=[
             pltpu.VMEM((3072, 128), BF),
@@ -163,55 +159,32 @@
         ),
         interpret=INTERPRET,
         name="attention",
-    )(info, own)
+    )(info, own, pairs)
 
 
 def group_sums_kernel(info_ref, own_ref, oth_ref, w_ref, o_ref):
     core = info_ref[1]
     total = jnp.zeros((256, D), F32)
     for src, side in ((own_ref, core), (oth_ref, 1 - core)):
-        pair = src[:, 0:16, :].reshape(256, 128)
-        last = src[:, 16:32, :].reshape(256, 128)[:, :HD]
+        pair = src[:, 0:64, :].reshape(256, 128)
+        last = src[:, 64:128, :].reshape(256, 128)[:, :HD]
         at = pl.multiple_of(side * 192, 64)
         total = total + dot(pair, w_ref[pl.ds(at, 128), :])
         total = total + dot(last, w_ref[pl.ds(pl.multiple_of(at + 128, 64), HD), :])
-    o_ref[...] = total.astype(BF).reshape(NT // 2, 16, D)
+    o_ref[...] = total.astype(BF).reshape(4, TOK, D)
 
 
 def group_sums(info, own, other, weight):
     return pl.pallas_call(
         group_sums_kernel,
-        out_shape=jax.ShapeDtypeStruct((NT // 2, 16, D), BF),
+        out_shape=jax.ShapeDtypeStruct((4, TOK, D), BF),
         in_specs=[pl.BlockSpec(memory_space=pltpu.SMEM)] + [vmem()] * 3,
         out_specs=vmem(),
-        compiler_params=params(24),
+        compiler_params=params(62.5),
         cost_estimate=pl.CostEstimate(flops=2 * 256 * 384 * D, bytes_accessed=2 << 20, transcendentals=0),
         interpret=INTERPRET,
         name="group_sums",
     )(info, own, other, weight)
-
-
-def merge_kernel(info_ref, own_ref, oth_ref, after_ref, o_ref):
-    zlo = info_ref[3]
-    o_ref[zlo] = own_ref[...]
-    o_ref[1 - zlo] = oth_ref[...]
-
-
-def merge(info, own, other, after):
-    return pl.pallas_call(
-        merge_kernel,
-        out_shape=jax.ShapeDtypeStruct((2,) + own.shape, BF),
-        in_specs=[
-            pl.BlockSpec(memory_space=pltpu.SMEM),
-            vmem(),
-            vmem(),
-            pl.BlockSpec(memory_space=pl.ANY),
-        ],
-        out_specs=vmem(),
-        cost_estimate=pl.CostEstimate(flops=1 << 33, bytes_accessed=1 << 20, transcendentals=0),
-        interpret=INTERPRET,
-        name="merge",
-    )(info, own, other, after)
 
 
 def prepare_kernel(up_ref, down_ref, after_ref, o_ref):
@@ -249,7 +222,7 @@
 
     total = hid_ref[...].astype(F32)
     for z in range(4):
-        total = total + sum_ref[z * 4 : z * 4 + 4].reshape(TOK, D).astype(F32)
+        total = total + sum_ref[z].astype(F32)
     res_ref[...] = total
     meansq = jnp.mean(total * total, 1, keepdims=True)
     normed = (total * lax.rsqrt(meansq + EPS) * gain_ref[...]).astype(BF)
@@ -297,15 +270,18 @@
     return out.astype(BF)
 
 
-def expert_kernel(in_ref, w_ref, o_ref, x, w1, w2, sems):
-    blocks = w_ref.shape[0]
+def expert_kernel(info_ref, in_ref, wo_ref, wx_ref, o_ref, x, w1, w2, sems):
+    zlo = info_ref[3]
     copies = []
-    for d in range(blocks):
+    for d in range(2 * wo_ref.shape[0]):
+        w_ref, block = (wo_ref, zlo) if d % 2 == 0 else (wx_ref, 1 - zlo)
+        block = block + d // 2 * 2
+        top = pl.multiple_of(block * 96, 32)
         pieces = (
-            (w_ref.at[d, 0:64, 0:1024], w1.at[d * 96 : d * 96 + 64, :]),
-            (w_ref.at[d, 0:32, 1024:1536], w1.at[d * 96 + 64 : d * 96 + 96, 0:512]),
-            (w_ref.at[d, 32:64, 1024:1536], w1.at[d * 96 + 64 : d * 96 + 96, 512:1024]),
-            (w_ref.at[d, 64:96, :], w2.at[d * 32 : d * 32 + 32, :]),
+            (w_ref.at[d // 2, 0:64, 0:1024], w1.at[pl.ds(top, 64), :]),
+            (w_ref.at[d // 2, 0:32, 1024:1536], w1.at[pl.ds(top + 64, 32), 0:512]),
+            (w_ref.at[d // 2, 32:64, 1024:1536], w1.at[pl.ds(top + 64, 32), 512:1024]),
+            (w_ref.at[d // 2, 64:96, :], w2.at[pl.ds(pl.multiple_of(block * 32, 32), 32), :]),
         )
         for n, (src, dst) in enumerate(pieces):
             copies.append(pltpu.make_async_copy(src, dst, sems.at[d, n]))
@@ -333,12 +309,13 @@
     o_ref[:, SLOT * CH : SROWS, :] = spread_extra(out[512:544, :]).reshape(NT, 16, 128)
 
 
-def expert(slots, weights):
-    blocks = weights.shape[0]
+def expert(info, slots, own_weights, other_weights):
+    blocks = 2 * own_weights.shape[0]
     return pl.pallas_call(
         expert_kernel,
         out_shape=jax.ShapeDtypeStruct((NT, SROWS, 128), BF),
-        in_specs=[vmem(), pl.BlockSpec(memory_space=pltpu.HBM)],
+        in_specs=[pl.BlockSpec(memory_space=pltpu.SMEM), vmem()]
+        + [pl.BlockSpec(memory_space=pltpu.HBM)] * 2,
         out_specs=vmem(),
         scratch_shapes=[
             pltpu.VMEM((544, D), BF),
@@ -352,7 +329,7 @@
         ),
         interpret=INTERPRET,
         name="expert",
-    )(slots, weights)
+    )(info, slots, own_weights, other_weights)
 
 
 def combine_kernel(in_ref, res_ref, ids_ref, gate_ref, o_ref):
@@ -421,28 +398,30 @@
 
     plane_weight = lax.all_gather(output_weight, ("x", "core"), axis=0, tiled=True)
     send = pack(rotated_queries[0, 0, 0], fresh_key_values[0, 0, 0], cached_key_values[0])
-    packed = prepare(gate_up[0], down_weight[0], send)
+    own = lax.all_to_all(send, ("zhi", "core"), split_axis=0, concat_axis=0, tiled=True)
+    packed = prepare(gate_up[0], down_weight[0], own)
+    own_weights = lax.all_gather(packed, "y", axis=0)
     across = lax.ppermute(packed, "zlo", [(0, 1), (1, 0)])
-    own = lax.all_to_all(send, TEN, split_axis=0, concat_axis=0, tiled=True)
-    own, across = lax.optimization_barrier((own, across))
-    kept, sent = attention(info, own)
+    spread = jnp.broadcast_to(own[None, :, 96:], (4, HKV, 96, 128))
+    pairs = lax.all_to_all(spread, "x", split_axis=0, concat_axis=0, tiled=True)
+    kept, sent = attention(info, own, pairs)
+    across, sent = lax.optimization_barrier((across, sent))
+    other_weights = lax.all_gather(across, "y", axis=0)
     swapped = lax.ppermute(sent, "core", [(0, 1), (1, 0)])
     terms = group_sums(info, kept, swapped, plane_weight)
-    both = merge(info, packed, across, terms)
-    weights = lax.all_gather(both, "y", axis=0, tiled=True)
-    sums = lax.all_to_all(terms, ("zhi", "x"), split_axis=0, concat_axis=0, tiled=True)
+    sums = lax.all_to_all(terms, "zhi", split_axis=0, concat_axis=0, tiled=True)
     residual, outbound = norm_dispatch(sums, hidden_in[0, 0, 0], norm_gain[None], ids.T)
     slots = lax.all_to_all(outbound, TEN, split_axis=0, concat_axis=0, tiled=True)
-    computed = expert(slots, weights)
+    computed = expert(info, slots, own_weights, other_weights)
     returned = lax.all_to_all(computed, TEN, split_axis=0, concat_axis=0, tiled=True)
     hidden_out = combine(returned, residual, ids, gates)
 
-    pairs = own[:, 16:112, :]
     low_x = x % 2
-    mine = lax.dynamic_slice_in_dim(pairs, (low_x * 2 + core) * 32, 32, 2)
-    for_other = lax.dynamic_slice_in_dim(pairs, (low_x * 2 + 1 - core) * 32, 32, 2)
+    mine = lax.dynamic_slice_in_dim(pairs, (low_x * 2 + core) * 32, 32, 3)
+    for_other = lax.dynamic_slice_in_dim(pairs, (low_x * 2 + 1 - core) * 32, 32, 3)
     theirs = lax.ppermute(for_other, "core", [(0, 1), (1, 0)])
-    chosen = jnp.where(core == x // 2, mine, theirs)
+    chosen = jnp.where(core == x // 2, mine, theirs).reshape(4, 4, 2, 96, 32)
+    chosen = jnp.transpose(chosen, (1, 0, 2, 3, 4)).reshape(NT, 96, 32)
     old_rows = chosen[:, :CROWS].reshape(NT * CROWS, 32)
     new_rows = chosen[:, CROWS:].reshape(NT * TOK, 32)
     total = NT * CROWS + NT * TOK

time: 221 us -> 219 us (level)
  the two profiles are of different devices: /device:TPU:36 before, /device:TPU:1 now
where the time goes in v5:
time: 219 us; the launch traced here: 218 us
  waiting for transfers between devices  103 us (47%)
  Pallas kernels  32.2 us (15%)
  starting transfers between devices  28 us (13%)
  blocking collectives  26.9 us (12%)
  between operations  14.6 us (7%)
  local copies, waits for them, and re-layouts  11.1 us (5%)
  other arithmetic  2.49 us (1%)
    all_to_all x1, waiting for transfers between devices, shards(): lax.all_to_all(computed, TEN, split_axis=0, concat_axis=0, tiled=True)  29.1 us
    all_to_all x1, blocking collectives, shards(): lax.all_to_all(send, ('zhi', 'core'), split_axis=0, concat_axis=0, tiled=...  26.9 us
    all_gather x1, waiting for transfers between devices, shards(): other_weights = lax.all_gather(across, 'y', axis=0)  26.1 us
    all_to_all x1, waiting for transfers between devices, shards(): sums = lax.all_to_all(terms, 'zhi', split_axis=0, concat_axis=0, tiled=True)  19.6 us
    all_to_all x1, waiting for transfers between devices, shards(): lax.all_to_all(outbound, TEN, split_axis=0, concat_axis=0, tiled=True)  16.5 us
    pallas_call x1, Pallas kernels, attention(): pl.pallas_call(attention_kernel, out_shape=(shape, shape), grid=(4,), in_...  11.1 us
    pallas_call x1, Pallas kernels, expert(): pl.pallas_call(expert_kernel, out_shape=jax.ShapeDtypeStruct((NT, SROWS,...  9.54 us
    all_to_all x1, waiting for transfers between devices, shards(): pairs = lax.all_to_all(spread, 'x', split_axis=0, concat_axis=0, tiled=True)  8.78 us
  transfers between devices with their start and end apart: 10, of which 7 were waited for; matrix products, arithmetic and copies ran while one was open for 5% of the time, Pallas kernels for 9%

profile of v5, /device:TPU:1, one launch (start us, length us, event | category | flops | bytes accessed | tf_op | source)
XLA Modules:
  0.0 218.5 jit_solution(316700247237429685)
XLA Ops:
  7.9 1.9 pack.1
  9.8 26.9 %all_to_all.25.own_ref.after_ref = bf16[8,192,128]{2,1,0:T(8,128)(2,1)} all-to-all(bf16[8,192,128]{2,1,0:T(8,128)(2,1)} %pack.1), channel_id=1, replica_groups=mesh['y'=8,'zlo'=2,'zhi'=4,'x'=4,'core'=2] {'zhi','core'}, dimensions={0} | all-to-all | bytes 786432 | tf_op jit(solution)/shard_map/all_to_all | solution.py:401
  36.7 1.8 prepare.1
  39.5 4.0 %all-to-all-start.1 = ((bf16[4,8,96,128]{3,2,1,0:T(8,128)(2,1)}), bf16[4,8,96,128]{3,2,1,0:T(8,128)(2,1)S(1)}, u32[]{:S(2)}, u32[]{:S(2)}) async-start(bf16[4,8,96,128]{3,2,1,0:T(8,128)(2,1)} %broadcast_in_dim.27), calls=%async_computation.1 | async-start | bytes 1572864 | tf_op jit(solution)/shard_map/all_to_all | solution.py:406
  43.5 2.0 collective-permute-start
  46.3 8.8 %all-to-all-done.1.pair_ref = bf16[4,8,96,128]{3,2,1,0:T(8,128)(2,1)S(1)} async-done(((bf16[4,8,96,128]{3,2,1,0:T(8,128)(2,1)}), bf16[4,8,96,128]{3,2,1,0:T(8,128)(2,1)S(1)}, u32[]{:S(2)}, u32[]{:S(2)}) %all-to-all-start.1) | async-done | bytes 786464 | tf_op jit(solution)/shard_map/all_to_all | solution.py:406
  55.0 11.1 %attention.1 = (bf16[4,128,128]{2,1,0:T(8,128)(2,1)S(1)}, bf16[4,128,128]{2,1,0:T(8,128)(2,1)S(1)}) custom-call(s32[4]{0:T(128)S(1)} %pad_add_fusion.info_ref, bf16[8,192,128]{2,1,0:T(8,128)(2,1)S(1)} %copy-done, bf16[4,8,96,128]{3,2,1,0:T(8,128)(2,1)S(1)} %all-to-all-done.1.pair_ref), custom_call_target="tpu_custom_call" | custom-call | flops 1811939328 | bytes 3145728 | tf_op jit(solution)/shard_map/attention/pallas_call | solution.py:144
  66.8 3.6 %collective-permute-start.1 = (bf16[4,128,128]{2,1,0:T(8,128)(2,1)S(1)}, bf16[4,128,128]{2,1,0:T(8,128)(2,1)S(1)}, u32[]{:S(2)}, u32[]{:S(2)}) collective-permute-start(bf16[4,128,128]{2,1,0:T(8,128)(2,1)S(1)} %get-tuple-element.10), channel_id=1, source_target_pairs={{0,1},{1,0},{2,3},{3,2},{4,5},{5,4},{6,7},{7,6},{8,9},{9,8},{10,11... | collective-permute-start | bytes 393224 | tf_op jit(solution)/shard_map/ppermute | solution.py:410
  72.1 3.4 %group_sums.1 = bf16[4,64,1536]{2,1,0:T(8,128)(2,1)} custom-call(s32[4]{0:T(128)} %copy-done.3, bf16[4,128,128]{2,1,0:T(8,128)(2,1)} %copy-done.1, bf16[4,128,128]{2,1,0:T(8,128)(2,1)} %copy-done.9, bf16[384,1536]{1,0:T(8,128)(2,1)} %all-gather.6.cloned.1.call-done.w_ref), custom_call_target="tpu_custom_call" | custom-call | flops 301989888 | bytes 2097152 | tf_op jit(solution)/shard_map/group_sums/pallas_call | solution.py:178
  75.4 3.5 %all-to-all-start.2 = ((bf16[4,64,1536]{2,1,0:T(8,128)(2,1)}), bf16[4,64,1536]{2,1,0:T(8,128)(2,1)S(1)}, u32[]{:S(2)}, u32[]{:S(2)}) async-start(bf16[4,64,1536]{2,1,0:T(8,128)(2,1)} %group_sums.1), calls=%async_computation.2 | async-start | bytes 1572864 | tf_op jit(solution)/shard_map/all_to_all | solution.py:412
  79.7 19.6 %all-to-all-done.2.sum_ref = bf16[4,64,1536]{2,1,0:T(8,128)(2,1)S(1)} async-done(((bf16[4,64,1536]{2,1,0:T(8,128)(2,1)}), bf16[4,64,1536]{2,1,0:T(8,128)(2,1)S(1)}, u32[]{:S(2)}, u32[]{:S(2)}) %all-to-all-start.2) | async-done | bytes 786464 | tf_op jit(solution)/shard_map/all_to_all | solution.py:412
  99.3 2.6 %norm_dispatch.1 = (f32[64,1536]{1,0:T(8,128)S(1)}, bf16[32,208,128]{2,1,0:T(8,128)(2,1)}) custom-call(bf16[4,64,1536]{2,1,0:T(8,128)(2,1)S(1)} %all-to-all-done.2.sum_ref, bf16[64,1536]{1,0:T(8,128)(2,1)S(1)} %bitcast.35, f32[1,1536]{1,0:T(1,128)S(1)} %broadcast_in_dim.28.gain_ref, s32[8,64]{1,0:T(8,128)S(1)} %bitcast.34), custom_call_target="tpu_custom_call" | custom-call | flops 1073741824 | bytes 4194304 | tf_op jit(solution)/shard_map/norm_dispatch/pallas_call | solution.py:240
  101.8 6.3 %all-to-all-start.3 = ((bf16[32,208,128]{2,1,0:T(8,128)(2,1)}), bf16[32,208,128]{2,1,0:T(8,128)(2,1)S(1)}, u32[]{:S(2)}, u32[]{:S(2)}) async-start(bf16[32,208,128]{2,1,0:T(8,128)(2,1)} %get-tuple-element.11), calls=%async_computation.3 | async-start | bytes 3407872 | tf_op jit(solution)/shard_map/all_to_all | solution.py:414
  108.2 26.1 %all-gather.10.cloned.1.call-done = bf16[768,1536]{1,0:T(8,128)(2,1)} async-done(((bf16[96,1536]{1,0:T(8,128)(2,1)}), bf16[768,1536]{1,0:T(8,128)(2,1)}) %all-gather.10.cloned.1.call-update) | async-done | bytes 2359312 | tf_op jit(solution)/shard_map/all_gather | solution.py:409
  134.3 16.5 %all-to-all-done.3.in_ref = bf16[32,208,128]{2,1,0:T(8,128)(2,1)S(1)} async-done(((bf16[32,208,128]{2,1,0:T(8,128)(2,1)}), bf16[32,208,128]{2,1,0:T(8,128)(2,1)S(1)}, u32[]{:S(2)}, u32[]{:S(2)}) %all-to-all-start.3) | async-done | bytes 1703968 | tf_op jit(solution)/shard_map/all_to_all | solution.py:414
  150.8 1.2 copy-done.5
  152.0 9.5 %expert.1 = bf16[32,208,128]{2,1,0:T(8,128)(2,1)} custom-call(s32[4]{0:T(128)} %copy-done.3, bf16[32,208,128]{2,1,0:T(8,128)(2,1)} %copy-done.5, bf16[8,96,1536]{2,1,0:T(8,128)(2,1)} %bitcast.43, bf16[8,96,1536]{2,1,0:T(8,128)(2,1)} %bitcast.44), custom_call_target="tpu_custom_call" | custom-call | flops 2566914048 | bytes 9437184 | tf_op jit(solution)/shard_map/expert/pallas_call | solution.py:314
  161.6 6.0 %all-to-all-start.4 = ((bf16[32,208,128]{2,1,0:T(8,128)(2,1)}), bf16[32,208,128]{2,1,0:T(8,128)(2,1)S(1)}, u32[]{:S(2)}, u32[]{:S(2)}) async-start(bf16[32,208,128]{2,1,0:T(8,128)(2,1)} %expert.1), calls=%async_computation.4 | async-start | bytes 3407872 | tf_op jit(solution)/shard_map/all_to_all | solution.py:416
  168.9 1.4 copy.29
  170.3 2.3 %collective-permute-start.2 = (bf16[4,8,96,32]{2,3,1,0:T(8,128)(2,1)S(1)}, bf16[4,8,96,32]{2,3,1,0:T(8,128)(2,1)S(1)}, u32[]{:S(2)}, u32[]{:S(2)}) collective-permute-start(bf16[4,8,96,32]{2,3,1,0:T(8,128)(2,1)S(1)} %copy.29), channel_id=1, source_target_pairs={{0,1},{1,0},{2,3},{3,2},{4,5},{5,4},{6,7},{7,6},{8,9},{9,8},{10,11... | collective-permute-start | bytes 589832 | tf_op jit(solution)/shard_map/ppermute | solution.py:422
  174.9 2.4 %dynamic-slice_select_fusion = bf16[4,8,96,32]{3,2,1,0:T(8,128)(2,1)} fusion(bf16[4,8,96,32]{3,2,1,0:T(8,128)(2,1)} %copy.30, bf16[4,8,96,128]{3,2,1,0:T(8,128)(2,1)S(1)} %all-to-all-done.1.pair_ref, s32[]{:T(128)S(6)} %select_n.35, pred[]{:T(512)S(6)} %eq.5), kind=kLoop, calls=%fused_computation | loop fusion | flops 98304 | bytes 589829 | tf_op jit(solution)/shard_map/jit(_where)/select_n | solution.py:423
  177.3 1.4 copy.31
  180.9 29.1 %all-to-all-done.4.in_ref = bf16[32,208,128]{2,1,0:T(8,128)(2,1)S(1)} async-done(((bf16[32,208,128]{2,1,0:T(8,128)(2,1)}), bf16[32,208,128]{2,1,0:T(8,128)(2,1)S(1)}, u32[]{:S(2)}, u32[]{:S(2)}) %all-to-all-start.4) | async-done | bytes 1703968 | tf_op jit(solution)/shard_map/all_to_all | solution.py:416
  209.9 2.0 combine.1
  (51 shorter events, 10.5 us)
Async XLA Ops:
  7.2 64.3 %all-gather.6.cloned.1.call-start = ((), (), s32[]{:S(2)}) async-start(), calls=%async_computation.5 | async-start | bytes 1327104 | tf_op jit(solution)/shard_map/all_gather | solution.py:399
  7.9 100.3 %all-gather.8.cloned.1.call-start = ((), (), s32[]{:S(2)}) async-start(), calls=%async_computation.6 | async-start | bytes 2654208 | tf_op jit(solution)/shard_map/all_gather | solution.py:403
  36.7 1.8 slice-start
  38.5 5.1 %copy-start.6 = (bf16[96,1536]{1,0:T(8,128)(2,1)S(1)}, bf16[96,1536]{1,0:T(8,128)(2,1)}, u32[]{:S(2)}) copy-start(bf16[96,1536]{1,0:T(8,128)(2,1)} %prepare.1) | copy-start | bytes 884740
  38.5 16.6 %copy-start = (bf16[8,192,128]{2,1,0:T(8,128)(2,1)S(1)}, bf16[8,192,128]{2,1,0:T(8,128)(2,1)}, u32[]{:S(2)}) copy-start(bf16[8,192,128]{2,1,0:T(8,128)(2,1)} %all_to_all.25.own_ref.after_ref) | copy-start | bytes 1179652
  39.5 15.5 %all-to-all-start.1 = ((bf16[4,8,96,128]{3,2,1,0:T(8,128)(2,1)}), bf16[4,8,96,128]{3,2,1,0:T(8,128)(2,1)S(1)}, u32[]{:S(2)}, u32[]{:S(2)}) async-start(bf16[4,8,96,128]{3,2,1,0:T(8,128)(2,1)} %broadcast_in_dim.27), calls=%async_computation.1 | async-start | bytes 1572864 | tf_op jit(solution)/shard_map/all_to_all | solution.py:406
  43.5 23.3 %collective-permute-start = (bf16[96,1536]{1,0:T(8,128)(2,1)S(1)}, bf16[96,1536]{1,0:T(8,128)(2,1)S(1)}, u32[]{:S(2)}, u32[]{:S(2)}) collective-permute-start(bf16[96,1536]{1,0:T(8,128)(2,1)S(1)} %copy-done.6), channel_id=1, source_target_pairs={{0,32},{32,0},{1,33},{33,1},{2,34},{34,2},{3,35},{35,3},{4,36},{36... | collective-permute-start | bytes 884744 | tf_op jit(solution)/shard_map/ppermute | solution.py:404
  46.2 19.9 %copy-start.3 = (s32[4]{0:T(128)}, s32[4]{0:T(128)S(1)}, u32[]{:S(2)}) copy-start(s32[4]{0:T(128)S(1)} %pad_add_fusion.info_ref) | copy-start | bytes 52
  66.1 0.7 copy-start.1
  66.8 4.6 %copy-start.7 = (bf16[96,1536]{1,0:T(8,128)(2,1)}, bf16[96,1536]{1,0:T(8,128)(2,1)S(1)}, u32[]{:S(2)}) copy-start(bf16[96,1536]{1,0:T(8,128)(2,1)S(1)} %collective-permute-done) | copy-start | bytes 884740
  66.8 4.6 %collective-permute-start.1 = (bf16[4,128,128]{2,1,0:T(8,128)(2,1)S(1)}, bf16[4,128,128]{2,1,0:T(8,128)(2,1)S(1)}, u32[]{:S(2)}, u32[]{:S(2)}) collective-permute-start(bf16[4,128,128]{2,1,0:T(8,128)(2,1)S(1)} %get-tuple-element.10), channel_id=1, source_target_pairs={{0,1},{1,0},{2,3},{3,2},{4,5},{5,4},{6,7},{7,6},{8,9},{9,8},{10,11... | collective-permute-start | bytes 393224 | tf_op jit(solution)/shard_map/ppermute | solution.py:410
  71.4 0.7 copy-start.9
  72.1 7.6 %copy-start.10 = (f32[1536]{0:T(1024)S(1)}, f32[1536]{0:T(1024)}, u32[]{:S(2)}) copy-start(f32[1536]{0:T(1024)} %param.19) | copy-start | bytes 18436
  72.1 27.2 %copy-start.2 = (s32[1,1,1,64,8]{3,4,2,1,0:T(8,128)S(1)}, s32[1,1,1,64,8]{3,4,2,1,0:T(8,128)}, u32[]{:S(2)}) copy-start(s32[1,1,1,64,8]{3,4,2,1,0:T(8,128)} %param.16) | copy-start | bytes 6148
  72.1 27.2 %copy-start.4 = (bf16[1,1,1,64,1536]{4,3,2,1,0:T(8,128)(2,1)S(1)}, bf16[1,1,1,64,1536]{4,3,2,1,0:T(8,128)(2,1)}, u32[]{:S(2)}) copy-start(bf16[1,1,1,64,1536]{4,3,2,1,0:T(8,128)(2,1)} %param.11) | copy-start | bytes 589828
  75.4 23.8 %all-to-all-start.2 = ((bf16[4,64,1536]{2,1,0:T(8,128)(2,1)}), bf16[4,64,1536]{2,1,0:T(8,128)(2,1)S(1)}, u32[]{:S(2)}, u32[]{:S(2)}) async-start(bf16[4,64,1536]{2,1,0:T(8,128)(2,1)} %group_sums.1), calls=%async_computation.2 | async-start | bytes 1572864 | tf_op jit(solution)/shard_map/all_to_all | solution.py:412
  78.9 55.3 %all-gather.10.cloned.1.call-start = ((), (), s32[]{:S(2)}) async-start(), calls=%async_computation.7 | async-start | bytes 2654208 | tf_op jit(solution)/shard_map/all_gather | solution.py:409
  101.8 49.0 %all-to-all-start.3 = ((bf16[32,208,128]{2,1,0:T(8,128)(2,1)}), bf16[32,208,128]{2,1,0:T(8,128)(2,1)S(1)}, u32[]{:S(2)}, u32[]{:S(2)}) async-start(bf16[32,208,128]{2,1,0:T(8,128)(2,1)} %get-tuple-element.11), calls=%async_computation.3 | async-start | bytes 3407872 | tf_op jit(solution)/shard_map/all_to_all | solution.py:414
  150.8 1.2 copy-start.5
  161.6 48.3 %all-to-all-start.4 = ((bf16[32,208,128]{2,1,0:T(8,128)(2,1)}), bf16[32,208,128]{2,1,0:T(8,128)(2,1)S(1)}, u32[]{:S(2)}, u32[]{:S(2)}) async-start(bf16[32,208,128]{2,1,0:T(8,128)(2,1)} %expert.1), calls=%async_computation.4 | async-start | bytes 3407872 | tf_op jit(solution)/shard_map/all_to_all | solution.py:416
  167.6 5.1 %copy-start.11 = (f32[1,1,1,64,8]{3,4,2,1,0:T(8,128)S(1)}, f32[1,1,1,64,8]{3,4,2,1,0:T(8,128)}, u32[]{:S(2)}) copy-start(f32[1,1,1,64,8]{3,4,2,1,0:T(8,128)} %param.17) | copy-start | bytes 6148
  170.3 3.4 %collective-permute-start.2 = (bf16[4,8,96,32]{2,3,1,0:T(8,128)(2,1)S(1)}, bf16[4,8,96,32]{2,3,1,0:T(8,128)(2,1)S(1)}, u32[]{:S(2)}, u32[]{:S(2)}) collective-permute-start(bf16[4,8,96,32]{2,3,1,0:T(8,128)(2,1)S(1)} %copy.29), channel_id=1, source_target_pairs={{0,1},{1,0},{2,3},{3,2},{4,5},{5,4},{6,7},{7,6},{8,9},{9,8},{10,11... | collective-permute-start | bytes 589832 | tf_op jit(solution)/shard_map/ppermute | solution.py:422
  180.9 31.1 %copy-start.8 = (bf16[1,3072,32]{1,2,0:T(8,128)(2,1)}, bf16[1,3072,32]{1,2,0:T(8,128)(2,1)S(1)}, u32[]{:S(2)}) copy-start(bf16[1,3072,32]{1,2,0:T(8,128)(2,1)S(1)} %dynamic_update_slice.4) | copy-start | bytes 589828
Sparse Core Ops, SparseCore 0:
  10.1 34.8 all-gather.5
  47.1 41.9 all-gather.7
  91.2 43.0 all-gather.9

commit v6 on v5

--- a/solution.py
+++ b/solution.py
@@ -162,48 +162,73 @@
     )(info, own, pairs)
 
 
-def group_sums_kernel(info_ref, own_ref, oth_ref, w_ref, o_ref):
-    core = info_ref[1]
-    total = jnp.zeros((256, D), F32)
-    for src, side in ((own_ref, core), (oth_ref, 1 - core)):
-        pair = src[:, 0:64, :].reshape(256, 128)
-        last = src[:, 64:128, :].reshape(256, 128)[:, :HD]
-        at = pl.multiple_of(side * 192, 64)
-        total = total + dot(pair, w_ref[pl.ds(at, 128), :])
-        total = total + dot(last, w_ref[pl.ds(pl.multiple_of(at + 128, 64), HD), :])
-    o_ref[...] = total.astype(BF).reshape(4, TOK, D)
-
-
-def group_sums(info, own, other, weight):
+def group_sums_kernel(info_ref, own_ref, oth_ref, wo_ref, wx_ref, o_ref, w, o, sems, out_sems):
+    core, x = info_ref[1], info_ref[2]
+    copies = []
+    for at in range(4):
+        turn = (x + 4 - at) % 4
+        for n, (src, side) in enumerate(((wo_ref, core), (wx_ref, 1 - core))):
+            row = pl.multiple_of((2 * at + side) * 48, 16)
+            copies.append(pltpu.make_async_copy(src.at[turn], w.at[pl.ds(row, 48), :], sems.at[at, n]))
+            copies[-1].start()
+    sides = ((own_ref, core), (oth_ref, 1 - core))
+    pairs = [src[:, 0:64, :].reshape(256, 128) for src, _ in sides]
+    lasts = [src[:, 64:128, :].reshape(256, 128)[:, :HD] for src, _ in sides]
+    for copy in copies:
+        copy.wait()
+    sent = []
+    for n in range(3):
+        cols = pl.ds(n * 512, 512)
+        total = jnp.zeros((256, 512), F32)
+        for pair, last, (_, side) in zip(pairs, lasts, sides):
+            at = pl.multiple_of(side * 192, 64)
+            total = total + dot(pair, w[pl.ds(at, 128), cols])
+            total = total + dot(last, w[pl.ds(pl.multiple_of(at + 128, 64), HD), cols])
+        o[:, :, cols] = total.astype(BF).reshape(4, TOK, 512)
+        sent.append(pltpu.make_async_copy(o.at[:, :, cols], o_ref.at[:, :, cols], out_sems.at[n]))
+        sent[-1].start()
+    for copy in sent:
+        copy.wait()
+
+
+def group_sums(info, own, other, own_weight, other_weight):
+    anywhere = pl.BlockSpec(memory_space=pl.ANY)
     return pl.pallas_call(
         group_sums_kernel,
         out_shape=jax.ShapeDtypeStruct((4, TOK, D), BF),
-        in_specs=[pl.BlockSpec(memory_space=pltpu.SMEM)] + [vmem()] * 3,
-        out_specs=vmem(),
-        compiler_params=params(62.5),
+        in_specs=[pl.BlockSpec(memory_space=pltpu.SMEM), vmem(), vmem(), anywhere, anywhere],
+        out_specs=pl.BlockSpec(memory_space=pltpu.HBM),
+        scratch_shapes=[
+            pltpu.VMEM((384, D), BF),
+            pltpu.VMEM((4, TOK, D), BF),
+            pltpu.SemaphoreType.DMA((4, 2)),
+            pltpu.SemaphoreType.DMA((3,)),
+        ],
+        compiler_params=params(20),
         cost_estimate=pl.CostEstimate(flops=2 * 256 * 384 * D, bytes_accessed=2 << 20, transcendentals=0),
         interpret=INTERPRET,
         name="group_sums",
-    )(info, own, other, weight)
-
-
-def prepare_kernel(up_ref, down_ref, after_ref, o_ref):
+    )(info, own, other, own_weight, other_weight)
+
+
+def prepare_kernel(up_ref, down_ref, shard_ref, after_ref, o_ref, so_ref):
     o_ref[0:64, 0:1024] = up_ref[0:64, :]
     o_ref[0:32, 1024:1536] = up_ref[64:96, 0:512]
     o_ref[32:64, 1024:1536] = up_ref[64:96, 512:1024]
     o_ref[64:96, :] = down_ref[...]
-
-
-def prepare(up, down, after):
+    so_ref[...] = shard_ref[...]
+
+
+def prepare(up, down, shard, after):
     return pl.pallas_call(
         prepare_kernel,
-        out_shape=jax.ShapeDtypeStruct((96, D), BF),
-        in_specs=[vmem()] * 2 + [pl.BlockSpec(memory_space=pl.ANY)],
-        out_specs=vmem(),
+        out_shape=(jax.ShapeDtypeStruct((96, D), BF), jax.ShapeDtypeStruct(shard.shape, BF)),
+        in_specs=[vmem()] * 3 + [pl.BlockSpec(memory_space=pl.ANY)],
+        out_specs=(vmem(), vmem()),
         cost_estimate=pl.CostEstimate(flops=1 << 33, bytes_accessed=1 << 20, transcendentals=0),
         interpret=INTERPRET,
         name="prepare",
-    )(up, down, after)
+    )(up, down, shard, after)
 
 
 def norm_dispatch_kernel(sum_ref, hid_ref, gain_ref, ids_ref, res_ref, disp_ref):
@@ -260,17 +285,7 @@
     return [stacked[c * NT : (c + 1) * NT, :] for c in range(CH)]
 
 
-def spread_extra(rows):
-    place = iota((512, NT), 0)
-    owner = place // 16 == iota((512, NT), 1)
-    out = jnp.zeros((512, 128), F32)
-    for c in range(CH):
-        match = jnp.where(owner & (place % 16 == c), 1.0, 0.0).astype(BF)
-        out = out + dot(match, rows[:, c * 128 : c * 128 + 128])
-    return out.astype(BF)
-
-
-def expert_kernel(info_ref, in_ref, wo_ref, wx_ref, o_ref, x, w1, w2, sems):
+def expert_kernel(info_ref, in_ref, wo_ref, wx_ref, o_ref, x, w1, w2, o, sems, out_sems):
     zlo = info_ref[3]
     copies = []
     for d in range(2 * wo_ref.shape[0]):
@@ -289,24 +304,42 @@
     lasts = copies[3::4]
     for copy in firsts + lasts:
         copy.start()
+    depth = w1.shape[0] // 4
     for c in range(CH):
         x[0:512, c * 128 : c * 128 + 128] = in_ref[:, c * SLOT : (c + 1) * SLOT, :].reshape(512, 128)
     chunks = gather_extra(in_ref[:, SLOT * CH : SROWS, :].reshape(512, 128))
     for c in range(CH):
         x[512:544, c * 128 : c * 128 + 128] = chunks[c]
-    for copy in firsts:
-        copy.wait()
-    hidden = dot(x[...], w1[...])
+    hidden = jnp.zeros((544, 2 * FFE), F32)
+    for n in range(4):
+        for copy in firsts[n * len(firsts) // 4 : (n + 1) * len(firsts) // 4]:
+            copy.wait()
+        at = n * depth
+        hidden = hidden + dot(x[:, at : at + depth], w1[at : at + depth, :])
     gate = hidden[:, :FFE]
     active = (gate / (1.0 + jnp.exp(-gate)) * hidden[:, FFE:]).astype(BF)
     for copy in lasts:
         copy.wait()
-    out = dot(active, w2[...]).astype(BF)
-    for c in range(CH):
-        o_ref[:, c * SLOT : (c + 1) * SLOT, :] = out[0:512, c * 128 : c * 128 + 128].reshape(
-            NT, SLOT, 128
-        )
-    o_ref[:, SLOT * CH : SROWS, :] = spread_extra(out[512:544, :]).reshape(NT, 16, 128)
+    place = iota((512, NT), 0)
+    owner = place // 16 == iota((512, NT), 1)
+    extra = jnp.zeros((512, 128), F32)
+    sent = []
+    for c in range(0, CH, 2):
+        out = dot(active, w2[:, c * 128 : c * 128 + 256]).astype(BF)
+        for n in range(2):
+            cols = slice(n * 128, n * 128 + 128)
+            o[:, (c + n) * SLOT : (c + n + 1) * SLOT, :] = out[0:512, cols].reshape(NT, SLOT, 128)
+            match = jnp.where(owner & (place % 16 == c + n), 1.0, 0.0).astype(BF)
+            extra = extra + dot(match, out[512:544, cols])
+        rows = pl.ds(c * SLOT, 2 * SLOT)
+        sent.append(pltpu.make_async_copy(o.at[:, rows, :], o_ref.at[:, rows, :], out_sems.at[c // 2]))
+        sent[-1].start()
+    o[:, SLOT * CH : SROWS, :] = extra.astype(BF).reshape(NT, 16, 128)
+    rows = pl.ds(CH * SLOT, 16)
+    sent.append(pltpu.make_async_copy(o.at[:, rows, :], o_ref.at[:, rows, :], out_sems.at[CH // 2]))
+    sent[-1].start()
+    for copy in sent:
+        copy.wait()
 
 
 def expert(info, slots, own_weights, other_weights):
@@ -316,12 +349,14 @@
         out_shape=jax.ShapeDtypeStruct((NT, SROWS, 128), BF),
         in_specs=[pl.BlockSpec(memory_space=pltpu.SMEM), vmem()]
         + [pl.BlockSpec(memory_space=pltpu.HBM)] * 2,
-        out_specs=vmem(),
+        out_specs=pl.BlockSpec(memory_space=pltpu.HBM),
         scratch_shapes=[
             pltpu.VMEM((544, D), BF),
             pltpu.VMEM((blocks * 96, 2 * FFE), BF),
             pltpu.VMEM((blocks * 32, D), BF),
+            pltpu.VMEM((NT, SROWS, 128), BF),
             pltpu.SemaphoreType.DMA((blocks, 4)),
+            pltpu.SemaphoreType.DMA((CH // 2 + 1,)),
         ],
         compiler_params=params(58),
         cost_estimate=pl.CostEstimate(
@@ -396,19 +431,24 @@
     ids = expert_ids[0, 0, 0]
     gates = route_gates[0, 0, 0]
 
-    plane_weight = lax.all_gather(output_weight, ("x", "core"), axis=0, tiled=True)
     send = pack(rotated_queries[0, 0, 0], fresh_key_values[0, 0, 0], cached_key_values[0])
+    packed, shard = prepare(gate_up[0], down_weight[0], output_weight, send)
+    own_weights = lax.all_gather(packed, "y", axis=0)
+    turns = [
+        lax.ppermute(shard, "x", [(n, (n + step) % 4) for n in range(4)]) for step in (1, 2, 3)
+    ]
     own = lax.all_to_all(send, ("zhi", "core"), split_axis=0, concat_axis=0, tiled=True)
-    packed = prepare(gate_up[0], down_weight[0], own)
-    own_weights = lax.all_gather(packed, "y", axis=0)
+    turns, packed, own = lax.optimization_barrier((turns, packed, own))
     across = lax.ppermute(packed, "zlo", [(0, 1), (1, 0)])
+    own_rows = jnp.stack([shard, *turns], 0)
+    other_rows = lax.ppermute(own_rows, "core", [(0, 1), (1, 0)])
     spread = jnp.broadcast_to(own[None, :, 96:], (4, HKV, 96, 128))
     pairs = lax.all_to_all(spread, "x", split_axis=0, concat_axis=0, tiled=True)
     kept, sent = attention(info, own, pairs)
-    across, sent = lax.optimization_barrier((across, sent))
+    across, other_rows, sent = lax.optimization_barrier((across, other_rows, sent))
     other_weights = lax.all_gather(across, "y", axis=0)
     swapped = lax.ppermute(sent, "core", [(0, 1), (1, 0)])
-    terms = group_sums(info, kept, swapped, plane_weight)
+    terms = group_sums(info, kept, swapped, own_rows, other_rows)
     sums = lax.all_to_all(terms, "zhi", split_axis=0, concat_axis=0, tiled=True)
     residual, outbound = norm_dispatch(sums, hidden_in[0, 0, 0], norm_gain[None], ids.T)
     slots = lax.all_to_all(outbound, TEN, split_axis=0, concat_axis=0, tiled=True)

time: 219 us -> 220 us (level)
  the two profiles are of different devices: /device:TPU:1 before, /device:TPU:60 now
where the time goes in v6:
time: 220 us; the launch traced here: 219 us
  waiting for transfers between devices  102 us (46%)
  starting transfers between devices  57.1 us (26%)
  Pallas kernels  32.8 us (15%)
  between operations  15 us (7%)
  local copies, waits for them, and re-layouts  9.78 us (4%)
  other arithmetic  2.56 us (1%)
    all_to_all x1, waiting for transfers between devices, shards(): lax.all_to_all(computed, TEN, split_axis=0, concat_axis=0, tiled=True)  29.8 us
    all_to_all x1, waiting for transfers between devices, shards(): lax.all_to_all(outbound, TEN, split_axis=0, concat_axis=0, tiled=True)  26.5 us
    all_gather x1, waiting for transfers between devices, shards(): other_weights = lax.all_gather(across, 'y', axis=0)  16.4 us
    all_to_all x1, waiting for transfers between devices, shards(): sums = lax.all_to_all(terms, 'zhi', split_axis=0, concat_axis=0, tiled=True)  16.3 us
    all_to_all x1, starting transfers between devices, shards(): lax.all_to_all(outbound, TEN, split_axis=0, concat_axis=0, tiled=True)  11.9 us
    pallas_call x1, Pallas kernels, attention(): pl.pallas_call(attention_kernel, out_shape=(shape, shape), grid=(4,), in_...  11.1 us
    all_to_all x1, starting transfers between devices, shards(): lax.all_to_all(send, ('zhi', 'core'), split_axis=0, concat_axis=0, tiled=...  10.4 us
    pallas_call x1, Pallas kernels, expert(): pl.pallas_call(expert_kernel, out_shape=jax.ShapeDtypeStruct((NT, SROWS,...  9.52 us
  transfers between devices with their start and end apart: 14, of which 10 were waited for; matrix products, arithmetic and copies ran while one was open for 5% of the time, Pallas kernels for 8%

profile of v6, /device:TPU:60, one launch (start us, length us, event | category | flops | bytes accessed | tf_op | source)
XLA Modules:
  0.0 219.3 jit_solution(12120763440494388122)
XLA Ops:
  10.9 10.4 %all-to-all-start = ((bf16[8,192,128]{2,1,0:T(8,128)(2,1)}), bf16[8,192,128]{2,1,0:T(8,128)(2,1)S(1)}, u32[]{:S(2)}, u32[]{:S(2)}) async-start(bf16[8,192,128]{2,1,0:T(8,128)(2,1)} %pack.1.after_ref), calls=%async_computation | async-start | bytes 786432 | tf_op jit(solution)/shard_map/all_to_all | solution.py:440
  21.4 3.1 %collective-permute-start = (bf16[48,1536]{1,0:T(8,128)(2,1)}, bf16[48,1536]{1,0:T(8,128)(2,1)S(1)}, u32[]{:S(2)}, u32[]{:S(2)}) collective-permute-start(bf16[48,1536]{1,0:T(8,128)(2,1)} %get-tuple-element.16), channel_id=1, source_target_pairs={{0,2},{2,4},{4,6},{6,0},{1,3},{3,5},{5,7},{7,1},{8,10},{10,12},{12... | collective-permute-start | bytes 442376 | tf_op jit(solution)/shard_map/ppermute | solution.py:438
  24.5 2.7 %collective-permute-start.1 = (bf16[48,1536]{1,0:T(8,128)(2,1)}, bf16[48,1536]{1,0:T(8,128)(2,1)S(1)}, u32[]{:S(2)}, u32[]{:S(2)}) collective-permute-start(bf16[48,1536]{1,0:T(8,128)(2,1)} %get-tuple-element.16), channel_id=1, source_target_pairs={{0,4},{2,6},{4,0},{6,2},{1,5},{3,7},{5,1},{7,3},{8,12},{10,14},{12... | collective-permute-start | bytes 442376 | tf_op jit(solution)/shard_map/ppermute | solution.py:438
  27.2 3.0 %collective-permute-start.2 = (bf16[48,1536]{1,0:T(8,128)(2,1)}, bf16[48,1536]{1,0:T(8,128)(2,1)S(1)}, u32[]{:S(2)}, u32[]{:S(2)}) collective-permute-start(bf16[48,1536]{1,0:T(8,128)(2,1)} %get-tuple-element.16), channel_id=1, source_target_pairs={{0,6},{2,0},{4,2},{6,4},{1,7},{3,1},{5,3},{7,5},{8,14},{10,8},{12,... | collective-permute-start | bytes 442376 | tf_op jit(solution)/shard_map/ppermute | solution.py:438
  30.3 3.8 %collective-permute-done.1 = bf16[48,1536]{1,0:T(8,128)(2,1)S(1)} collective-permute-done((bf16[48,1536]{1,0:T(8,128)(2,1)}, bf16[48,1536]{1,0:T(8,128)(2,1)S(1)}, u32[]{:S(2)}, u32[]{:S(2)}) %collective-permute-start.1) | collective-permute-done | bytes 147488 | tf_op jit(solution)/shard_map/ppermute | solution.py:438
  34.1 2.5 %collective-permute-done.2 = bf16[48,1536]{1,0:T(8,128)(2,1)S(1)} collective-permute-done((bf16[48,1536]{1,0:T(8,128)(2,1)}, bf16[48,1536]{1,0:T(8,128)(2,1)S(1)}, u32[]{:S(2)}, u32[]{:S(2)}) %collective-permute-start.2) | collective-permute-done | bytes 147488 | tf_op jit(solution)/shard_map/ppermute | solution.py:438
  38.0 4.8 %all-to-all-start.1 = ((bf16[4,8,96,128]{3,2,1,0:T(8,128)(2,1)}), bf16[4,8,96,128]{3,2,1,0:T(8,128)(2,1)S(1)}, u32[]{:S(2)}, u32[]{:S(2)}) async-start(bf16[4,8,96,128]{3,2,1,0:T(8,128)(2,1)} %broadcast_in_dim.27), calls=%async_computation.1 | async-start | bytes 1572864 | tf_op jit(solution)/shard_map/all_to_all | solution.py:446
  42.9 1.9 collective-permute-start.4
  44.8 3.3 %collective-permute-start.3 = (bf16[96,1536]{1,0:T(8,128)(2,1)S(1)}, bf16[96,1536]{1,0:T(8,128)(2,1)S(1)}, u32[]{:S(2)}, u32[]{:S(2)}) collective-permute-start(bf16[96,1536]{1,0:T(8,128)(2,1)S(1)} %copy-done.4), channel_id=1, source_target_pairs={{0,32},{32,0},{1,33},{33,1},{2,34},{34,2},{3,35},{35,3},{4,36},{36... | collective-permute-start | bytes 884744 | tf_op jit(solution)/shard_map/ppermute | solution.py:442
  48.8 3.3 %all-to-all-done.1.pair_ref = bf16[4,8,96,128]{3,2,1,0:T(8,128)(2,1)S(1)} async-done(((bf16[4,8,96,128]{3,2,1,0:T(8,128)(2,1)}), bf16[4,8,96,128]{3,2,1,0:T(8,128)(2,1)S(1)}, u32[]{:S(2)}, u32[]{:S(2)}) %all-to-all-start.1) | async-done | bytes 786464 | tf_op jit(solution)/shard_map/all_to_all | solution.py:446
  52.2 11.1 %attention.1 = (bf16[4,128,128]{2,1,0:T(8,128)(2,1)S(1)}, bf16[4,128,128]{2,1,0:T(8,128)(2,1)S(1)}) custom-call(s32[4]{0:T(128)S(1)} %pad_add_fusion.info_ref, bf16[8,192,128]{2,1,0:T(8,128)(2,1)S(1)} %all-to-all-done.own_ref, bf16[4,8,96,128]{3,2,1,0:T(8,128)(2,1)S(1)} %all-to-all-done.1.pair_ref), custom_call_target="tpu_custom_call" | custom-call | flops 1811939328 | bytes 3145728 | tf_op jit(solution)/shard_map/attention/pallas_call | solution.py:144
  66.6 3.9 %group_sums.1 = bf16[4,64,1536]{2,1,0:T(8,128)(2,1)} custom-call(s32[4]{0:T(128)S(1)} %pad_add_fusion.info_ref, bf16[4,128,128]{2,1,0:T(8,128)(2,1)S(1)} %get-tuple-element.19.own_ref, bf16[4,128,128]{2,1,0:T(8,128)(2,1)S(1)} %collective-permute-done.5.oth_ref, bf16[4,48,1536]{2,1,0:T(8,128)(2,1)S(1)} %pad_maximum_fusion.wo_ref, ...), custom_call_target="tpu_custom_call" | custom-call | flops 301989888 | bytes 2097152 | tf_op jit(solution)/shard_map/group_sums/pallas_call | solution.py:196
  70.5 6.6 %all-to-all-start.2 = ((bf16[4,64,1536]{2,1,0:T(8,128)(2,1)}), bf16[4,64,1536]{2,1,0:T(8,128)(2,1)S(1)}, u32[]{:S(2)}, u32[]{:S(2)}) async-start(bf16[4,64,1536]{2,1,0:T(8,128)(2,1)} %group_sums.1), calls=%async_computation.2 | async-start | bytes 1572864 | tf_op jit(solution)/shard_map/all_to_all | solution.py:452
  77.9 16.3 %all-to-all-done.2.sum_ref = bf16[4,64,1536]{2,1,0:T(8,128)(2,1)S(1)} async-done(((bf16[4,64,1536]{2,1,0:T(8,128)(2,1)}), bf16[4,64,1536]{2,1,0:T(8,128)(2,1)S(1)}, u32[]{:S(2)}, u32[]{:S(2)}) %all-to-all-start.2) | async-done | bytes 786464 | tf_op jit(solution)/shard_map/all_to_all | solution.py:452
  94.2 2.6 %norm_dispatch.1 = (f32[64,1536]{1,0:T(8,128)S(1)}, bf16[32,208,128]{2,1,0:T(8,128)(2,1)}) custom-call(bf16[4,64,1536]{2,1,0:T(8,128)(2,1)S(1)} %all-to-all-done.2.sum_ref, bf16[64,1536]{1,0:T(8,128)(2,1)S(1)} %bitcast.39, f32[1,1536]{1,0:T(1,128)S(1)} %broadcast_in_dim.28.gain_ref, s32[8,64]{1,0:T(8,128)S(1)} %bitcast.38), custom_call_target="tpu_custom_call" | custom-call | flops 1073741824 | bytes 4194304 | tf_op jit(solution)/shard_map/norm_dispatch/pallas_call | solution.py:265
  96.8 11.9 %all-to-all-start.3 = ((bf16[32,208,128]{2,1,0:T(8,128)(2,1)}), bf16[32,208,128]{2,1,0:T(8,128)(2,1)S(1)}, u32[]{:S(2)}, u32[]{:S(2)}) async-start(bf16[32,208,128]{2,1,0:T(8,128)(2,1)} %get-tuple-element.27), calls=%async_computation.3 | async-start | bytes 3407872 | tf_op jit(solution)/shard_map/all_to_all | solution.py:454
  108.7 16.4 %all-gather.7.cloned.1.call-done = bf16[768,1536]{1,0:T(8,128)(2,1)} async-done(((bf16[96,1536]{1,0:T(8,128)(2,1)}), bf16[768,1536]{1,0:T(8,128)(2,1)}) %all-gather.7.cloned.1.call-update) | async-done | bytes 2359312 | tf_op jit(solution)/shard_map/all_gather | solution.py:449
  125.2 26.5 %all-to-all-done.3.in_ref = bf16[32,208,128]{2,1,0:T(8,128)(2,1)S(1)} async-done(((bf16[32,208,128]{2,1,0:T(8,128)(2,1)}), bf16[32,208,128]{2,1,0:T(8,128)(2,1)S(1)}, u32[]{:S(2)}, u32[]{:S(2)}) %all-to-all-start.3) | async-done | bytes 1703968 | tf_op jit(solution)/shard_map/all_to_all | solution.py:454
  153.0 9.5 %expert.1 = bf16[32,208,128]{2,1,0:T(8,128)(2,1)} custom-call(s32[4]{0:T(128)} %copy-done.1, bf16[32,208,128]{2,1,0:T(8,128)(2,1)} %copy-done.3, bf16[8,96,1536]{2,1,0:T(8,128)(2,1)} %bitcast.51, bf16[8,96,1536]{2,1,0:T(8,128)(2,1)} %bitcast.52), custom_call_target="tpu_custom_call" | custom-call | flops 2566914048 | bytes 9437184 | tf_op jit(solution)/shard_map/expert/pallas_call | solution.py:347
  162.5 5.0 %all-to-all-start.4 = ((bf16[32,208,128]{2,1,0:T(8,128)(2,1)}), bf16[32,208,128]{2,1,0:T(8,128)(2,1)S(1)}, u32[]{:S(2)}, u32[]{:S(2)}) async-start(bf16[32,208,128]{2,1,0:T(8,128)(2,1)} %expert.1), calls=%async_computation.4 | async-start | bytes 3407872 | tf_op jit(solution)/shard_map/all_to_all | solution.py:456
  170.1 2.2 %collective-permute-start.6 = (bf16[4,8,96,32]{2,3,1,0:T(8,128)(2,1)S(1)}, bf16[4,8,96,32]{2,3,1,0:T(8,128)(2,1)S(1)}, u32[]{:S(2)}, u32[]{:S(2)}) collective-permute-start(bf16[4,8,96,32]{2,3,1,0:T(8,128)(2,1)S(1)} %copy.29), channel_id=1, source_target_pairs={{0,1},{1,0},{2,3},{3,2},{4,5},{5,4},{6,7},{7,6},{8,9},{9,8},{10,11... | collective-permute-start | bytes 589832 | tf_op jit(solution)/shard_map/ppermute | solution.py:462
  174.7 2.4 %dynamic-slice_select_fusion = bf16[4,8,96,32]{3,2,1,0:T(8,128)(2,1)} fusion(bf16[4,8,96,32]{3,2,1,0:T(8,128)(2,1)} %copy.30, bf16[4,8,96,128]{3,2,1,0:T(8,128)(2,1)S(1)} %all-to-all-done.1.pair_ref, s32[]{:T(128)S(6)} %select_n.35, pred[]{:T(512)S(6)} %eq.5), kind=kLoop, calls=%fused_computation | loop fusion | flops 98304 | bytes 589829 | tf_op jit(solution)/shard_map/jit(_where)/select_n | solution.py:463
  180.7 29.8 %all-to-all-done.4.in_ref = bf16[32,208,128]{2,1,0:T(8,128)(2,1)S(1)} async-done(((bf16[32,208,128]{2,1,0:T(8,128)(2,1)}), bf16[32,208,128]{2,1,0:T(8,128)(2,1)S(1)}, u32[]{:S(2)}, u32[]{:S(2)}) %all-to-all-start.4) | async-done | bytes 1703968 | tf_op jit(solution)/shard_map/all_to_all | solution.py:456
  210.5 2.0 combine.1
  (53 shorter events, 19.0 us)
Async XLA Ops:
  7.2 101.6 %all-gather.5.cloned.1.call-start = ((), (), s32[]{:S(2)}) async-start(), calls=%async_computation.5 | async-start | bytes 2654208 | tf_op jit(solution)/shard_map/all_gather | solution.py:436
  10.9 31.9 %copy-start.7 = (bf16[48,1536]{1,0:T(8,128)(2,1)S(1)}, bf16[48,1536]{1,0:T(8,128)(2,1)}, u32[]{:S(2)}) copy-start(bf16[48,1536]{1,0:T(8,128)(2,1)} %get-tuple-element.16) | copy-start | bytes 442372
  10.9 26.0 %all-to-all-start = ((bf16[8,192,128]{2,1,0:T(8,128)(2,1)}), bf16[8,192,128]{2,1,0:T(8,128)(2,1)S(1)}, u32[]{:S(2)}, u32[]{:S(2)}) async-start(bf16[8,192,128]{2,1,0:T(8,128)(2,1)} %pack.1.after_ref), calls=%async_computation | async-start | bytes 786432 | tf_op jit(solution)/shard_map/all_to_all | solution.py:440
  21.4 8.9 %collective-permute-start = (bf16[48,1536]{1,0:T(8,128)(2,1)}, bf16[48,1536]{1,0:T(8,128)(2,1)S(1)}, u32[]{:S(2)}, u32[]{:S(2)}) collective-permute-start(bf16[48,1536]{1,0:T(8,128)(2,1)} %get-tuple-element.16), channel_id=1, source_target_pairs={{0,2},{2,4},{4,6},{6,0},{1,3},{3,5},{5,7},{7,1},{8,10},{10,12},{12... | collective-permute-start | bytes 442376 | tf_op jit(solution)/shard_map/ppermute | solution.py:438
  24.5 9.6 %collective-permute-start.1 = (bf16[48,1536]{1,0:T(8,128)(2,1)}, bf16[48,1536]{1,0:T(8,128)(2,1)S(1)}, u32[]{:S(2)}, u32[]{:S(2)}) collective-permute-start(bf16[48,1536]{1,0:T(8,128)(2,1)} %get-tuple-element.16), channel_id=1, source_target_pairs={{0,4},{2,6},{4,0},{6,2},{1,5},{3,7},{5,1},{7,3},{8,12},{10,14},{12... | collective-permute-start | bytes 442376 | tf_op jit(solution)/shard_map/ppermute | solution.py:438
  27.2 9.4 %collective-permute-start.2 = (bf16[48,1536]{1,0:T(8,128)(2,1)}, bf16[48,1536]{1,0:T(8,128)(2,1)S(1)}, u32[]{:S(2)}, u32[]{:S(2)}) collective-permute-start(bf16[48,1536]{1,0:T(8,128)(2,1)} %get-tuple-element.16), channel_id=1, source_target_pairs={{0,6},{2,0},{4,2},{6,4},{1,7},{3,1},{5,3},{7,5},{8,14},{10,8},{12,... | collective-permute-start | bytes 442376 | tf_op jit(solution)/shard_map/ppermute | solution.py:438
  37.0 7.8 %copy-start.4 = (bf16[96,1536]{1,0:T(8,128)(2,1)S(1)}, bf16[96,1536]{1,0:T(8,128)(2,1)}, u32[]{:S(2)}) copy-start(bf16[96,1536]{1,0:T(8,128)(2,1)} %get-tuple-element.20) | copy-start | bytes 884740
  38.0 14.2 %all-to-all-start.1 = ((bf16[4,8,96,128]{3,2,1,0:T(8,128)(2,1)}), bf16[4,8,96,128]{3,2,1,0:T(8,128)(2,1)S(1)}, u32[]{:S(2)}, u32[]{:S(2)}) async-start(bf16[4,8,96,128]{3,2,1,0:T(8,128)(2,1)} %broadcast_in_dim.27), calls=%async_computation.1 | async-start | bytes 1572864 | tf_op jit(solution)/shard_map/all_to_all | solution.py:446
  42.9 20.4 %collective-permute-start.4 = (bf16[4,48,1536]{2,1,0:T(8,128)(2,1)S(1)}, bf16[4,48,1536]{2,1,0:T(8,128)(2,1)S(1)}, u32[]{:S(2)}, u32[]{:S(2)}) collective-permute-start(bf16[4,48,1536]{2,1,0:T(8,128)(2,1)S(1)} %pad_maximum_fusion.wo_ref), channel_id=1, source_target_pairs={{0,1},{1,0},{2,3},{3,2},{4,5},{5,4},{6,7},{7,6},{8,9},{9,8},{10,11... | collective-permute-start | bytes 1769480 | tf_op jit(solution)/shard_map/ppermute | solution.py:444
  44.8 18.5 %collective-permute-start.3 = (bf16[96,1536]{1,0:T(8,128)(2,1)S(1)}, bf16[96,1536]{1,0:T(8,128)(2,1)S(1)}, u32[]{:S(2)}, u32[]{:S(2)}) collective-permute-start(bf16[96,1536]{1,0:T(8,128)(2,1)S(1)} %copy-done.4), channel_id=1, source_target_pairs={{0,32},{32,0},{1,33},{33,1},{2,34},{34,2},{3,35},{35,3},{4,36},{36... | collective-permute-start | bytes 884744 | tf_op jit(solution)/shard_map/ppermute | solution.py:442
  48.8 17.7 %copy-start.1 = (s32[4]{0:T(128)}, s32[4]{0:T(128)S(1)}, u32[]{:S(2)}) copy-start(s32[4]{0:T(128)S(1)} %pad_add_fusion.info_ref) | copy-start | bytes 52
  63.3 7.2 %copy-start.5 = (bf16[96,1536]{1,0:T(8,128)(2,1)}, bf16[96,1536]{1,0:T(8,128)(2,1)S(1)}, u32[]{:S(2)}) copy-start(bf16[96,1536]{1,0:T(8,128)(2,1)S(1)} %collective-permute-done.3) | copy-start | bytes 884740
  63.3 3.2 %collective-permute-start.5 = (bf16[4,128,128]{2,1,0:T(8,128)(2,1)S(1)}, bf16[4,128,128]{2,1,0:T(8,128)(2,1)S(1)}, u32[]{:S(2)}, u32[]{:S(2)}) collective-permute-start(bf16[4,128,128]{2,1,0:T(8,128)(2,1)S(1)} %get-tuple-element.25), channel_id=1, source_target_pairs={{0,1},{1,0},{2,3},{3,2},{4,5},{5,4},{6,7},{7,6},{8,9},{9,8},{10,11... | collective-permute-start | bytes 393224 | tf_op jit(solution)/shard_map/ppermute | solution.py:450
  66.6 11.3 %copy-start.8 = (f32[1536]{0:T(1024)S(1)}, f32[1536]{0:T(1024)}, u32[]{:S(2)}) copy-start(f32[1536]{0:T(1024)} %param.19) | copy-start | bytes 18436
  66.6 27.6 %copy-start = (s32[1,1,1,64,8]{3,4,2,1,0:T(8,128)S(1)}, s32[1,1,1,64,8]{3,4,2,1,0:T(8,128)}, u32[]{:S(2)}) copy-start(s32[1,1,1,64,8]{3,4,2,1,0:T(8,128)} %param.16) | copy-start | bytes 6148
  66.6 27.6 %copy-start.2 = (bf16[1,1,1,64,1536]{4,3,2,1,0:T(8,128)(2,1)S(1)}, bf16[1,1,1,64,1536]{4,3,2,1,0:T(8,128)(2,1)}, u32[]{:S(2)}) copy-start(bf16[1,1,1,64,1536]{4,3,2,1,0:T(8,128)(2,1)} %param.11) | copy-start | bytes 589828
  70.5 23.7 %all-to-all-start.2 = ((bf16[4,64,1536]{2,1,0:T(8,128)(2,1)}), bf16[4,64,1536]{2,1,0:T(8,128)(2,1)S(1)}, u32[]{:S(2)}, u32[]{:S(2)}) async-start(bf16[4,64,1536]{2,1,0:T(8,128)(2,1)} %group_sums.1), calls=%async_computation.2 | async-start | bytes 1572864 | tf_op jit(solution)/shard_map/all_to_all | solution.py:452
  77.1 48.0 %all-gather.7.cloned.1.call-start = ((), (), s32[]{:S(2)}) async-start(), calls=%async_computation.6 | async-start | bytes 2654208 | tf_op jit(solution)/shard_map/all_gather | solution.py:449
  96.8 55.0 %all-to-all-start.3 = ((bf16[32,208,128]{2,1,0:T(8,128)(2,1)}), bf16[32,208,128]{2,1,0:T(8,128)(2,1)S(1)}, u32[]{:S(2)}, u32[]{:S(2)}) async-start(bf16[32,208,128]{2,1,0:T(8,128)(2,1)} %get-tuple-element.27), calls=%async_computation.3 | async-start | bytes 3407872 | tf_op jit(solution)/shard_map/all_to_all | solution.py:454
  151.7 1.2 copy-start.3
  162.5 48.0 %all-to-all-start.4 = ((bf16[32,208,128]{2,1,0:T(8,128)(2,1)}), bf16[32,208,128]{2,1,0:T(8,128)(2,1)S(1)}, u32[]{:S(2)}, u32[]{:S(2)}) async-start(bf16[32,208,128]{2,1,0:T(8,128)(2,1)} %expert.1), calls=%async_computation.4 | async-start | bytes 3407872 | tf_op jit(solution)/shard_map/all_to_all | solution.py:456
  167.5 5.0 %copy-start.9 = (f32[1,1,1,64,8]{3,4,2,1,0:T(8,128)S(1)}, f32[1,1,1,64,8]{3,4,2,1,0:T(8,128)}, u32[]{:S(2)}) copy-start(f32[1,1,1,64,8]{3,4,2,1,0:T(8,128)} %param.17) | copy-start | bytes 6148
  170.1 3.4 %collective-permute-start.6 = (bf16[4,8,96,32]{2,3,1,0:T(8,128)(2,1)S(1)}, bf16[4,8,96,32]{2,3,1,0:T(8,128)(2,1)S(1)}, u32[]{:S(2)}, u32[]{:S(2)}) collective-permute-start(bf16[4,8,96,32]{2,3,1,0:T(8,128)(2,1)S(1)} %copy.29), channel_id=1, source_target_pairs={{0,1},{1,0},{2,3},{3,2},{4,5},{5,4},{6,7},{7,6},{8,9},{9,8},{10,11... | collective-permute-start | bytes 589832 | tf_op jit(solution)/shard_map/ppermute | solution.py:462
  180.7 31.8 %copy-start.6 = (bf16[1,3072,32]{1,2,0:T(8,128)(2,1)}, bf16[1,3072,32]{1,2,0:T(8,128)(2,1)S(1)}, u32[]{:S(2)}) copy-start(bf16[1,3072,32]{1,2,0:T(8,128)(2,1)S(1)} %dynamic_update_slice.4) | copy-start | bytes 589828
Sparse Core Ops, SparseCore 0:
  11.1 47.5 all-gather.4
  80.0 45.0 all-gather.6

commit v7 on v6

--- a/solution.py
+++ b/solution.py
@@ -66,7 +66,7 @@
     )(queries, fresh, cache)
 
 
-def attention_kernel(info_ref, own_ref, pair_ref, keep_ref, send_ref, kv, sc, bias_c, bias_d):
+def attention_kernel(info_ref, own_ref, pair_ref, keep_ref, send_ref, kv, vals, keys, sc, probs, bias_c, bias_d):
     b = pl.program_id(0)
     length, core, x = info_ref[0], info_ref[1], info_ref[2]
 
@@ -76,67 +76,58 @@
             src = pair_ref.at[t // 2 % 4, t // 8 * 2 + t % 2]
             kv[t * 32 : t * 32 + 32, :] = src[0:32, :]
             kv[1024 + t * 64 : 1088 + t * 64, :] = src[32:96, :]
+        for t in range(6):
+            some = kv[t * 512 : t * 512 + 512, :].astype(F32)
+            vals[t * 512 : t * 512 + 512, :] = jnp.where(iota((512, 128), 1) < HD, 1.0, some).astype(BF)
+            keys[:, t * 512 : t * 512 + 512] = some.T.astype(BF)
         bias_c[...] = jnp.where(iota((8, 1024), 1) < length, 0.0, NEG)
         query_at = x * 128 + iota((128, 512), 0)
         bias_d[...] = jnp.where(iota((128, 512), 1) <= query_at, 0.0, NEG)
 
-    first = own_ref[pl.ds(b * 2, 2), 0:64, :].reshape(128, 128).astype(F32) * 0.125
-    last = own_ref[pl.ds(b * 2, 2), 64:96, :].reshape(64, 128).astype(F32) * 0.125
     low = iota((128, 128), 1) < HD
-    turned = pltpu.roll(last, HD, 1)
-    third = jnp.concatenate([last[0:32], turned[0:32], last[32:64], turned[32:64]], 0)
-    q = jnp.concatenate(
-        [
-            jnp.where(low, first, 0.0),
-            jnp.where(low, pltpu.roll(first, HD, 1), 0.0),
-            jnp.where(low, third, 0.0),
-        ],
-        0,
-    ).astype(BF)
-
-    def scores(k):
-        keys = kv[pl.ds(pl.multiple_of(k * 512, 512), 512), :]
-        return lax.dot_general(q, keys, (((1,), (1,)), ((), ())), preferred_element_type=F32)
-
-    def fold(fn, top, s):
-        for j in range(4):
-            top = fn(top, s[:, j * 128 : j * 128 + 128])
-        return top
-
-    top = jnp.full((384, 128), NEG, F32)
-    for k in range(2):
-        s = scores(k) + bias_c[0:1, k * 512 : k * 512 + 512]
-        sc[k] = s
-        top = fold(jnp.maximum, top, s)
-    s = scores(2 + b)
-    s = s + jnp.concatenate([bias_d[...]] * 3, 0)
-    sc[2 + b] = s
-    top = fold(jnp.maximum, top, s)
-
-    def middle(k, top):
-        s = scores(k)
-        sc[k] = s
-        return fold(jnp.maximum, top, s)
-
-    top = lax.fori_loop(2, 2 + b, middle, top)
-    highest = jnp.max(top, 1, keepdims=True)
-
-    def mix(k, carry):
-        total, acc = carry
-        p = jnp.exp(sc[k] - highest)
-        values = kv[pl.ds(pl.multiple_of(k * 512, 512), 512), :]
-        return fold(jnp.add, total, p), acc + dot(p.astype(BF), values)
-
-    zero = jnp.zeros((384, 128), F32)
-    total, acc = lax.fori_loop(0, 3 + b, mix, (zero, zero))
-    out = acc / jnp.sum(total, 1, keepdims=True)
-    a0, a1, a2 = out[0:128], out[128:256], out[256:384]
-    tiles = (jnp.where(low, pltpu.roll(a0, HD, 1), a1), jnp.where(low, pltpu.roll(a2, HD, 1), 0.0))
-    for n, tile in enumerate(tiles):
-        even, odd = tile[0:64], tile[64:128]
-        rows = slice(n * 64, n * 64 + 64)
-        keep_ref[b, rows, :] = jnp.where(core == 0, even, odd).astype(BF)
-        send_ref[b, rows, :] = jnp.where(core == 0, odd, even).astype(BF)
+
+    def block(b):
+        first = own_ref[b * 2 : b * 2 + 2, 0:64, :].reshape(128, 128).astype(F32) * 0.125
+        last = own_ref[b * 2 : b * 2 + 2, 64:96, :].reshape(64, 128).astype(F32) * 0.125
+        turned = pltpu.roll(last, HD, 1)
+        third = jnp.concatenate([last[0:32], turned[0:32], last[32:64], turned[32:64]], 0)
+        heads = (first, pltpu.roll(first, HD, 1), third)
+        q = jnp.concatenate([jnp.where(low, head, 0.0) for head in heads], 0).astype(BF)
+        count = 3 + b
+        top = jnp.full((384, 128), NEG, F32)
+        for k in range(count):
+            at = k * 512
+            s = dot(q, keys[:, at : at + 512])
+            if k < 2:
+                s = s + bias_c[0:1, at : at + 512]
+            elif k == count - 1:
+                s = s + jnp.concatenate([bias_d[...]] * 3, 0)
+            sc[k] = s
+            for j in range(4):
+                top = jnp.maximum(top, s[:, j * 128 : j * 128 + 128])
+        highest = jnp.max(top, 1, keepdims=True)
+        accs = []
+        for h in range(3):
+            rows = slice(h * 128, h * 128 + 128)
+            for k in range(count):
+                part = jnp.exp(sc[k, rows, :] - highest[rows])
+                probs[rows, k * 512 : k * 512 + 512] = part.astype(BF)
+            accs.append(dot(probs[rows, : count * 512], vals[: count * 512, :]))
+        acc = jnp.concatenate(accs, 0)
+        out = acc / pltpu.roll(acc, HD, 1)
+        a0, a1, a2 = out[0:128], out[128:256], out[256:384]
+        tiles = (
+            jnp.where(low, pltpu.roll(a0, HD, 1), a1),
+            jnp.where(low, pltpu.roll(a2, HD, 1), 0.0),
+        )
+        for n, tile in enumerate(tiles):
+            even, odd = tile[0:64], tile[64:128]
+            rows = slice(n * 64, n * 64 + 64)
+            keep_ref[b, rows, :] = jnp.where(core == 0, even, odd).astype(BF)
+            send_ref[b, rows, :] = jnp.where(core == 0, odd, even).astype(BF)
+
+    for n in range(4):
+        pl.when(b == n)(functools.partial(block, n))
 
 
 def attention(info, own, pairs):
@@ -149,7 +140,10 @@
         out_specs=(vmem(), vmem()),
         scratch_shapes=[
             pltpu.VMEM((3072, 128), BF),
+            pltpu.VMEM((3072, 128), BF),
+            pltpu.VMEM((128, 3072), BF),
             pltpu.VMEM((6, 384, 512), F32),
+            pltpu.VMEM((384, 3072), BF),
             pltpu.VMEM((8, 1024), F32),
             pltpu.VMEM((128, 512), F32),
         ],
@@ -285,41 +279,55 @@
     return [stacked[c * NT : (c + 1) * NT, :] for c in range(CH)]
 
 
-def expert_kernel(info_ref, in_ref, wo_ref, wx_ref, o_ref, x, w1, w2, o, sems, out_sems):
+def unpack_kernel(info_ref, wo_ref, wx_ref, w1_ref, w2_ref):
     zlo = info_ref[3]
-    copies = []
     for d in range(2 * wo_ref.shape[0]):
-        w_ref, block = (wo_ref, zlo) if d % 2 == 0 else (wx_ref, 1 - zlo)
+        src, block = (wo_ref, zlo) if d % 2 == 0 else (wx_ref, 1 - zlo)
         block = block + d // 2 * 2
         top = pl.multiple_of(block * 96, 32)
-        pieces = (
-            (w_ref.at[d // 2, 0:64, 0:1024], w1.at[pl.ds(top, 64), :]),
-            (w_ref.at[d // 2, 0:32, 1024:1536], w1.at[pl.ds(top + 64, 32), 0:512]),
-            (w_ref.at[d // 2, 32:64, 1024:1536], w1.at[pl.ds(top + 64, 32), 512:1024]),
-            (w_ref.at[d // 2, 64:96, :], w2.at[pl.ds(pl.multiple_of(block * 32, 32), 32), :]),
+        w1_ref[pl.ds(top, 64), :] = src[d // 2, 0:64, 0:1024]
+        w1_ref[pl.ds(top + 64, 32), 0:512] = src[d // 2, 0:32, 1024:1536]
+        w1_ref[pl.ds(top + 64, 32), 512:1024] = src[d // 2, 32:64, 1024:1536]
+        w2_ref[pl.ds(pl.multiple_of(block * 32, 32), 32), :] = src[d // 2, 64:96, :]
+
+
+def unpack(info, own_weights, other_weights):
+    blocks = 2 * own_weights.shape[0]
+    return pl.pallas_call(
+        unpack_kernel,
+        out_shape=(
+            jax.ShapeDtypeStruct((blocks * 96, 2 * FFE), BF),
+            jax.ShapeDtypeStruct((blocks * 32, D), BF),
+        ),
+        in_specs=[pl.BlockSpec(memory_space=pltpu.SMEM), vmem(), vmem()],
+        out_specs=(vmem(), vmem()),
+        compiler_params=params(20),
+        interpret=INTERPRET,
+        name="unpack",
+    )(info, own_weights, other_weights)
+
+
+def expert_kernel(in_ref, up_ref, down_ref, o_ref, x, w1, w2, o, sems, out_sems):
+    loads = [
+        pltpu.make_async_copy(src.at[rows, :], dst.at[rows, :], sems.at[n])
+        for n, (src, dst, rows) in enumerate(
+            ((up_ref, w1, pl.ds(0, 768)), (up_ref, w1, pl.ds(768, 768)), (down_ref, w2, pl.ds(0, FFE)))
         )
-        for n, (src, dst) in enumerate(pieces):
-            copies.append(pltpu.make_async_copy(src, dst, sems.at[d, n]))
-    firsts = [copy for i, copy in enumerate(copies) if i % 4 < 3]
-    lasts = copies[3::4]
-    for copy in firsts + lasts:
+    ]
+    for copy in loads:
         copy.start()
-    depth = w1.shape[0] // 4
     for c in range(CH):
         x[0:512, c * 128 : c * 128 + 128] = in_ref[:, c * SLOT : (c + 1) * SLOT, :].reshape(512, 128)
     chunks = gather_extra(in_ref[:, SLOT * CH : SROWS, :].reshape(512, 128))
     for c in range(CH):
         x[512:544, c * 128 : c * 128 + 128] = chunks[c]
-    hidden = jnp.zeros((544, 2 * FFE), F32)
-    for n in range(4):
-        for copy in firsts[n * len(firsts) // 4 : (n + 1) * len(firsts) // 4]:
-            copy.wait()
-        at = n * depth
-        hidden = hidden + dot(x[:, at : at + depth], w1[at : at + depth, :])
+    loads[0].wait()
+    hidden = dot(x[:, 0:768], w1[0:768, :])
+    loads[1].wait()
+    hidden = hidden + dot(x[:, 768:1536], w1[768:1536, :])
     gate = hidden[:, :FFE]
     active = (gate / (1.0 + jnp.exp(-gate)) * hidden[:, FFE:]).astype(BF)
-    for copy in lasts:
-        copy.wait()
+    loads[2].wait()
     place = iota((512, NT), 0)
     owner = place // 16 == iota((512, NT), 1)
     extra = jnp.zeros((512, 128), F32)
@@ -342,20 +350,18 @@
         copy.wait()
 
 
-def expert(info, slots, own_weights, other_weights):
-    blocks = 2 * own_weights.shape[0]
+def expert(slots, up, down):
     return pl.pallas_call(
         expert_kernel,
         out_shape=jax.ShapeDtypeStruct((NT, SROWS, 128), BF),
-        in_specs=[pl.BlockSpec(memory_space=pltpu.SMEM), vmem()]
-        + [pl.BlockSpec(memory_space=pltpu.HBM)] * 2,
+        in_specs=[vmem()] + [pl.BlockSpec(memory_space=pltpu.HBM)] * 2,
         out_specs=pl.BlockSpec(memory_space=pltpu.HBM),
         scratch_shapes=[
             pltpu.VMEM((544, D), BF),
-            pltpu.VMEM((blocks * 96, 2 * FFE), BF),
-            pltpu.VMEM((blocks * 32, D), BF),
+            pltpu.VMEM(up.shape, BF),
+            pltpu.VMEM(down.shape, BF),
             pltpu.VMEM((NT, SROWS, 128), BF),
-            pltpu.SemaphoreType.DMA((blocks, 4)),
+            pltpu.SemaphoreType.DMA((3,)),
             pltpu.SemaphoreType.DMA((CH // 2 + 1,)),
         ],
         compiler_params=params(58),
@@ -364,7 +370,7 @@
         ),
         interpret=INTERPRET,
         name="expert",
-    )(info, slots, own_weights, other_weights)
+    )(slots, up, down)
 
 
 def combine_kernel(in_ref, res_ref, ids_ref, gate_ref, o_ref):
@@ -433,12 +439,12 @@
 
     send = pack(rotated_queries[0, 0, 0], fresh_key_values[0, 0, 0], cached_key_values[0])
     packed, shard = prepare(gate_up[0], down_weight[0], output_weight, send)
-    own_weights = lax.all_gather(packed, "y", axis=0)
     turns = [
         lax.ppermute(shard, "x", [(n, (n + step) % 4) for n in range(4)]) for step in (1, 2, 3)
     ]
     own = lax.all_to_all(send, ("zhi", "core"), split_axis=0, concat_axis=0, tiled=True)
     turns, packed, own = lax.optimization_barrier((turns, packed, own))
+    own_weights = lax.all_gather(packed, "y", axis=0)
     across = lax.ppermute(packed, "zlo", [(0, 1), (1, 0)])
     own_rows = jnp.stack([shard, *turns], 0)
     other_rows = lax.ppermute(own_rows, "core", [(0, 1), (1, 0)])
@@ -452,7 +458,7 @@
     sums = lax.all_to_all(terms, "zhi", split_axis=0, concat_axis=0, tiled=True)
     residual, outbound = norm_dispatch(sums, hidden_in[0, 0, 0], norm_gain[None], ids.T)
     slots = lax.all_to_all(outbound, TEN, split_axis=0, concat_axis=0, tiled=True)
-    computed = expert(info, slots, own_weights, other_weights)
+    computed = expert(slots, *unpack(info, own_weights, other_weights))
     returned = lax.all_to_all(computed, TEN, split_axis=0, concat_axis=0, tiled=True)
     hidden_out = combine(returned, residual, ids, gates)
 

time: 220 us -> 214 us (0.973)
  the two profiles are of different devices: /device:TPU:60 before, /device:TPU:36 now
where the time goes in v7:
time: 214 us; the launch traced here: 213 us
  waiting for transfers between devices  94.8 us (44%)
  starting transfers between devices  57.3 us (27%)
  Pallas kernels  28.3 us (13%)
  between operations  15 us (7%)
  local copies, waits for them, and re-layouts  14.7 us (7%)
  other arithmetic  2.56 us (1%)
    all_to_all x1, waiting for transfers between devices, shards(): lax.all_to_all(computed, TEN, split_axis=0, concat_axis=0, tiled=True)  29.8 us
    all_gather x1, waiting for transfers between devices, shards(): other_weights = lax.all_gather(across, 'y', axis=0)  20.3 us
    all_to_all x1, waiting for transfers between devices, shards(): sums = lax.all_to_all(terms, 'zhi', split_axis=0, concat_axis=0, tiled=True)  16.3 us
    all_to_all x1, waiting for transfers between devices, shards(): lax.all_to_all(outbound, TEN, split_axis=0, concat_axis=0, tiled=True)  15.6 us
    all_to_all x1, starting transfers between devices, shards(): lax.all_to_all(outbound, TEN, split_axis=0, concat_axis=0, tiled=True)  12 us
    all_to_all x1, starting transfers between devices, shards(): lax.all_to_all(send, ('zhi', 'core'), split_axis=0, concat_axis=0, tiled=...  10.3 us
    ppermute x3, starting transfers between devices, shards(): lax.ppermute(shard, 'x', [(n, (n + step) % 4) for n in range(4)])  8.98 us
    pallas_call x1, Pallas kernels, expert(): pl.pallas_call(expert_kernel, out_shape=jax.ShapeDtypeStruct((NT, SROWS,...  8.31 us
  transfers between devices with their start and end apart: 14, of which 9 were waited for; matrix products, arithmetic and copies ran while one was open for 5% of the time, Pallas kernels for 8%

profile of v7, /device:TPU:36, one launch (start us, length us, event | category | flops | bytes accessed | tf_op | source)
XLA Modules:
  0.0 212.6 jit_solution(9521327207892688165)
XLA Ops:
  9.0 10.3 %all-to-all-start = ((bf16[8,192,128]{2,1,0:T(8,128)(2,1)}), bf16[8,192,128]{2,1,0:T(8,128)(2,1)S(1)}, u32[]{:S(2)}, u32[]{:S(2)}) async-start(bf16[8,192,128]{2,1,0:T(8,128)(2,1)} %pack.1.after_ref), calls=%async_computation | async-start | bytes 786432 | tf_op jit(solution)/shard_map/all_to_all | solution.py:445
  21.2 3.2 %collective-permute-start = (bf16[48,1536]{1,0:T(8,128)(2,1)}, bf16[48,1536]{1,0:T(8,128)(2,1)S(1)}, u32[]{:S(2)}, u32[]{:S(2)}) collective-permute-start(bf16[48,1536]{1,0:T(8,128)(2,1)} %get-tuple-element.18), channel_id=1, source_target_pairs={{0,2},{2,4},{4,6},{6,0},{1,3},{3,5},{5,7},{7,1},{8,10},{10,12},{12... | collective-permute-start | bytes 442376 | tf_op jit(solution)/shard_map/ppermute | solution.py:443
  24.5 2.7 %collective-permute-start.1 = (bf16[48,1536]{1,0:T(8,128)(2,1)}, bf16[48,1536]{1,0:T(8,128)(2,1)S(1)}, u32[]{:S(2)}, u32[]{:S(2)}) collective-permute-start(bf16[48,1536]{1,0:T(8,128)(2,1)} %get-tuple-element.18), channel_id=1, source_target_pairs={{0,4},{2,6},{4,0},{6,2},{1,5},{3,7},{5,1},{7,3},{8,12},{10,14},{12... | collective-permute-start | bytes 442376 | tf_op jit(solution)/shard_map/ppermute | solution.py:443
  27.2 3.0 %collective-permute-start.2 = (bf16[48,1536]{1,0:T(8,128)(2,1)}, bf16[48,1536]{1,0:T(8,128)(2,1)S(1)}, u32[]{:S(2)}, u32[]{:S(2)}) collective-permute-start(bf16[48,1536]{1,0:T(8,128)(2,1)} %get-tuple-element.18), channel_id=1, source_target_pairs={{0,6},{2,0},{4,2},{6,4},{1,7},{3,1},{5,3},{7,5},{8,14},{10,8},{12,... | collective-permute-start | bytes 442376 | tf_op jit(solution)/shard_map/ppermute | solution.py:443
  30.2 3.8 %collective-permute-done.1 = bf16[48,1536]{1,0:T(8,128)(2,1)S(1)} collective-permute-done((bf16[48,1536]{1,0:T(8,128)(2,1)}, bf16[48,1536]{1,0:T(8,128)(2,1)S(1)}, u32[]{:S(2)}, u32[]{:S(2)}) %collective-permute-start.1) | collective-permute-done | bytes 147488 | tf_op jit(solution)/shard_map/ppermute | solution.py:443
  34.0 2.5 %collective-permute-done.2 = bf16[48,1536]{1,0:T(8,128)(2,1)S(1)} collective-permute-done((bf16[48,1536]{1,0:T(8,128)(2,1)}, bf16[48,1536]{1,0:T(8,128)(2,1)S(1)}, u32[]{:S(2)}, u32[]{:S(2)}) %collective-permute-start.2) | collective-permute-done | bytes 147488 | tf_op jit(solution)/shard_map/ppermute | solution.py:443
  37.6 5.0 %all-to-all-start.1 = ((bf16[4,8,96,128]{3,2,1,0:T(8,128)(2,1)}), bf16[4,8,96,128]{3,2,1,0:T(8,128)(2,1)S(1)}, u32[]{:S(2)}, u32[]{:S(2)}) async-start(bf16[4,8,96,128]{3,2,1,0:T(8,128)(2,1)} %broadcast_in_dim.27), calls=%async_computation.1 | async-start | bytes 1572864 | tf_op jit(solution)/shard_map/all_to_all | solution.py:452
  42.7 1.9 collective-permute-start.4
  44.7 3.4 %collective-permute-start.3 = (bf16[96,1536]{1,0:T(8,128)(2,1)S(1)}, bf16[96,1536]{1,0:T(8,128)(2,1)S(1)}, u32[]{:S(2)}, u32[]{:S(2)}) collective-permute-start(bf16[96,1536]{1,0:T(8,128)(2,1)S(1)} %copy-done.6), channel_id=1, source_target_pairs={{0,32},{32,0},{1,33},{33,1},{2,34},{34,2},{3,35},{35,3},{4,36},{36... | collective-permute-start | bytes 884744 | tf_op jit(solution)/shard_map/ppermute | solution.py:448
  48.8 3.2 %all-to-all-done.1.pair_ref = bf16[4,8,96,128]{3,2,1,0:T(8,128)(2,1)S(1)} async-done(((bf16[4,8,96,128]{3,2,1,0:T(8,128)(2,1)}), bf16[4,8,96,128]{3,2,1,0:T(8,128)(2,1)S(1)}, u32[]{:S(2)}, u32[]{:S(2)}) %all-to-all-start.1) | async-done | bytes 786464 | tf_op jit(solution)/shard_map/all_to_all | solution.py:452
  52.0 6.9 %attention.1 = (bf16[4,128,128]{2,1,0:T(8,128)(2,1)S(1)}, bf16[4,128,128]{2,1,0:T(8,128)(2,1)S(1)}) custom-call(s32[4]{0:T(128)S(1)} %pad_add_fusion.info_ref, bf16[8,192,128]{2,1,0:T(8,128)(2,1)S(1)} %all-to-all-done.own_ref, bf16[4,8,96,128]{3,2,1,0:T(8,128)(2,1)S(1)} %all-to-all-done.1.pair_ref), custom_call_target="tpu_custom_call" | custom-call | flops 1811939328 | bytes 3145728 | tf_op jit(solution)/shard_map/attention/pallas_call | solution.py:135
  62.2 3.9 %group_sums.1 = bf16[4,64,1536]{2,1,0:T(8,128)(2,1)} custom-call(s32[4]{0:T(128)S(1)} %pad_add_fusion.info_ref, bf16[4,128,128]{2,1,0:T(8,128)(2,1)S(1)} %get-tuple-element.21.own_ref, bf16[4,128,128]{2,1,0:T(8,128)(2,1)S(1)} %collective-permute-done.5.oth_ref, bf16[4,48,1536]{2,1,0:T(8,128)(2,1)S(1)} %pad_maximum_fusion.wo_ref, ...), custom_call_target="tpu_custom_call" | custom-call | flops 301989888 | bytes 2097152 | tf_op jit(solution)/shard_map/group_sums/pallas_call | solution.py:190
  66.1 6.7 %all-to-all-start.2 = ((bf16[4,64,1536]{2,1,0:T(8,128)(2,1)}), bf16[4,64,1536]{2,1,0:T(8,128)(2,1)S(1)}, u32[]{:S(2)}, u32[]{:S(2)}) async-start(bf16[4,64,1536]{2,1,0:T(8,128)(2,1)} %group_sums.1), calls=%async_computation.2 | async-start | bytes 1572864 | tf_op jit(solution)/shard_map/all_to_all | solution.py:458
  73.5 16.3 %all-to-all-done.2.sum_ref = bf16[4,64,1536]{2,1,0:T(8,128)(2,1)S(1)} async-done(((bf16[4,64,1536]{2,1,0:T(8,128)(2,1)}), bf16[4,64,1536]{2,1,0:T(8,128)(2,1)S(1)}, u32[]{:S(2)}, u32[]{:S(2)}) %all-to-all-start.2) | async-done | bytes 786464 | tf_op jit(solution)/shard_map/all_to_all | solution.py:458
  89.9 2.6 %norm_dispatch.1 = (f32[64,1536]{1,0:T(8,128)S(1)}, bf16[32,208,128]{2,1,0:T(8,128)(2,1)}) custom-call(bf16[4,64,1536]{2,1,0:T(8,128)(2,1)S(1)} %all-to-all-done.2.sum_ref, bf16[64,1536]{1,0:T(8,128)(2,1)S(1)} %bitcast.41, f32[1,1536]{1,0:T(1,128)S(1)} %broadcast_in_dim.28.gain_ref, s32[8,64]{1,0:T(8,128)S(1)} %bitcast.40), custom_call_target="tpu_custom_call" | custom-call | flops 1073741824 | bytes 4194304 | tf_op jit(solution)/shard_map/norm_dispatch/pallas_call | solution.py:259
  92.4 12.0 %all-to-all-start.3 = ((bf16[32,208,128]{2,1,0:T(8,128)(2,1)}), bf16[32,208,128]{2,1,0:T(8,128)(2,1)}, u32[]{:S(2)}, u32[]{:S(2)}) async-start(bf16[32,208,128]{2,1,0:T(8,128)(2,1)} %get-tuple-element.29), calls=%async_computation.3 | async-start | bytes 3407872 | tf_op jit(solution)/shard_map/all_to_all | solution.py:460
  104.5 20.3 %all-gather.7.cloned.1.call-done = bf16[768,1536]{1,0:T(8,128)(2,1)} async-done(((bf16[96,1536]{1,0:T(8,128)(2,1)}), bf16[768,1536]{1,0:T(8,128)(2,1)}) %all-gather.7.cloned.1.call-update) | async-done | bytes 2359312 | tf_op jit(solution)/shard_map/all_gather | solution.py:455
  131.9 15.6 %all-to-all-done.3.in_ref = bf16[32,208,128]{2,1,0:T(8,128)(2,1)} async-done(((bf16[32,208,128]{2,1,0:T(8,128)(2,1)}), bf16[32,208,128]{2,1,0:T(8,128)(2,1)}, u32[]{:S(2)}, u32[]{:S(2)}) %all-to-all-start.3) | async-done | bytes 1703968 | tf_op jit(solution)/shard_map/all_to_all | solution.py:460
  147.5 8.3 %expert.1 = bf16[32,208,128]{2,1,0:T(8,128)(2,1)} custom-call(bf16[32,208,128]{2,1,0:T(8,128)(2,1)} %all-to-all-done.3.in_ref, bf16[1536,1024]{1,0:T(8,128)(2,1)} %copy-done.3, bf16[512,1536]{1,0:T(8,128)(2,1)} %copy-done.4), custom_call_target="tpu_custom_call" | custom-call | flops 2566914048 | bytes 9437184 | tf_op jit(solution)/shard_map/expert/pallas_call | solution.py:354
  155.8 5.0 %all-to-all-start.4 = ((bf16[32,208,128]{2,1,0:T(8,128)(2,1)}), bf16[32,208,128]{2,1,0:T(8,128)(2,1)S(1)}, u32[]{:S(2)}, u32[]{:S(2)}) async-start(bf16[32,208,128]{2,1,0:T(8,128)(2,1)} %expert.1), calls=%async_computation.4 | async-start | bytes 3407872 | tf_op jit(solution)/shard_map/all_to_all | solution.py:462
  163.4 2.1 collective-permute-start.6
  168.0 2.4 %dynamic-slice_select_fusion = bf16[4,8,96,32]{3,2,1,0:T(8,128)(2,1)} fusion(bf16[4,8,96,32]{3,2,1,0:T(8,128)(2,1)} %copy.30, bf16[4,8,96,128]{3,2,1,0:T(8,128)(2,1)S(1)} %all-to-all-done.1.pair_ref, s32[]{:T(128)S(6)} %select_n.35, pred[]{:T(512)S(6)} %eq.5), kind=kLoop, calls=%fused_computation | loop fusion | flops 98304 | bytes 589829 | tf_op jit(solution)/shard_map/jit(_where)/select_n | solution.py:469
  174.0 29.8 %all-to-all-done.4.in_ref = bf16[32,208,128]{2,1,0:T(8,128)(2,1)S(1)} async-done(((bf16[32,208,128]{2,1,0:T(8,128)(2,1)}), bf16[32,208,128]{2,1,0:T(8,128)(2,1)S(1)}, u32[]{:S(2)}, u32[]{:S(2)}) %all-to-all-start.4) | async-done | bytes 1703968 | tf_op jit(solution)/shard_map/all_to_all | solution.py:462
  203.8 2.0 combine.1
  (58 shorter events, 24.7 us)
Async XLA Ops:
  9.0 27.5 %all-to-all-start = ((bf16[8,192,128]{2,1,0:T(8,128)(2,1)}), bf16[8,192,128]{2,1,0:T(8,128)(2,1)S(1)}, u32[]{:S(2)}, u32[]{:S(2)}) async-start(bf16[8,192,128]{2,1,0:T(8,128)(2,1)} %pack.1.after_ref), calls=%async_computation | async-start | bytes 786432 | tf_op jit(solution)/shard_map/all_to_all | solution.py:445
  19.3 85.1 %all-gather.5.cloned.1.call-start = ((), (), s32[]{:S(2)}) async-start(), calls=%async_computation.5 | async-start | bytes 2654208 | tf_op jit(solution)/shard_map/all_gather | solution.py:447
  21.2 21.4 %copy-start.9 = (bf16[48,1536]{1,0:T(8,128)(2,1)S(1)}, bf16[48,1536]{1,0:T(8,128)(2,1)}, u32[]{:S(2)}) copy-start(bf16[48,1536]{1,0:T(8,128)(2,1)} %get-tuple-element.18) | copy-start | bytes 442372
  21.2 9.0 %collective-permute-start = (bf16[48,1536]{1,0:T(8,128)(2,1)}, bf16[48,1536]{1,0:T(8,128)(2,1)S(1)}, u32[]{:S(2)}, u32[]{:S(2)}) collective-permute-start(bf16[48,1536]{1,0:T(8,128)(2,1)} %get-tuple-element.18), channel_id=1, source_target_pairs={{0,2},{2,4},{4,6},{6,0},{1,3},{3,5},{5,7},{7,1},{8,10},{10,12},{12... | collective-permute-start | bytes 442376 | tf_op jit(solution)/shard_map/ppermute | solution.py:443
  24.5 9.5 %collective-permute-start.1 = (bf16[48,1536]{1,0:T(8,128)(2,1)}, bf16[48,1536]{1,0:T(8,128)(2,1)S(1)}, u32[]{:S(2)}, u32[]{:S(2)}) collective-permute-start(bf16[48,1536]{1,0:T(8,128)(2,1)} %get-tuple-element.18), channel_id=1, source_target_pairs={{0,4},{2,6},{4,0},{6,2},{1,5},{3,7},{5,1},{7,3},{8,12},{10,14},{12... | collective-permute-start | bytes 442376 | tf_op jit(solution)/shard_map/ppermute | solution.py:443
  27.2 9.4 %collective-permute-start.2 = (bf16[48,1536]{1,0:T(8,128)(2,1)}, bf16[48,1536]{1,0:T(8,128)(2,1)S(1)}, u32[]{:S(2)}, u32[]{:S(2)}) collective-permute-start(bf16[48,1536]{1,0:T(8,128)(2,1)} %get-tuple-element.18), channel_id=1, source_target_pairs={{0,6},{2,0},{4,2},{6,4},{1,7},{3,1},{5,3},{7,5},{8,14},{10,8},{12,... | collective-permute-start | bytes 442376 | tf_op jit(solution)/shard_map/ppermute | solution.py:443
  36.6 8.1 %copy-start.6 = (bf16[96,1536]{1,0:T(8,128)(2,1)S(1)}, bf16[96,1536]{1,0:T(8,128)(2,1)}, u32[]{:S(2)}) copy-start(bf16[96,1536]{1,0:T(8,128)(2,1)} %get-tuple-element.22) | copy-start | bytes 884740
  37.6 14.4 %all-to-all-start.1 = ((bf16[4,8,96,128]{3,2,1,0:T(8,128)(2,1)}), bf16[4,8,96,128]{3,2,1,0:T(8,128)(2,1)S(1)}, u32[]{:S(2)}, u32[]{:S(2)}) async-start(bf16[4,8,96,128]{3,2,1,0:T(8,128)(2,1)} %broadcast_in_dim.27), calls=%async_computation.1 | async-start | bytes 1572864 | tf_op jit(solution)/shard_map/all_to_all | solution.py:452
  42.7 16.2 %collective-permute-start.4 = (bf16[4,48,1536]{2,1,0:T(8,128)(2,1)S(1)}, bf16[4,48,1536]{2,1,0:T(8,128)(2,1)S(1)}, u32[]{:S(2)}, u32[]{:S(2)}) collective-permute-start(bf16[4,48,1536]{2,1,0:T(8,128)(2,1)S(1)} %pad_maximum_fusion.wo_ref), channel_id=1, source_target_pairs={{0,1},{1,0},{2,3},{3,2},{4,5},{5,4},{6,7},{7,6},{8,9},{9,8},{10,11... | collective-permute-start | bytes 1769480 | tf_op jit(solution)/shard_map/ppermute | solution.py:450
  44.7 14.3 %collective-permute-start.3 = (bf16[96,1536]{1,0:T(8,128)(2,1)S(1)}, bf16[96,1536]{1,0:T(8,128)(2,1)S(1)}, u32[]{:S(2)}, u32[]{:S(2)}) collective-permute-start(bf16[96,1536]{1,0:T(8,128)(2,1)S(1)} %copy-done.6), channel_id=1, source_target_pairs={{0,32},{32,0},{1,33},{33,1},{2,34},{34,2},{3,35},{35,3},{4,36},{36... | collective-permute-start | bytes 884744 | tf_op jit(solution)/shard_map/ppermute | solution.py:448
  58.9 7.2 %copy-start.7 = (bf16[96,1536]{1,0:T(8,128)(2,1)}, bf16[96,1536]{1,0:T(8,128)(2,1)S(1)}, u32[]{:S(2)}) copy-start(bf16[96,1536]{1,0:T(8,128)(2,1)S(1)} %collective-permute-done.3) | copy-start | bytes 884740
  59.0 3.2 %collective-permute-start.5 = (bf16[4,128,128]{2,1,0:T(8,128)(2,1)S(1)}, bf16[4,128,128]{2,1,0:T(8,128)(2,1)S(1)}, u32[]{:S(2)}, u32[]{:S(2)}) collective-permute-start(bf16[4,128,128]{2,1,0:T(8,128)(2,1)S(1)} %get-tuple-element.27), channel_id=1, source_target_pairs={{0,1},{1,0},{2,3},{3,2},{4,5},{5,4},{6,7},{7,6},{8,9},{9,8},{10,11... | collective-permute-start | bytes 393224 | tf_op jit(solution)/shard_map/ppermute | solution.py:456
  62.2 11.3 %copy-start.10 = (f32[1536]{0:T(1024)S(1)}, f32[1536]{0:T(1024)}, u32[]{:S(2)}) copy-start(f32[1536]{0:T(1024)} %param.19) | copy-start | bytes 18436
  62.2 27.6 %copy-start.2 = (s32[1,1,1,64,8]{3,4,2,1,0:T(8,128)S(1)}, s32[1,1,1,64,8]{3,4,2,1,0:T(8,128)}, u32[]{:S(2)}) copy-start(s32[1,1,1,64,8]{3,4,2,1,0:T(8,128)} %param.16) | copy-start | bytes 6148
  62.2 27.7 %copy-start.5 = (bf16[1,1,1,64,1536]{4,3,2,1,0:T(8,128)(2,1)S(1)}, bf16[1,1,1,64,1536]{4,3,2,1,0:T(8,128)(2,1)}, u32[]{:S(2)}) copy-start(bf16[1,1,1,64,1536]{4,3,2,1,0:T(8,128)(2,1)} %param.11) | copy-start | bytes 589828
  66.1 23.7 %all-to-all-start.2 = ((bf16[4,64,1536]{2,1,0:T(8,128)(2,1)}), bf16[4,64,1536]{2,1,0:T(8,128)(2,1)S(1)}, u32[]{:S(2)}, u32[]{:S(2)}) async-start(bf16[4,64,1536]{2,1,0:T(8,128)(2,1)} %group_sums.1), calls=%async_computation.2 | async-start | bytes 1572864 | tf_op jit(solution)/shard_map/all_to_all | solution.py:458
  72.8 52.0 %all-gather.7.cloned.1.call-start = ((), (), s32[]{:S(2)}) async-start(), calls=%async_computation.6 | async-start | bytes 2654208 | tf_op jit(solution)/shard_map/all_gather | solution.py:455
  92.4 55.0 %all-to-all-start.3 = ((bf16[32,208,128]{2,1,0:T(8,128)(2,1)}), bf16[32,208,128]{2,1,0:T(8,128)(2,1)}, u32[]{:S(2)}, u32[]{:S(2)}) async-start(bf16[32,208,128]{2,1,0:T(8,128)(2,1)} %get-tuple-element.29), calls=%async_computation.3 | async-start | bytes 3407872 | tf_op jit(solution)/shard_map/all_to_all | solution.py:460
  124.8 1.7 copy-start
  126.5 1.7 copy-start.1
  155.8 48.0 %all-to-all-start.4 = ((bf16[32,208,128]{2,1,0:T(8,128)(2,1)}), bf16[32,208,128]{2,1,0:T(8,128)(2,1)S(1)}, u32[]{:S(2)}, u32[]{:S(2)}) async-start(bf16[32,208,128]{2,1,0:T(8,128)(2,1)} %expert.1), calls=%async_computation.4 | async-start | bytes 3407872 | tf_op jit(solution)/shard_map/all_to_all | solution.py:462
  160.8 4.8 %copy-start.11 = (f32[1,1,1,64,8]{3,4,2,1,0:T(8,128)S(1)}, f32[1,1,1,64,8]{3,4,2,1,0:T(8,128)}, u32[]{:S(2)}) copy-start(f32[1,1,1,64,8]{3,4,2,1,0:T(8,128)} %param.17) | copy-start | bytes 6148
  163.4 3.4 %collective-permute-start.6 = (bf16[4,8,96,32]{2,3,1,0:T(8,128)(2,1)S(1)}, bf16[4,8,96,32]{2,3,1,0:T(8,128)(2,1)S(1)}, u32[]{:S(2)}, u32[]{:S(2)}) collective-permute-start(bf16[4,8,96,32]{2,3,1,0:T(8,128)(2,1)S(1)} %copy.29), channel_id=1, source_target_pairs={{0,1},{1,0},{2,3},{3,2},{4,5},{5,4},{6,7},{7,6},{8,9},{9,8},{10,11... | collective-permute-start | bytes 589832 | tf_op jit(solution)/shard_map/ppermute | solution.py:468
  174.0 31.8 %copy-start.8 = (bf16[1,3072,32]{1,2,0:T(8,128)(2,1)}, bf16[1,3072,32]{1,2,0:T(8,128)(2,1)S(1)}, u32[]{:S(2)}) copy-start(bf16[1,3072,32]{1,2,0:T(8,128)(2,1)S(1)} %dynamic_update_slice.4) | copy-start | bytes 589828
  (2 other events, 2.8 us)
Sparse Core Ops, SparseCore 0:
  36.7 42.8 all-gather.4
  81.7 43.0 all-gather.6

commit v8 on v7

--- a/solution.py
+++ b/solution.py
@@ -156,20 +156,11 @@
     )(info, own, pairs)
 
 
-def group_sums_kernel(info_ref, own_ref, oth_ref, wo_ref, wx_ref, o_ref, w, o, sems, out_sems):
-    core, x = info_ref[1], info_ref[2]
-    copies = []
-    for at in range(4):
-        turn = (x + 4 - at) % 4
-        for n, (src, side) in enumerate(((wo_ref, core), (wx_ref, 1 - core))):
-            row = pl.multiple_of((2 * at + side) * 48, 16)
-            copies.append(pltpu.make_async_copy(src.at[turn], w.at[pl.ds(row, 48), :], sems.at[at, n]))
-            copies[-1].start()
+def group_sums_kernel(info_ref, own_ref, oth_ref, w, o_ref, o, out_sems):
+    core = info_ref[1]
     sides = ((own_ref, core), (oth_ref, 1 - core))
     pairs = [src[:, 0:64, :].reshape(256, 128) for src, _ in sides]
     lasts = [src[:, 64:128, :].reshape(256, 128)[:, :HD] for src, _ in sides]
-    for copy in copies:
-        copy.wait()
     sent = []
     for n in range(3):
         cols = pl.ds(n * 512, 512)
@@ -185,44 +176,40 @@
         copy.wait()
 
 
-def group_sums(info, own, other, own_weight, other_weight):
-    anywhere = pl.BlockSpec(memory_space=pl.ANY)
+def group_sums(info, own, other, weight):
     return pl.pallas_call(
         group_sums_kernel,
         out_shape=jax.ShapeDtypeStruct((4, TOK, D), BF),
-        in_specs=[pl.BlockSpec(memory_space=pltpu.SMEM), vmem(), vmem(), anywhere, anywhere],
+        in_specs=[pl.BlockSpec(memory_space=pltpu.SMEM)] + [vmem()] * 3,
         out_specs=pl.BlockSpec(memory_space=pltpu.HBM),
         scratch_shapes=[
-            pltpu.VMEM((384, D), BF),
             pltpu.VMEM((4, TOK, D), BF),
-            pltpu.SemaphoreType.DMA((4, 2)),
             pltpu.SemaphoreType.DMA((3,)),
         ],
         compiler_params=params(20),
         cost_estimate=pl.CostEstimate(flops=2 * 256 * 384 * D, bytes_accessed=2 << 20, transcendentals=0),
         interpret=INTERPRET,
         name="group_sums",
-    )(info, own, other, own_weight, other_weight)
-
-
-def prepare_kernel(up_ref, down_ref, shard_ref, after_ref, o_ref, so_ref):
+    )(info, own, other, weight)
+
+
+def prepare_kernel(up_ref, down_ref, after_ref, o_ref):
     o_ref[0:64, 0:1024] = up_ref[0:64, :]
     o_ref[0:32, 1024:1536] = up_ref[64:96, 0:512]
     o_ref[32:64, 1024:1536] = up_ref[64:96, 512:1024]
     o_ref[64:96, :] = down_ref[...]
-    so_ref[...] = shard_ref[...]
-
-
-def prepare(up, down, shard, after):
+
+
+def prepare(up, down, after):
     return pl.pallas_call(
         prepare_kernel,
-        out_shape=(jax.ShapeDtypeStruct((96, D), BF), jax.ShapeDtypeStruct(shard.shape, BF)),
-        in_specs=[vmem()] * 3 + [pl.BlockSpec(memory_space=pl.ANY)],
-        out_specs=(vmem(), vmem()),
+        out_shape=jax.ShapeDtypeStruct((96, D), BF),
+        in_specs=[vmem()] * 2 + [pl.BlockSpec(memory_space=pl.ANY)],
+        out_specs=vmem(),
         cost_estimate=pl.CostEstimate(flops=1 << 33, bytes_accessed=1 << 20, transcendentals=0),
         interpret=INTERPRET,
         name="prepare",
-    )(up, down, shard, after)
+    )(up, down, after)
 
 
 def norm_dispatch_kernel(sum_ref, hid_ref, gain_ref, ids_ref, res_ref, disp_ref):
@@ -438,23 +425,20 @@
     gates = route_gates[0, 0, 0]
 
     send = pack(rotated_queries[0, 0, 0], fresh_key_values[0, 0, 0], cached_key_values[0])
-    packed, shard = prepare(gate_up[0], down_weight[0], output_weight, send)
-    turns = [
-        lax.ppermute(shard, "x", [(n, (n + step) % 4) for n in range(4)]) for step in (1, 2, 3)
-    ]
+    plane_weight = lax.all_gather(output_weight, ("x", "core"), axis=0, tiled=True)
+    packed = prepare(gate_up[0], down_weight[0], send)
     own = lax.all_to_all(send, ("zhi", "core"), split_axis=0, concat_axis=0, tiled=True)
-    turns, packed, own = lax.optimization_barrier((turns, packed, own))
+    packed, own = lax.optimization_barrier((packed, own))
     own_weights = lax.all_gather(packed, "y", axis=0)
     across = lax.ppermute(packed, "zlo", [(0, 1), (1, 0)])
-    own_rows = jnp.stack([shard, *turns], 0)
-    other_rows = lax.ppermute(own_rows, "core", [(0, 1), (1, 0)])
     spread = jnp.broadcast_to(own[None, :, 96:], (4, HKV, 96, 128))
     pairs = lax.all_to_all(spread, "x", split_axis=0, concat_axis=0, tiled=True)
+    pairs, plane_weight = lax.optimization_barrier((pairs, plane_weight))
     kept, sent = attention(info, own, pairs)
-    across, other_rows, sent = lax.optimization_barrier((across, other_rows, sent))
+    across, sent = lax.optimization_barrier((across, sent))
     other_weights = lax.all_gather(across, "y", axis=0)
     swapped = lax.ppermute(sent, "core", [(0, 1), (1, 0)])
-    terms = group_sums(info, kept, swapped, own_rows, other_rows)
+    terms = group_sums(info, kept, swapped, plane_weight)
     sums = lax.all_to_all(terms, "zhi", split_axis=0, concat_axis=0, tiled=True)
     residual, outbound = norm_dispatch(sums, hidden_in[0, 0, 0], norm_gain[None], ids.T)
     slots = lax.all_to_all(outbound, TEN, split_axis=0, concat_axis=0, tiled=True)

time: 214 us -> 216 us (level)
  the two profiles are of different devices: /device:TPU:36 before, /device:TPU:1 now
where the time goes in v8:
time: 216 us; the launch traced here: 215 us
  waiting for transfers between devices  96.4 us (45%)
  starting transfers between devices  60.3 us (28%)
  Pallas kernels  26.6 us (12%)
  local copies, waits for them, and re-layouts  14.6 us (7%)
  between operations  14.6 us (7%)
  other arithmetic  2.48 us (1%)
    all_gather x1, waiting for transfers between devices, shards(): other_weights = lax.all_gather(across, 'y', axis=0)  35.9 us
    all_to_all x1, waiting for transfers between devices, shards(): lax.all_to_all(computed, TEN, split_axis=0, concat_axis=0, tiled=True)  29.6 us
    all_to_all x1, waiting for transfers between devices, shards(): sums = lax.all_to_all(terms, 'zhi', split_axis=0, concat_axis=0, tiled=True)  14.5 us
    all_to_all x1, starting transfers between devices, shards(): lax.all_to_all(computed, TEN, split_axis=0, concat_axis=0, tiled=True)  13.8 us
    all_to_all x1, starting transfers between devices, shards(): lax.all_to_all(outbound, TEN, split_axis=0, concat_axis=0, tiled=True)  12 us
    all_to_all x1, starting transfers between devices, shards(): lax.all_to_all(send, ('zhi', 'core'), split_axis=0, concat_axis=0, tiled=...  11.8 us
    all_to_all x1, waiting for transfers between devices, shards(): lax.all_to_all(send, ('zhi', 'core'), split_axis=0, concat_axis=0, tiled=...  9.77 us
    pallas_call x1, Pallas kernels, expert(): pl.pallas_call(expert_kernel, out_shape=jax.ShapeDtypeStruct((NT, SROWS,...  8.32 us
  transfers between devices with their start and end apart: 11, of which 7 were waited for; matrix products, arithmetic and copies ran while one was open for 5% of the time, Pallas kernels for 8%

profile of v8, /device:TPU:1, one launch (start us, length us, event | category | flops | bytes accessed | tf_op | source)
XLA Modules:
  0.0 214.9 jit_solution(3122869855834470840)
XLA Ops:
  7.9 1.9 pack.1.after_ref
  9.8 11.8 %all-to-all-start = ((bf16[8,192,128]{2,1,0:T(8,128)(2,1)}), bf16[8,192,128]{2,1,0:T(8,128)(2,1)S(1)}, u32[]{:S(2)}, u32[]{:S(2)}) async-start(bf16[8,192,128]{2,1,0:T(8,128)(2,1)} %pack.1.after_ref), calls=%async_computation | async-start | bytes 786432 | tf_op jit(solution)/shard_map/all_to_all | solution.py:430
  21.6 1.7 prepare.1
  23.3 9.8 %all-to-all-done.own_ref = bf16[8,192,128]{2,1,0:T(8,128)(2,1)S(1)} async-done(((bf16[8,192,128]{2,1,0:T(8,128)(2,1)}), bf16[8,192,128]{2,1,0:T(8,128)(2,1)S(1)}, u32[]{:S(2)}, u32[]{:S(2)}) %all-to-all-start) | async-done | bytes 393248 | tf_op jit(solution)/shard_map/all_to_all | solution.py:430
  34.1 4.0 %all-to-all-start.1 = ((bf16[4,8,96,128]{3,2,1,0:T(8,128)(2,1)}), bf16[4,8,96,128]{3,2,1,0:T(8,128)(2,1)S(1)}, u32[]{:S(2)}, u32[]{:S(2)}) async-start(bf16[4,8,96,128]{3,2,1,0:T(8,128)(2,1)} %broadcast_in_dim.27), calls=%async_computation.1 | async-start | bytes 1572864 | tf_op jit(solution)/shard_map/all_to_all | solution.py:435
  38.1 4.8 %collective-permute-start = (bf16[96,1536]{1,0:T(8,128)(2,1)S(1)}, bf16[96,1536]{1,0:T(8,128)(2,1)S(1)}, u32[]{:S(2)}, u32[]{:S(2)}) collective-permute-start(bf16[96,1536]{1,0:T(8,128)(2,1)S(1)} %copy-done.7), channel_id=1, source_target_pairs={{0,32},{32,0},{1,33},{33,1},{2,34},{34,2},{3,35},{35,3},{4,36},{36... | collective-permute-start | bytes 884744 | tf_op jit(solution)/shard_map/ppermute | solution.py:433
  43.7 3.1 %all-to-all-done.1.pair_ref = bf16[4,8,96,128]{3,2,1,0:T(8,128)(2,1)S(1)} async-done(((bf16[4,8,96,128]{3,2,1,0:T(8,128)(2,1)}), bf16[4,8,96,128]{3,2,1,0:T(8,128)(2,1)S(1)}, u32[]{:S(2)}, u32[]{:S(2)}) %all-to-all-start.1) | async-done | bytes 786464 | tf_op jit(solution)/shard_map/all_to_all | solution.py:435
  46.8 6.9 %attention.1 = (bf16[4,128,128]{2,1,0:T(8,128)(2,1)S(1)}, bf16[4,128,128]{2,1,0:T(8,128)(2,1)S(1)}) custom-call(s32[4]{0:T(128)S(1)} %pad_add_fusion.info_ref, bf16[8,192,128]{2,1,0:T(8,128)(2,1)S(1)} %all-to-all-done.own_ref, bf16[4,8,96,128]{3,2,1,0:T(8,128)(2,1)S(1)} %all-to-all-done.1.pair_ref), custom_call_target="tpu_custom_call" | custom-call | flops 1811939328 | bytes 3145728 | tf_op jit(solution)/shard_map/attention/pallas_call | solution.py:135
  53.7 7.1 %collective-permute-start.1 = (bf16[4,128,128]{2,1,0:T(8,128)(2,1)S(1)}, bf16[4,128,128]{2,1,0:T(8,128)(2,1)S(1)}, u32[]{:S(2)}, u32[]{:S(2)}) collective-permute-start(bf16[4,128,128]{2,1,0:T(8,128)(2,1)S(1)} %get-tuple-element.19), channel_id=1, source_target_pairs={{0,1},{1,0},{2,3},{3,2},{4,5},{5,4},{6,7},{7,6},{8,9},{9,8},{10,11... | collective-permute-start | bytes 393224 | tf_op jit(solution)/shard_map/ppermute | solution.py:440
  61.8 2.3 %group_sums.1 = bf16[4,64,1536]{2,1,0:T(8,128)(2,1)} custom-call(s32[4]{0:T(128)S(1)} %pad_add_fusion.info_ref, bf16[4,128,128]{2,1,0:T(8,128)(2,1)S(1)} %get-tuple-element.16.own_ref, bf16[4,128,128]{2,1,0:T(8,128)(2,1)S(1)} %collective-permute-done.1.oth_ref, bf16[384,1536]{1,0:T(8,128)(2,1)S(1)} %copy-done.2), custom_call_target="tpu_custom_call" | custom-call | flops 301989888 | bytes 2097152 | tf_op jit(solution)/shard_map/group_sums/pallas_call | solution.py:180
  64.1 4.5 %all-to-all-start.2 = ((bf16[4,64,1536]{2,1,0:T(8,128)(2,1)}), bf16[4,64,1536]{2,1,0:T(8,128)(2,1)S(1)}, u32[]{:S(2)}, u32[]{:S(2)}) async-start(bf16[4,64,1536]{2,1,0:T(8,128)(2,1)} %group_sums.1), calls=%async_computation.2 | async-start | bytes 1572864 | tf_op jit(solution)/shard_map/all_to_all | solution.py:442
  69.4 14.5 %all-to-all-done.2.sum_ref = bf16[4,64,1536]{2,1,0:T(8,128)(2,1)S(1)} async-done(((bf16[4,64,1536]{2,1,0:T(8,128)(2,1)}), bf16[4,64,1536]{2,1,0:T(8,128)(2,1)S(1)}, u32[]{:S(2)}, u32[]{:S(2)}) %all-to-all-start.2) | async-done | bytes 786464 | tf_op jit(solution)/shard_map/all_to_all | solution.py:442
  83.9 2.6 %norm_dispatch.1 = (f32[64,1536]{1,0:T(8,128)S(1)}, bf16[32,208,128]{2,1,0:T(8,128)(2,1)}) custom-call(bf16[4,64,1536]{2,1,0:T(8,128)(2,1)S(1)} %all-to-all-done.2.sum_ref, bf16[64,1536]{1,0:T(8,128)(2,1)S(1)} %bitcast.37, f32[1,1536]{1,0:T(1,128)S(1)} %broadcast_in_dim.28.gain_ref, s32[8,64]{1,0:T(8,128)S(1)} %bitcast.36), custom_call_target="tpu_custom_call" | custom-call | flops 1073741824 | bytes 4194304 | tf_op jit(solution)/shard_map/norm_dispatch/pallas_call | solution.py:246
  86.5 12.0 %all-to-all-start.3 = ((bf16[32,208,128]{2,1,0:T(8,128)(2,1)}), bf16[32,208,128]{2,1,0:T(8,128)(2,1)}, u32[]{:S(2)}, u32[]{:S(2)}) async-start(bf16[32,208,128]{2,1,0:T(8,128)(2,1)} %get-tuple-element.21), calls=%async_computation.3 | async-start | bytes 3407872 | tf_op jit(solution)/shard_map/all_to_all | solution.py:444
  98.6 35.9 %all-gather.10.cloned.1.call-done = bf16[768,1536]{1,0:T(8,128)(2,1)} async-done(((bf16[96,1536]{1,0:T(8,128)(2,1)}), bf16[768,1536]{1,0:T(8,128)(2,1)}) %all-gather.10.cloned.1.call-update) | async-done | bytes 2359312 | tf_op jit(solution)/shard_map/all_gather | solution.py:439
  134.4 1.7 copy-done
  136.1 1.7 copy-done.1
  138.7 1.6 copy-done.4
  141.5 8.3 %expert.1 = bf16[32,208,128]{2,1,0:T(8,128)(2,1)} custom-call(bf16[32,208,128]{2,1,0:T(8,128)(2,1)} %all-to-all-done.3.in_ref, bf16[1536,1024]{1,0:T(8,128)(2,1)} %copy-done.4, bf16[512,1536]{1,0:T(8,128)(2,1)} %copy-done.5), custom_call_target="tpu_custom_call" | custom-call | flops 2566914048 | bytes 9437184 | tf_op jit(solution)/shard_map/expert/pallas_call | solution.py:341
  149.8 13.8 %all-to-all-start.4 = ((bf16[32,208,128]{2,1,0:T(8,128)(2,1)}), bf16[32,208,128]{2,1,0:T(8,128)(2,1)S(1)}, u32[]{:S(2)}, u32[]{:S(2)}) async-start(bf16[32,208,128]{2,1,0:T(8,128)(2,1)} %expert.1), calls=%async_computation.4 | async-start | bytes 3407872 | tf_op jit(solution)/shard_map/all_to_all | solution.py:446
  166.3 2.1 collective-permute-start.2
  170.9 2.4 %dynamic-slice_select_fusion = bf16[4,8,96,32]{3,2,1,0:T(8,128)(2,1)} fusion(bf16[4,8,96,32]{3,2,1,0:T(8,128)(2,1)} %copy.30, bf16[4,8,96,128]{3,2,1,0:T(8,128)(2,1)S(1)} %all-to-all-done.1.pair_ref, s32[]{:T(128)S(6)} %select_n.35, pred[]{:T(512)S(6)} %eq.5), kind=kLoop, calls=%fused_computation | loop fusion | flops 98304 | bytes 589829 | tf_op jit(solution)/shard_map/jit(_where)/select_n | solution.py:453
  176.8 29.6 %all-to-all-done.4.in_ref = bf16[32,208,128]{2,1,0:T(8,128)(2,1)S(1)} async-done(((bf16[32,208,128]{2,1,0:T(8,128)(2,1)}), bf16[32,208,128]{2,1,0:T(8,128)(2,1)S(1)}, u32[]{:S(2)}, u32[]{:S(2)}) %all-to-all-start.4) | async-done | bytes 1703968 | tf_op jit(solution)/shard_map/all_to_all | solution.py:446
  206.3 2.0 combine.1
  (52 shorter events, 14.1 us)
Async XLA Ops:
  7.2 39.6 %all-gather.6.cloned.1.call-start = ((), (), s32[]{:S(2)}) async-start(), calls=%async_computation.5 | async-start | bytes 1327104 | tf_op jit(solution)/shard_map/all_gather | solution.py:428
  9.8 23.3 %all-to-all-start = ((bf16[8,192,128]{2,1,0:T(8,128)(2,1)}), bf16[8,192,128]{2,1,0:T(8,128)(2,1)S(1)}, u32[]{:S(2)}, u32[]{:S(2)}) async-start(bf16[8,192,128]{2,1,0:T(8,128)(2,1)} %pack.1.after_ref), calls=%async_computation | async-start | bytes 786432 | tf_op jit(solution)/shard_map/all_to_all | solution.py:430
  21.6 77.0 %all-gather.8.cloned.1.call-start = ((), (), s32[]{:S(2)}) async-start(), calls=%async_computation.6 | async-start | bytes 2654208 | tf_op jit(solution)/shard_map/all_gather | solution.py:432
  23.3 14.8 %copy-start.7 = (bf16[96,1536]{1,0:T(8,128)(2,1)S(1)}, bf16[96,1536]{1,0:T(8,128)(2,1)}, u32[]{:S(2)}) copy-start(bf16[96,1536]{1,0:T(8,128)(2,1)} %prepare.1) | copy-start | bytes 884740
  34.1 12.7 %all-to-all-start.1 = ((bf16[4,8,96,128]{3,2,1,0:T(8,128)(2,1)}), bf16[4,8,96,128]{3,2,1,0:T(8,128)(2,1)S(1)}, u32[]{:S(2)}, u32[]{:S(2)}) async-start(bf16[4,8,96,128]{3,2,1,0:T(8,128)(2,1)} %broadcast_in_dim.27), calls=%async_computation.1 | async-start | bytes 1572864 | tf_op jit(solution)/shard_map/all_to_all | solution.py:435
  38.1 15.6 %collective-permute-start = (bf16[96,1536]{1,0:T(8,128)(2,1)S(1)}, bf16[96,1536]{1,0:T(8,128)(2,1)S(1)}, u32[]{:S(2)}, u32[]{:S(2)}) collective-permute-start(bf16[96,1536]{1,0:T(8,128)(2,1)S(1)} %copy-done.7), channel_id=1, source_target_pairs={{0,32},{32,0},{1,33},{33,1},{2,34},{34,2},{3,35},{35,3},{4,36},{36... | collective-permute-start | bytes 884744 | tf_op jit(solution)/shard_map/ppermute | solution.py:433
  46.8 15.0 %copy-start.2 = (bf16[384,1536]{1,0:T(8,128)(2,1)S(1)}, bf16[384,1536]{1,0:T(8,128)(2,1)}, u32[]{:S(2)}) copy-start(bf16[384,1536]{1,0:T(8,128)(2,1)} %all-gather.6.cloned.1.call-done.w) | copy-start | bytes 3538948
  53.7 10.3 %copy-start.8 = (bf16[96,1536]{1,0:T(8,128)(2,1)}, bf16[96,1536]{1,0:T(8,128)(2,1)S(1)}, u32[]{:S(2)}) copy-start(bf16[96,1536]{1,0:T(8,128)(2,1)S(1)} %collective-permute-done) | copy-start | bytes 884740
  53.7 8.0 %collective-permute-start.1 = (bf16[4,128,128]{2,1,0:T(8,128)(2,1)S(1)}, bf16[4,128,128]{2,1,0:T(8,128)(2,1)S(1)}, u32[]{:S(2)}, u32[]{:S(2)}) collective-permute-start(bf16[4,128,128]{2,1,0:T(8,128)(2,1)S(1)} %get-tuple-element.19), channel_id=1, source_target_pairs={{0,1},{1,0},{2,3},{3,2},{4,5},{5,4},{6,7},{7,6},{8,9},{9,8},{10,11... | collective-permute-start | bytes 393224 | tf_op jit(solution)/shard_map/ppermute | solution.py:440
  61.8 7.6 %copy-start.10 = (f32[1536]{0:T(1024)S(1)}, f32[1536]{0:T(1024)}, u32[]{:S(2)}) copy-start(f32[1536]{0:T(1024)} %param.19) | copy-start | bytes 18436
  61.8 22.1 %copy-start.3 = (s32[1,1,1,64,8]{3,4,2,1,0:T(8,128)S(1)}, s32[1,1,1,64,8]{3,4,2,1,0:T(8,128)}, u32[]{:S(2)}) copy-start(s32[1,1,1,64,8]{3,4,2,1,0:T(8,128)} %param.16) | copy-start | bytes 6148
  61.8 22.1 %copy-start.6 = (bf16[1,1,1,64,1536]{4,3,2,1,0:T(8,128)(2,1)S(1)}, bf16[1,1,1,64,1536]{4,3,2,1,0:T(8,128)(2,1)}, u32[]{:S(2)}) copy-start(bf16[1,1,1,64,1536]{4,3,2,1,0:T(8,128)(2,1)} %param.11) | copy-start | bytes 589828
  64.1 19.8 %all-to-all-start.2 = ((bf16[4,64,1536]{2,1,0:T(8,128)(2,1)}), bf16[4,64,1536]{2,1,0:T(8,128)(2,1)S(1)}, u32[]{:S(2)}, u32[]{:S(2)}) async-start(bf16[4,64,1536]{2,1,0:T(8,128)(2,1)} %group_sums.1), calls=%async_computation.2 | async-start | bytes 1572864 | tf_op jit(solution)/shard_map/all_to_all | solution.py:442
  68.6 65.8 %all-gather.10.cloned.1.call-start = ((), (), s32[]{:S(2)}) async-start(), calls=%async_computation.7 | async-start | bytes 2654208 | tf_op jit(solution)/shard_map/all_gather | solution.py:439
  86.5 55.0 %all-to-all-start.3 = ((bf16[32,208,128]{2,1,0:T(8,128)(2,1)}), bf16[32,208,128]{2,1,0:T(8,128)(2,1)}, u32[]{:S(2)}, u32[]{:S(2)}) async-start(bf16[32,208,128]{2,1,0:T(8,128)(2,1)} %get-tuple-element.21), calls=%async_computation.3 | async-start | bytes 3407872 | tf_op jit(solution)/shard_map/all_to_all | solution.py:444
  134.4 1.7 copy-start
  136.1 1.7 copy-start.1
  138.6 1.6 copy-start.4
  140.3 1.2 copy-start.5
  149.8 56.5 %all-to-all-start.4 = ((bf16[32,208,128]{2,1,0:T(8,128)(2,1)}), bf16[32,208,128]{2,1,0:T(8,128)(2,1)S(1)}, u32[]{:S(2)}, u32[]{:S(2)}) async-start(bf16[32,208,128]{2,1,0:T(8,128)(2,1)} %expert.1), calls=%async_computation.4 | async-start | bytes 3407872 | tf_op jit(solution)/shard_map/all_to_all | solution.py:446
  163.6 4.9 %copy-start.11 = (f32[1,1,1,64,8]{3,4,2,1,0:T(8,128)S(1)}, f32[1,1,1,64,8]{3,4,2,1,0:T(8,128)}, u32[]{:S(2)}) copy-start(f32[1,1,1,64,8]{3,4,2,1,0:T(8,128)} %param.17) | copy-start | bytes 6148
  166.3 3.4 %collective-permute-start.2 = (bf16[4,8,96,32]{2,3,1,0:T(8,128)(2,1)S(1)}, bf16[4,8,96,32]{2,3,1,0:T(8,128)(2,1)S(1)}, u32[]{:S(2)}, u32[]{:S(2)}) collective-permute-start(bf16[4,8,96,32]{2,3,1,0:T(8,128)(2,1)S(1)} %copy.29), channel_id=1, source_target_pairs={{0,1},{1,0},{2,3},{3,2},{4,5},{5,4},{6,7},{7,6},{8,9},{9,8},{10,11... | collective-permute-start | bytes 589832 | tf_op jit(solution)/shard_map/ppermute | solution.py:452
  176.8 31.6 %copy-start.9 = (bf16[1,3072,32]{1,2,0:T(8,128)(2,1)}, bf16[1,3072,32]{1,2,0:T(8,128)(2,1)S(1)}, u32[]{:S(2)}) copy-start(bf16[1,3072,32]{1,2,0:T(8,128)(2,1)S(1)} %dynamic_update_slice.4) | copy-start | bytes 589828
Sparse Core Ops, SparseCore 0:
  10.1 35.2 all-gather.5
  47.5 41.6 all-gather.7
  91.3 43.1 all-gather.9

commit v9 on v8

--- a/solution.py
+++ b/solution.py
@@ -266,32 +266,51 @@
     return [stacked[c * NT : (c + 1) * NT, :] for c in range(CH)]
 
 
-def unpack_kernel(info_ref, wo_ref, wx_ref, w1_ref, w2_ref):
+def merge_kernel(info_ref, own_ref, oth_ref, o_ref):
     zlo = info_ref[3]
-    for d in range(2 * wo_ref.shape[0]):
-        src, block = (wo_ref, zlo) if d % 2 == 0 else (wx_ref, 1 - zlo)
-        block = block + d // 2 * 2
-        top = pl.multiple_of(block * 96, 32)
-        w1_ref[pl.ds(top, 64), :] = src[d // 2, 0:64, 0:1024]
-        w1_ref[pl.ds(top + 64, 32), 0:512] = src[d // 2, 0:32, 1024:1536]
-        w1_ref[pl.ds(top + 64, 32), 512:1024] = src[d // 2, 32:64, 1024:1536]
-        w2_ref[pl.ds(pl.multiple_of(block * 32, 32), 32), :] = src[d // 2, 64:96, :]
-
-
-def unpack(info, own_weights, other_weights):
-    blocks = 2 * own_weights.shape[0]
+    o_ref[zlo] = own_ref[...]
+    o_ref[1 - zlo] = oth_ref[...]
+
+
+def merge(info, own, other):
+    return pl.pallas_call(
+        merge_kernel,
+        out_shape=jax.ShapeDtypeStruct((2,) + own.shape, BF),
+        in_specs=[
+            pl.BlockSpec(memory_space=pltpu.SMEM),
+            vmem(),
+            vmem(),
+        ],
+        out_specs=vmem(),
+        cost_estimate=pl.CostEstimate(flops=1 << 33, bytes_accessed=1 << 20, transcendentals=0),
+        interpret=INTERPRET,
+        name="merge",
+    )(info, own, other)
+
+
+def unpack_kernel(src, w1_ref, w2_ref):
+    for d in range(src.shape[0]):
+        top = d * 96
+        w1_ref[top : top + 64, :] = src[d, 0:64, 0:1024]
+        w1_ref[top + 64 : top + 96, 0:512] = src[d, 0:32, 1024:1536]
+        w1_ref[top + 64 : top + 96, 512:1024] = src[d, 32:64, 1024:1536]
+        w2_ref[d * 32 : d * 32 + 32, :] = src[d, 64:96, :]
+
+
+def unpack(weights):
+    blocks = weights.shape[0]
     return pl.pallas_call(
         unpack_kernel,
         out_shape=(
             jax.ShapeDtypeStruct((blocks * 96, 2 * FFE), BF),
             jax.ShapeDtypeStruct((blocks * 32, D), BF),
         ),
-        in_specs=[pl.BlockSpec(memory_space=pltpu.SMEM), vmem(), vmem()],
+        in_specs=[vmem()],
         out_specs=(vmem(), vmem()),
         compiler_params=params(20),
         interpret=INTERPRET,
         name="unpack",
-    )(info, own_weights, other_weights)
+    )(weights)
 
 
 def expert_kernel(in_ref, up_ref, down_ref, o_ref, x, w1, w2, o, sems, out_sems):
@@ -428,21 +447,20 @@
     plane_weight = lax.all_gather(output_weight, ("x", "core"), axis=0, tiled=True)
     packed = prepare(gate_up[0], down_weight[0], send)
     own = lax.all_to_all(send, ("zhi", "core"), split_axis=0, concat_axis=0, tiled=True)
-    packed, own = lax.optimization_barrier((packed, own))
-    own_weights = lax.all_gather(packed, "y", axis=0)
     across = lax.ppermute(packed, "zlo", [(0, 1), (1, 0)])
+    packed, across, own = lax.optimization_barrier((packed, across, own))
+    both = merge(info, packed, across)
     spread = jnp.broadcast_to(own[None, :, 96:], (4, HKV, 96, 128))
     pairs = lax.all_to_all(spread, "x", split_axis=0, concat_axis=0, tiled=True)
-    pairs, plane_weight = lax.optimization_barrier((pairs, plane_weight))
+    pairs, plane_weight, both = lax.optimization_barrier((pairs, plane_weight, both))
+    weights = lax.all_gather(both, "y", axis=0, tiled=True)
     kept, sent = attention(info, own, pairs)
-    across, sent = lax.optimization_barrier((across, sent))
-    other_weights = lax.all_gather(across, "y", axis=0)
     swapped = lax.ppermute(sent, "core", [(0, 1), (1, 0)])
     terms = group_sums(info, kept, swapped, plane_weight)
     sums = lax.all_to_all(terms, "zhi", split_axis=0, concat_axis=0, tiled=True)
     residual, outbound = norm_dispatch(sums, hidden_in[0, 0, 0], norm_gain[None], ids.T)
     slots = lax.all_to_all(outbound, TEN, split_axis=0, concat_axis=0, tiled=True)
-    computed = expert(slots, *unpack(info, own_weights, other_weights))
+    computed = expert(slots, *unpack(weights))
     returned = lax.all_to_all(computed, TEN, split_axis=0, concat_axis=0, tiled=True)
     hidden_out = combine(returned, residual, ids, gates)
 

time: 216 us -> 212 us (0.981)
  the two profiles are of different devices: /device:TPU:1 before, /device:TPU:36 now
where the time goes in v9:
time: 212 us; the launch traced here: 211 us
  waiting for transfers between devices  106 us (50%)
  starting transfers between devices  45.3 us (21%)
  Pallas kernels  28 us (13%)
  between operations  14.9 us (7%)
  local copies, waits for them, and re-layouts  13.8 us (7%)
  other arithmetic  3.06 us (1%)
    all_to_all x1, waiting for transfers between devices, shards(): lax.all_to_all(computed, TEN, split_axis=0, concat_axis=0, tiled=True)  29.7 us
    all_to_all x1, waiting for transfers between devices, shards(): lax.all_to_all(outbound, TEN, split_axis=0, concat_axis=0, tiled=True)  27.1 us
    all_to_all x1, waiting for transfers between devices, shards(): sums = lax.all_to_all(terms, 'zhi', split_axis=0, concat_axis=0, tiled=True)  17 us
    all_to_all x1, starting transfers between devices, shards(): lax.all_to_all(outbound, TEN, split_axis=0, concat_axis=0, tiled=True)  12 us
    ppermute x1, waiting for transfers between devices, shards(): across = lax.ppermute(packed, 'zlo', [(0, 1), (1, 0)])  11.4 us
    all_gather x1, waiting for transfers between devices, shards(): weights = lax.all_gather(both, 'y', axis=0, tiled=True)  10.4 us
    all_to_all x1, starting transfers between devices, shards(): lax.all_to_all(send, ('zhi', 'core'), split_axis=0, concat_axis=0, tiled=...  10.3 us
    pallas_call x1, Pallas kernels, expert(): pl.pallas_call(expert_kernel, out_shape=jax.ShapeDtypeStruct((NT, SROWS,...  8.36 us
  transfers between devices with their start and end apart: 10, of which 8 were waited for; matrix products, arithmetic and copies ran while one was open for 6% of the time, Pallas kernels for 8%

profile of v9, /device:TPU:36, one launch (start us, length us, event | category | flops | bytes accessed | tf_op | source)
XLA Modules:
  0.0 211.4 jit_solution(5445844748304952019)
XLA Ops:
  7.9 1.9 pack.1.after_ref
  9.8 10.3 %all-to-all-start = ((bf16[8,192,128]{2,1,0:T(8,128)(2,1)}), bf16[8,192,128]{2,1,0:T(8,128)(2,1)S(1)}, u32[]{:S(2)}, u32[]{:S(2)}) async-start(bf16[8,192,128]{2,1,0:T(8,128)(2,1)} %pack.1.after_ref), calls=%async_computation | async-start | bytes 786432 | tf_op jit(solution)/shard_map/all_to_all | solution.py:449
  20.1 1.7 prepare.1.own_ref
  21.8 3.4 %collective-permute-start = (bf16[96,1536]{1,0:T(8,128)(2,1)}, bf16[96,1536]{1,0:T(8,128)(2,1)S(1)}, u32[]{:S(2)}, u32[]{:S(2)}) collective-permute-start(bf16[96,1536]{1,0:T(8,128)(2,1)} %prepare.1.own_ref), channel_id=1, source_target_pairs={{0,32},{32,0},{1,33},{33,1},{2,34},{34,2},{3,35},{35,3},{4,36},{36... | collective-permute-start | bytes 884744 | tf_op jit(solution)/shard_map/ppermute | solution.py:450
  26.5 11.4 %collective-permute-done.oth_ref = bf16[96,1536]{1,0:T(8,128)(2,1)S(1)} collective-permute-done((bf16[96,1536]{1,0:T(8,128)(2,1)}, bf16[96,1536]{1,0:T(8,128)(2,1)S(1)}, u32[]{:S(2)}, u32[]{:S(2)}) %collective-permute-start) | collective-permute-done | bytes 294944 | tf_op jit(solution)/shard_map/ppermute | solution.py:450
  38.9 4.8 %all-to-all-start.1 = ((bf16[4,8,96,128]{3,2,1,0:T(8,128)(2,1)}), bf16[4,8,96,128]{3,2,1,0:T(8,128)(2,1)S(1)}, u32[]{:S(2)}, u32[]{:S(2)}) async-start(bf16[4,8,96,128]{3,2,1,0:T(8,128)(2,1)} %broadcast_in_dim.27), calls=%async_computation.1 | async-start | bytes 1572864 | tf_op jit(solution)/shard_map/all_to_all | solution.py:454
  43.7 2.0 merge.1
  45.7 7.4 %all-to-all-done.1.pair_ref = bf16[4,8,96,128]{3,2,1,0:T(8,128)(2,1)S(1)} async-done(((bf16[4,8,96,128]{3,2,1,0:T(8,128)(2,1)}), bf16[4,8,96,128]{3,2,1,0:T(8,128)(2,1)S(1)}, u32[]{:S(2)}, u32[]{:S(2)}) %all-to-all-start.1) | async-done | bytes 786464 | tf_op jit(solution)/shard_map/all_to_all | solution.py:454
  53.2 6.9 %attention.1 = (bf16[4,128,128]{2,1,0:T(8,128)(2,1)S(1)}, bf16[4,128,128]{2,1,0:T(8,128)(2,1)S(1)}) custom-call(s32[4]{0:T(128)S(1)} %copy-done.3, bf16[8,192,128]{2,1,0:T(8,128)(2,1)S(1)} %all-to-all-done.own_ref, bf16[4,8,96,128]{3,2,1,0:T(8,128)(2,1)S(1)} %all-to-all-done.1.pair_ref), custom_call_target="tpu_custom_call" | custom-call | flops 1811939328 | bytes 3145728 | tf_op jit(solution)/shard_map/attention/pallas_call | solution.py:135
  60.1 1.9 collective-permute-start.1
  63.4 2.3 %group_sums.1 = bf16[4,64,1536]{2,1,0:T(8,128)(2,1)} custom-call(s32[4]{0:T(128)S(1)} %copy-done.3, bf16[4,128,128]{2,1,0:T(8,128)(2,1)S(1)} %get-tuple-element.18.own_ref, bf16[4,128,128]{2,1,0:T(8,128)(2,1)S(1)} %collective-permute-done.1.oth_ref, bf16[384,1536]{1,0:T(8,128)(2,1)S(1)} %copy-done.1), custom_call_target="tpu_custom_call" | custom-call | flops 301989888 | bytes 2097152 | tf_op jit(solution)/shard_map/group_sums/pallas_call | solution.py:180
  65.6 5.9 %all-to-all-start.2 = ((bf16[4,64,1536]{2,1,0:T(8,128)(2,1)}), bf16[4,64,1536]{2,1,0:T(8,128)(2,1)S(1)}, u32[]{:S(2)}, u32[]{:S(2)}) async-start(bf16[4,64,1536]{2,1,0:T(8,128)(2,1)} %group_sums.1), calls=%async_computation.2 | async-start | bytes 1572864 | tf_op jit(solution)/shard_map/all_to_all | solution.py:460
  71.5 17.0 %all-to-all-done.2.sum_ref = bf16[4,64,1536]{2,1,0:T(8,128)(2,1)S(1)} async-done(((bf16[4,64,1536]{2,1,0:T(8,128)(2,1)}), bf16[4,64,1536]{2,1,0:T(8,128)(2,1)S(1)}, u32[]{:S(2)}, u32[]{:S(2)}) %all-to-all-start.2) | async-done | bytes 786464 | tf_op jit(solution)/shard_map/all_to_all | solution.py:460
  88.6 2.5 %norm_dispatch.1 = (f32[64,1536]{1,0:T(8,128)S(1)}, bf16[32,208,128]{2,1,0:T(8,128)(2,1)}) custom-call(bf16[4,64,1536]{2,1,0:T(8,128)(2,1)S(1)} %all-to-all-done.2.sum_ref, bf16[64,1536]{1,0:T(8,128)(2,1)S(1)} %bitcast.33, f32[1,1536]{1,0:T(1,128)S(1)} %broadcast_in_dim.28.gain_ref, s32[8,64]{1,0:T(8,128)S(1)} %bitcast.32), custom_call_target="tpu_custom_call" | custom-call | flops 1073741824 | bytes 4194304 | tf_op jit(solution)/shard_map/norm_dispatch/pallas_call | solution.py:246
  91.1 12.0 %all-to-all-start.3 = ((bf16[32,208,128]{2,1,0:T(8,128)(2,1)}), bf16[32,208,128]{2,1,0:T(8,128)(2,1)}, u32[]{:S(2)}, u32[]{:S(2)}) async-start(bf16[32,208,128]{2,1,0:T(8,128)(2,1)} %get-tuple-element.21), calls=%async_computation.3 | async-start | bytes 3407872 | tf_op jit(solution)/shard_map/all_to_all | solution.py:462
  103.1 10.4 %all-gather.5.cloned.1.call-done.src = bf16[16,96,1536]{2,1,0:T(8,128)(2,1)} async-done(((bf16[2,96,1536]{2,1,0:T(8,128)(2,1)}), bf16[16,96,1536]{2,1,0:T(8,128)(2,1)}) %all-gather.5.cloned.1.call-update) | async-done | bytes 4718608 | tf_op jit(solution)/shard_map/all_gather | solution.py:456
  113.6 2.3 %copy-done = bf16[16,96,1536]{2,1,0:T(8,128)(2,1)S(1)} copy-done((bf16[16,96,1536]{2,1,0:T(8,128)(2,1)S(1)}, bf16[16,96,1536]{2,1,0:T(8,128)(2,1)}, u32[]{:S(2)}) %copy-start) | copy-done | bytes 4718616
  119.0 27.1 %all-to-all-done.3.in_ref = bf16[32,208,128]{2,1,0:T(8,128)(2,1)} async-done(((bf16[32,208,128]{2,1,0:T(8,128)(2,1)}), bf16[32,208,128]{2,1,0:T(8,128)(2,1)}, u32[]{:S(2)}, u32[]{:S(2)}) %all-to-all-start.3) | async-done | bytes 1703968 | tf_op jit(solution)/shard_map/all_to_all | solution.py:462
  146.2 8.4 %expert.1 = bf16[32,208,128]{2,1,0:T(8,128)(2,1)} custom-call(bf16[32,208,128]{2,1,0:T(8,128)(2,1)} %all-to-all-done.3.in_ref, bf16[1536,1024]{1,0:T(8,128)(2,1)} %copy-done.4, bf16[512,1536]{1,0:T(8,128)(2,1)} %copy-done.5), custom_call_target="tpu_custom_call" | custom-call | flops 2566914048 | bytes 9437184 | tf_op jit(solution)/shard_map/expert/pallas_call | solution.py:360
  154.5 5.0 %all-to-all-start.4 = ((bf16[32,208,128]{2,1,0:T(8,128)(2,1)}), bf16[32,208,128]{2,1,0:T(8,128)(2,1)S(1)}, u32[]{:S(2)}, u32[]{:S(2)}) async-start(bf16[32,208,128]{2,1,0:T(8,128)(2,1)} %expert.1), calls=%async_computation.4 | async-start | bytes 3407872 | tf_op jit(solution)/shard_map/all_to_all | solution.py:464
  162.2 2.1 collective-permute-start.2
  166.8 2.4 %dynamic-slice_select_fusion = bf16[4,8,96,32]{3,2,1,0:T(8,128)(2,1)} fusion(bf16[4,8,96,32]{3,2,1,0:T(8,128)(2,1)} %copy.30, bf16[4,8,96,128]{3,2,1,0:T(8,128)(2,1)S(1)} %all-to-all-done.1.pair_ref, s32[]{:T(128)S(6)} %select_n.35, pred[]{:T(512)S(6)} %eq.5), kind=kLoop, calls=%fused_computation | loop fusion | flops 98304 | bytes 589829 | tf_op jit(solution)/shard_map/jit(_where)/select_n | solution.py:471
  172.8 29.7 %all-to-all-done.4.in_ref = bf16[32,208,128]{2,1,0:T(8,128)(2,1)S(1)} async-done(((bf16[32,208,128]{2,1,0:T(8,128)(2,1)}), bf16[32,208,128]{2,1,0:T(8,128)(2,1)S(1)}, u32[]{:S(2)}, u32[]{:S(2)}) %all-to-all-start.4) | async-done | bytes 1703968 | tf_op jit(solution)/shard_map/all_to_all | solution.py:464
  202.5 2.0 combine.1
  (48 shorter events, 15.6 us)
Async XLA Ops:
  7.2 46.0 %all-gather.3.cloned.1.call-start = ((), (), s32[]{:S(2)}) async-start(), calls=%async_computation.5 | async-start | bytes 1327104 | tf_op jit(solution)/shard_map/all_gather | solution.py:447
  9.8 28.1 %all-to-all-start = ((bf16[8,192,128]{2,1,0:T(8,128)(2,1)}), bf16[8,192,128]{2,1,0:T(8,128)(2,1)S(1)}, u32[]{:S(2)}, u32[]{:S(2)}) async-start(bf16[8,192,128]{2,1,0:T(8,128)(2,1)} %pack.1.after_ref), calls=%async_computation | async-start | bytes 786432 | tf_op jit(solution)/shard_map/all_to_all | solution.py:449
  21.8 16.1 %collective-permute-start = (bf16[96,1536]{1,0:T(8,128)(2,1)}, bf16[96,1536]{1,0:T(8,128)(2,1)S(1)}, u32[]{:S(2)}, u32[]{:S(2)}) collective-permute-start(bf16[96,1536]{1,0:T(8,128)(2,1)} %prepare.1.own_ref), channel_id=1, source_target_pairs={{0,32},{32,0},{1,33},{33,1},{2,34},{34,2},{3,35},{35,3},{4,36},{36... | collective-permute-start | bytes 884744 | tf_op jit(solution)/shard_map/ppermute | solution.py:450
  37.9 5.8 %copy-start.10 = (bf16[96,1536]{1,0:T(8,128)(2,1)}, bf16[96,1536]{1,0:T(8,128)(2,1)S(1)}, u32[]{:S(2)}) copy-start(bf16[96,1536]{1,0:T(8,128)(2,1)S(1)} %collective-permute-done.oth_ref) | copy-start | bytes 884740
  38.9 14.2 %all-to-all-start.1 = ((bf16[4,8,96,128]{3,2,1,0:T(8,128)(2,1)}), bf16[4,8,96,128]{3,2,1,0:T(8,128)(2,1)S(1)}, u32[]{:S(2)}, u32[]{:S(2)}) async-start(bf16[4,8,96,128]{3,2,1,0:T(8,128)(2,1)} %broadcast_in_dim.27), calls=%async_computation.1 | async-start | bytes 1572864 | tf_op jit(solution)/shard_map/all_to_all | solution.py:454
  43.7 9.4 %copy-start.3 = (s32[4]{0:T(128)S(1)}, s32[4]{0:T(128)}, u32[]{:S(2)}) copy-start(s32[4]{0:T(128)} %pad_add_fusion.info_ref) | copy-start | bytes 52
  43.7 69.8 %all-gather.5.cloned.1.call-start = ((), (), s32[]{:S(2)}) async-start(), calls=%async_computation.6 | async-start | bytes 5308416 | tf_op jit(solution)/shard_map/all_gather | solution.py:456
  53.2 10.2 %copy-start.1 = (bf16[384,1536]{1,0:T(8,128)(2,1)S(1)}, bf16[384,1536]{1,0:T(8,128)(2,1)}, u32[]{:S(2)}) copy-start(bf16[384,1536]{1,0:T(8,128)(2,1)} %all-gather.3.cloned.1.call-done.w) | copy-start | bytes 3538948
  60.1 3.2 %collective-permute-start.1 = (bf16[4,128,128]{2,1,0:T(8,128)(2,1)S(1)}, bf16[4,128,128]{2,1,0:T(8,128)(2,1)S(1)}, u32[]{:S(2)}, u32[]{:S(2)}) collective-permute-start(bf16[4,128,128]{2,1,0:T(8,128)(2,1)S(1)} %get-tuple-element.19), channel_id=1, source_target_pairs={{0,1},{1,0},{2,3},{3,2},{4,5},{5,4},{6,7},{7,6},{8,9},{9,8},{10,11... | collective-permute-start | bytes 393224 | tf_op jit(solution)/shard_map/ppermute | solution.py:458
  63.4 8.2 %copy-start.8 = (f32[1536]{0:T(1024)S(1)}, f32[1536]{0:T(1024)}, u32[]{:S(2)}) copy-start(f32[1536]{0:T(1024)} %param.19) | copy-start | bytes 18436
  63.4 25.2 %copy-start.2 = (s32[1,1,1,64,8]{3,4,2,1,0:T(8,128)S(1)}, s32[1,1,1,64,8]{3,4,2,1,0:T(8,128)}, u32[]{:S(2)}) copy-start(s32[1,1,1,64,8]{3,4,2,1,0:T(8,128)} %param.16) | copy-start | bytes 6148
  63.4 25.2 %copy-start.6 = (bf16[1,1,1,64,1536]{4,3,2,1,0:T(8,128)(2,1)S(1)}, bf16[1,1,1,64,1536]{4,3,2,1,0:T(8,128)(2,1)}, u32[]{:S(2)}) copy-start(bf16[1,1,1,64,1536]{4,3,2,1,0:T(8,128)(2,1)} %param.11) | copy-start | bytes 589828
  65.6 22.9 %all-to-all-start.2 = ((bf16[4,64,1536]{2,1,0:T(8,128)(2,1)}), bf16[4,64,1536]{2,1,0:T(8,128)(2,1)S(1)}, u32[]{:S(2)}, u32[]{:S(2)}) async-start(bf16[4,64,1536]{2,1,0:T(8,128)(2,1)} %group_sums.1), calls=%async_computation.2 | async-start | bytes 1572864 | tf_op jit(solution)/shard_map/all_to_all | solution.py:460
  91.1 55.0 %all-to-all-start.3 = ((bf16[32,208,128]{2,1,0:T(8,128)(2,1)}), bf16[32,208,128]{2,1,0:T(8,128)(2,1)}, u32[]{:S(2)}, u32[]{:S(2)}) async-start(bf16[32,208,128]{2,1,0:T(8,128)(2,1)} %get-tuple-element.21), calls=%async_computation.3 | async-start | bytes 3407872 | tf_op jit(solution)/shard_map/all_to_all | solution.py:462
  113.6 2.3 %copy-start = (bf16[16,96,1536]{2,1,0:T(8,128)(2,1)S(1)}, bf16[16,96,1536]{2,1,0:T(8,128)(2,1)}, u32[]{:S(2)}) copy-start(bf16[16,96,1536]{2,1,0:T(8,128)(2,1)} %all-gather.5.cloned.1.call-done.src) | copy-start | bytes 14155780
  116.2 1.6 copy-start.4
  117.8 1.2 copy-start.5
  154.5 48.0 %all-to-all-start.4 = ((bf16[32,208,128]{2,1,0:T(8,128)(2,1)}), bf16[32,208,128]{2,1,0:T(8,128)(2,1)S(1)}, u32[]{:S(2)}, u32[]{:S(2)}) async-start(bf16[32,208,128]{2,1,0:T(8,128)(2,1)} %expert.1), calls=%async_computation.4 | async-start | bytes 3407872 | tf_op jit(solution)/shard_map/all_to_all | solution.py:464
  159.5 4.8 %copy-start.9 = (f32[1,1,1,64,8]{3,4,2,1,0:T(8,128)S(1)}, f32[1,1,1,64,8]{3,4,2,1,0:T(8,128)}, u32[]{:S(2)}) copy-start(f32[1,1,1,64,8]{3,4,2,1,0:T(8,128)} %param.17) | copy-start | bytes 6148
  162.2 3.4 %collective-permute-start.2 = (bf16[4,8,96,32]{2,3,1,0:T(8,128)(2,1)S(1)}, bf16[4,8,96,32]{2,3,1,0:T(8,128)(2,1)S(1)}, u32[]{:S(2)}, u32[]{:S(2)}) collective-permute-start(bf16[4,8,96,32]{2,3,1,0:T(8,128)(2,1)S(1)} %copy.29), channel_id=1, source_target_pairs={{0,1},{1,0},{2,3},{3,2},{4,5},{5,4},{6,7},{7,6},{8,9},{9,8},{10,11... | collective-permute-start | bytes 589832 | tf_op jit(solution)/shard_map/ppermute | solution.py:470
  172.8 31.7 %copy-start.7 = (bf16[1,3072,32]{1,2,0:T(8,128)(2,1)}, bf16[1,3072,32]{1,2,0:T(8,128)(2,1)S(1)}, u32[]{:S(2)}) copy-start(bf16[1,3072,32]{1,2,0:T(8,128)(2,1)S(1)} %dynamic_update_slice.4) | copy-start | bytes 589828
Sparse Core Ops, SparseCore 0:
  10.1 31.8 all-gather.2
  53.3 60.2 all-gather.4

commit v10 on v9

--- a/solution.py
+++ b/solution.py
@@ -447,8 +447,8 @@
     plane_weight = lax.all_gather(output_weight, ("x", "core"), axis=0, tiled=True)
     packed = prepare(gate_up[0], down_weight[0], send)
     own = lax.all_to_all(send, ("zhi", "core"), split_axis=0, concat_axis=0, tiled=True)
+    packed, own = lax.optimization_barrier((packed, own))
     across = lax.ppermute(packed, "zlo", [(0, 1), (1, 0)])
-    packed, across, own = lax.optimization_barrier((packed, across, own))
     both = merge(info, packed, across)
     spread = jnp.broadcast_to(own[None, :, 96:], (4, HKV, 96, 128))
     pairs = lax.all_to_all(spread, "x", split_axis=0, concat_axis=0, tiled=True)

time: 212 us -> 211 us (level)
  the two profiles are of different devices: /device:TPU:36 before, /device:TPU:1 now
where the time goes in v10:
time: 211 us
  waiting for transfers between devices  107 us (51%)
  starting transfers between devices  43.9 us (21%)
  Pallas kernels  28 us (13%)
  between operations  14.9 us (7%)
  local copies, waits for them, and re-layouts  14.3 us (7%)
  other arithmetic  3.06 us (1%)
    all_to_all x1, waiting for transfers between devices, shards(): lax.all_to_all(computed, TEN, split_axis=0, concat_axis=0, tiled=True)  29.1 us
    all_to_all x1, waiting for transfers between devices, shards(): lax.all_to_all(outbound, TEN, split_axis=0, concat_axis=0, tiled=True)  25.6 us
    all_to_all x1, waiting for transfers between devices, shards(): sums = lax.all_to_all(terms, 'zhi', split_axis=0, concat_axis=0, tiled=True)  20.4 us
    all_to_all x1, starting transfers between devices, shards(): lax.all_to_all(send, ('zhi', 'core'), split_axis=0, concat_axis=0, tiled=...  11.8 us
    all_gather x1, waiting for transfers between devices, shards(): weights = lax.all_gather(both, 'y', axis=0, tiled=True)  11.7 us
    all_to_all x1, waiting for transfers between devices, shards(): lax.all_to_all(send, ('zhi', 'core'), split_axis=0, concat_axis=0, tiled=...  9.8 us
    pallas_call x1, Pallas kernels, expert(): pl.pallas_call(expert_kernel, out_shape=jax.ShapeDtypeStruct((NT, SROWS,...  8.35 us
    all_to_all x1, waiting for transfers between devices, shards(): pairs = lax.all_to_all(spread, 'x', split_axis=0, concat_axis=0, tiled=True)  7.22 us
  transfers between devices with their start and end apart: 10, of which 8 were waited for; matrix products, arithmetic and copies ran while one was open for 5% of the time, Pallas kernels for 8%

profile of v10, /device:TPU:1, one launch (start us, length us, event | category | flops | bytes accessed | tf_op | source)
XLA Modules:
  0.0 210.6 jit_solution(11828665170245218776)
XLA Ops:
  7.9 1.9 pack.1.after_ref
  9.8 11.8 %all-to-all-start = ((bf16[8,192,128]{2,1,0:T(8,128)(2,1)}), bf16[8,192,128]{2,1,0:T(8,128)(2,1)S(1)}, u32[]{:S(2)}, u32[]{:S(2)}) async-start(bf16[8,192,128]{2,1,0:T(8,128)(2,1)} %pack.1.after_ref), calls=%async_computation | async-start | bytes 786432 | tf_op jit(solution)/shard_map/all_to_all | solution.py:449
  21.6 1.7 prepare.1.own_ref
  23.3 9.8 %all-to-all-done.own_ref = bf16[8,192,128]{2,1,0:T(8,128)(2,1)S(1)} async-done(((bf16[8,192,128]{2,1,0:T(8,128)(2,1)}), bf16[8,192,128]{2,1,0:T(8,128)(2,1)S(1)}, u32[]{:S(2)}, u32[]{:S(2)}) %all-to-all-start) | async-done | bytes 393248 | tf_op jit(solution)/shard_map/all_to_all | solution.py:449
  33.1 4.8 %collective-permute-start = (bf16[96,1536]{1,0:T(8,128)(2,1)}, bf16[96,1536]{1,0:T(8,128)(2,1)S(1)}, u32[]{:S(2)}, u32[]{:S(2)}) collective-permute-start(bf16[96,1536]{1,0:T(8,128)(2,1)} %prepare.1.own_ref), channel_id=1, source_target_pairs={{0,32},{32,0},{1,33},{33,1},{2,34},{34,2},{3,35},{35,3},{4,36},{36... | collective-permute-start | bytes 884744 | tf_op jit(solution)/shard_map/ppermute | solution.py:451
  40.2 4.0 %all-to-all-start.1 = ((bf16[4,8,96,128]{3,2,1,0:T(8,128)(2,1)}), bf16[4,8,96,128]{3,2,1,0:T(8,128)(2,1)S(1)}, u32[]{:S(2)}, u32[]{:S(2)}) async-start(bf16[4,8,96,128]{3,2,1,0:T(8,128)(2,1)} %broadcast_in_dim.27), calls=%async_computation.1 | async-start | bytes 1572864 | tf_op jit(solution)/shard_map/all_to_all | solution.py:454
  45.0 2.0 merge.1
  47.0 7.2 %all-to-all-done.1.pair_ref = bf16[4,8,96,128]{3,2,1,0:T(8,128)(2,1)S(1)} async-done(((bf16[4,8,96,128]{3,2,1,0:T(8,128)(2,1)}), bf16[4,8,96,128]{3,2,1,0:T(8,128)(2,1)S(1)}, u32[]{:S(2)}, u32[]{:S(2)}) %all-to-all-start.1) | async-done | bytes 786464 | tf_op jit(solution)/shard_map/all_to_all | solution.py:454
  54.2 6.9 %attention.1 = (bf16[4,128,128]{2,1,0:T(8,128)(2,1)S(1)}, bf16[4,128,128]{2,1,0:T(8,128)(2,1)S(1)}) custom-call(s32[4]{0:T(128)S(1)} %copy-done.3, bf16[8,192,128]{2,1,0:T(8,128)(2,1)S(1)} %all-to-all-done.own_ref, bf16[4,8,96,128]{3,2,1,0:T(8,128)(2,1)S(1)} %all-to-all-done.1.pair_ref), custom_call_target="tpu_custom_call" | custom-call | flops 1811939328 | bytes 3145728 | tf_op jit(solution)/shard_map/attention/pallas_call | solution.py:135
  61.1 5.2 %collective-permute-start.1 = (bf16[4,128,128]{2,1,0:T(8,128)(2,1)S(1)}, bf16[4,128,128]{2,1,0:T(8,128)(2,1)S(1)}, u32[]{:S(2)}, u32[]{:S(2)}) collective-permute-start(bf16[4,128,128]{2,1,0:T(8,128)(2,1)S(1)} %get-tuple-element.17), channel_id=1, source_target_pairs={{0,1},{1,0},{2,3},{3,2},{4,5},{5,4},{6,7},{7,6},{8,9},{9,8},{10,11... | collective-permute-start | bytes 393224 | tf_op jit(solution)/shard_map/ppermute | solution.py:458
  67.3 2.3 %group_sums.1 = bf16[4,64,1536]{2,1,0:T(8,128)(2,1)} custom-call(s32[4]{0:T(128)S(1)} %copy-done.3, bf16[4,128,128]{2,1,0:T(8,128)(2,1)S(1)} %get-tuple-element.16.own_ref, bf16[4,128,128]{2,1,0:T(8,128)(2,1)S(1)} %collective-permute-done.1.oth_ref, bf16[384,1536]{1,0:T(8,128)(2,1)S(1)} %copy-done.1), custom_call_target="tpu_custom_call" | custom-call | flops 301989888 | bytes 2097152 | tf_op jit(solution)/shard_map/group_sums/pallas_call | solution.py:180
  69.6 3.5 %all-to-all-start.2 = ((bf16[4,64,1536]{2,1,0:T(8,128)(2,1)}), bf16[4,64,1536]{2,1,0:T(8,128)(2,1)S(1)}, u32[]{:S(2)}, u32[]{:S(2)}) async-start(bf16[4,64,1536]{2,1,0:T(8,128)(2,1)} %group_sums.1), calls=%async_computation.2 | async-start | bytes 1572864 | tf_op jit(solution)/shard_map/all_to_all | solution.py:460
  73.1 20.4 %all-to-all-done.2.sum_ref = bf16[4,64,1536]{2,1,0:T(8,128)(2,1)S(1)} async-done(((bf16[4,64,1536]{2,1,0:T(8,128)(2,1)}), bf16[4,64,1536]{2,1,0:T(8,128)(2,1)S(1)}, u32[]{:S(2)}, u32[]{:S(2)}) %all-to-all-start.2) | async-done | bytes 786464 | tf_op jit(solution)/shard_map/all_to_all | solution.py:460
  93.5 2.5 %norm_dispatch.1 = (f32[64,1536]{1,0:T(8,128)S(1)}, bf16[32,208,128]{2,1,0:T(8,128)(2,1)}) custom-call(bf16[4,64,1536]{2,1,0:T(8,128)(2,1)S(1)} %all-to-all-done.2.sum_ref, bf16[64,1536]{1,0:T(8,128)(2,1)S(1)} %bitcast.33, f32[1,1536]{1,0:T(1,128)S(1)} %broadcast_in_dim.28.gain_ref, s32[8,64]{1,0:T(8,128)S(1)} %bitcast.32), custom_call_target="tpu_custom_call" | custom-call | flops 1073741824 | bytes 4194304 | tf_op jit(solution)/shard_map/norm_dispatch/pallas_call | solution.py:246
  96.1 6.2 %all-to-all-start.3 = ((bf16[32,208,128]{2,1,0:T(8,128)(2,1)}), bf16[32,208,128]{2,1,0:T(8,128)(2,1)}, u32[]{:S(2)}, u32[]{:S(2)}) async-start(bf16[32,208,128]{2,1,0:T(8,128)(2,1)} %get-tuple-element.19), calls=%async_computation.3 | async-start | bytes 3407872 | tf_op jit(solution)/shard_map/all_to_all | solution.py:462
  102.3 11.7 %all-gather.5.cloned.1.call-done.src = bf16[16,96,1536]{2,1,0:T(8,128)(2,1)} async-done(((bf16[2,96,1536]{2,1,0:T(8,128)(2,1)}), bf16[16,96,1536]{2,1,0:T(8,128)(2,1)}) %all-gather.5.cloned.1.call-update) | async-done | bytes 4718608 | tf_op jit(solution)/shard_map/all_gather | solution.py:456
  114.0 2.3 %copy-done = bf16[16,96,1536]{2,1,0:T(8,128)(2,1)S(1)} copy-done((bf16[16,96,1536]{2,1,0:T(8,128)(2,1)S(1)}, bf16[16,96,1536]{2,1,0:T(8,128)(2,1)}, u32[]{:S(2)}) %copy-start) | copy-done | bytes 4718616
  119.5 25.6 %all-to-all-done.3.in_ref = bf16[32,208,128]{2,1,0:T(8,128)(2,1)} async-done(((bf16[32,208,128]{2,1,0:T(8,128)(2,1)}), bf16[32,208,128]{2,1,0:T(8,128)(2,1)}, u32[]{:S(2)}, u32[]{:S(2)}) %all-to-all-start.3) | async-done | bytes 1703968 | tf_op jit(solution)/shard_map/all_to_all | solution.py:462
  145.0 8.4 %expert.1 = bf16[32,208,128]{2,1,0:T(8,128)(2,1)} custom-call(bf16[32,208,128]{2,1,0:T(8,128)(2,1)} %all-to-all-done.3.in_ref, bf16[1536,1024]{1,0:T(8,128)(2,1)} %copy-done.4, bf16[512,1536]{1,0:T(8,128)(2,1)} %copy-done.5), custom_call_target="tpu_custom_call" | custom-call | flops 2566914048 | bytes 9437184 | tf_op jit(solution)/shard_map/expert/pallas_call | solution.py:360
  153.4 6.1 %all-to-all-start.4 = ((bf16[32,208,128]{2,1,0:T(8,128)(2,1)}), bf16[32,208,128]{2,1,0:T(8,128)(2,1)S(1)}, u32[]{:S(2)}, u32[]{:S(2)}) async-start(bf16[32,208,128]{2,1,0:T(8,128)(2,1)} %expert.1), calls=%async_computation.4 | async-start | bytes 3407872 | tf_op jit(solution)/shard_map/all_to_all | solution.py:464
  162.1 2.1 %collective-permute-start.2 = (bf16[4,8,96,32]{2,3,1,0:T(8,128)(2,1)S(1)}, bf16[4,8,96,32]{2,3,1,0:T(8,128)(2,1)S(1)}, u32[]{:S(2)}, u32[]{:S(2)}) collective-permute-start(bf16[4,8,96,32]{2,3,1,0:T(8,128)(2,1)S(1)} %copy.29), channel_id=1, source_target_pairs={{0,1},{1,0},{2,3},{3,2},{4,5},{5,4},{6,7},{7,6},{8,9},{9,8},{10,11... | collective-permute-start | bytes 589832 | tf_op jit(solution)/shard_map/ppermute | solution.py:470
  166.7 2.4 %dynamic-slice_select_fusion = bf16[4,8,96,32]{3,2,1,0:T(8,128)(2,1)} fusion(bf16[4,8,96,32]{3,2,1,0:T(8,128)(2,1)} %copy.30, bf16[4,8,96,128]{3,2,1,0:T(8,128)(2,1)S(1)} %all-to-all-done.1.pair_ref, s32[]{:T(128)S(6)} %select_n.35, pred[]{:T(512)S(6)} %eq.5), kind=kLoop, calls=%fused_computation | loop fusion | flops 98304 | bytes 589829 | tf_op jit(solution)/shard_map/jit(_where)/select_n | solution.py:471
  172.6 29.1 %all-to-all-done.4.in_ref = bf16[32,208,128]{2,1,0:T(8,128)(2,1)S(1)} async-done(((bf16[32,208,128]{2,1,0:T(8,128)(2,1)}), bf16[32,208,128]{2,1,0:T(8,128)(2,1)S(1)}, u32[]{:S(2)}, u32[]{:S(2)}) %all-to-all-start.4) | async-done | bytes 1703968 | tf_op jit(solution)/shard_map/all_to_all | solution.py:464
  201.8 2.0 combine.1
  (48 shorter events, 15.8 us)
Async XLA Ops:
  7.2 47.0 %all-gather.3.cloned.1.call-start = ((), (), s32[]{:S(2)}) async-start(), calls=%async_computation.5 | async-start | bytes 1327104 | tf_op jit(solution)/shard_map/all_gather | solution.py:447
  9.8 23.3 %all-to-all-start = ((bf16[8,192,128]{2,1,0:T(8,128)(2,1)}), bf16[8,192,128]{2,1,0:T(8,128)(2,1)S(1)}, u32[]{:S(2)}, u32[]{:S(2)}) async-start(bf16[8,192,128]{2,1,0:T(8,128)(2,1)} %pack.1.after_ref), calls=%async_computation | async-start | bytes 786432 | tf_op jit(solution)/shard_map/all_to_all | solution.py:449
  33.1 11.2 %collective-permute-start = (bf16[96,1536]{1,0:T(8,128)(2,1)}, bf16[96,1536]{1,0:T(8,128)(2,1)S(1)}, u32[]{:S(2)}, u32[]{:S(2)}) collective-permute-start(bf16[96,1536]{1,0:T(8,128)(2,1)} %prepare.1.own_ref), channel_id=1, source_target_pairs={{0,32},{32,0},{1,33},{33,1},{2,34},{34,2},{3,35},{35,3},{4,36},{36... | collective-permute-start | bytes 884744 | tf_op jit(solution)/shard_map/ppermute | solution.py:451
  40.2 13.9 %all-to-all-start.1 = ((bf16[4,8,96,128]{3,2,1,0:T(8,128)(2,1)}), bf16[4,8,96,128]{3,2,1,0:T(8,128)(2,1)S(1)}, u32[]{:S(2)}, u32[]{:S(2)}) async-start(bf16[4,8,96,128]{3,2,1,0:T(8,128)(2,1)} %broadcast_in_dim.27), calls=%async_computation.1 | async-start | bytes 1572864 | tf_op jit(solution)/shard_map/all_to_all | solution.py:454
  44.2 10.0 %copy-start.3 = (s32[4]{0:T(128)S(1)}, s32[4]{0:T(128)}, u32[]{:S(2)}) copy-start(s32[4]{0:T(128)} %pad_add_fusion.info_ref) | copy-start | bytes 52
  44.2 69.7 %all-gather.5.cloned.1.call-start = ((), (), s32[]{:S(2)}) async-start(), calls=%async_computation.6 | async-start | bytes 5308416 | tf_op jit(solution)/shard_map/all_gather | solution.py:456
  44.3 0.7 copy-start.10
  54.2 13.1 %copy-start.1 = (bf16[384,1536]{1,0:T(8,128)(2,1)S(1)}, bf16[384,1536]{1,0:T(8,128)(2,1)}, u32[]{:S(2)}) copy-start(bf16[384,1536]{1,0:T(8,128)(2,1)} %all-gather.3.cloned.1.call-done.w) | copy-start | bytes 3538948
  61.1 6.2 %collective-permute-start.1 = (bf16[4,128,128]{2,1,0:T(8,128)(2,1)S(1)}, bf16[4,128,128]{2,1,0:T(8,128)(2,1)S(1)}, u32[]{:S(2)}, u32[]{:S(2)}) collective-permute-start(bf16[4,128,128]{2,1,0:T(8,128)(2,1)S(1)} %get-tuple-element.17), channel_id=1, source_target_pairs={{0,1},{1,0},{2,3},{3,2},{4,5},{5,4},{6,7},{7,6},{8,9},{9,8},{10,11... | collective-permute-start | bytes 393224 | tf_op jit(solution)/shard_map/ppermute | solution.py:458
  67.3 5.8 %copy-start.8 = (f32[1536]{0:T(1024)S(1)}, f32[1536]{0:T(1024)}, u32[]{:S(2)}) copy-start(f32[1536]{0:T(1024)} %param.19) | copy-start | bytes 18436
  67.3 26.2 %copy-start.2 = (s32[1,1,1,64,8]{3,4,2,1,0:T(8,128)S(1)}, s32[1,1,1,64,8]{3,4,2,1,0:T(8,128)}, u32[]{:S(2)}) copy-start(s32[1,1,1,64,8]{3,4,2,1,0:T(8,128)} %param.16) | copy-start | bytes 6148
  67.3 26.2 %copy-start.6 = (bf16[1,1,1,64,1536]{4,3,2,1,0:T(8,128)(2,1)S(1)}, bf16[1,1,1,64,1536]{4,3,2,1,0:T(8,128)(2,1)}, u32[]{:S(2)}) copy-start(bf16[1,1,1,64,1536]{4,3,2,1,0:T(8,128)(2,1)} %param.11) | copy-start | bytes 589828
  69.6 23.9 %all-to-all-start.2 = ((bf16[4,64,1536]{2,1,0:T(8,128)(2,1)}), bf16[4,64,1536]{2,1,0:T(8,128)(2,1)S(1)}, u32[]{:S(2)}, u32[]{:S(2)}) async-start(bf16[4,64,1536]{2,1,0:T(8,128)(2,1)} %group_sums.1), calls=%async_computation.2 | async-start | bytes 1572864 | tf_op jit(solution)/shard_map/all_to_all | solution.py:460
  96.1 49.0 %all-to-all-start.3 = ((bf16[32,208,128]{2,1,0:T(8,128)(2,1)}), bf16[32,208,128]{2,1,0:T(8,128)(2,1)}, u32[]{:S(2)}, u32[]{:S(2)}) async-start(bf16[32,208,128]{2,1,0:T(8,128)(2,1)} %get-tuple-element.19), calls=%async_computation.3 | async-start | bytes 3407872 | tf_op jit(solution)/shard_map/all_to_all | solution.py:462
  114.0 2.3 %copy-start = (bf16[16,96,1536]{2,1,0:T(8,128)(2,1)S(1)}, bf16[16,96,1536]{2,1,0:T(8,128)(2,1)}, u32[]{:S(2)}) copy-start(bf16[16,96,1536]{2,1,0:T(8,128)(2,1)} %all-gather.5.cloned.1.call-done.src) | copy-start | bytes 14155780
  116.6 1.6 copy-start.4
  118.3 1.2 copy-start.5
  153.4 48.4 %all-to-all-start.4 = ((bf16[32,208,128]{2,1,0:T(8,128)(2,1)}), bf16[32,208,128]{2,1,0:T(8,128)(2,1)S(1)}, u32[]{:S(2)}, u32[]{:S(2)}) async-start(bf16[32,208,128]{2,1,0:T(8,128)(2,1)} %expert.1), calls=%async_computation.4 | async-start | bytes 3407872 | tf_op jit(solution)/shard_map/all_to_all | solution.py:464
  159.5 4.9 %copy-start.9 = (f32[1,1,1,64,8]{3,4,2,1,0:T(8,128)S(1)}, f32[1,1,1,64,8]{3,4,2,1,0:T(8,128)}, u32[]{:S(2)}) copy-start(f32[1,1,1,64,8]{3,4,2,1,0:T(8,128)} %param.17) | copy-start | bytes 6148
  162.1 3.4 %collective-permute-start.2 = (bf16[4,8,96,32]{2,3,1,0:T(8,128)(2,1)S(1)}, bf16[4,8,96,32]{2,3,1,0:T(8,128)(2,1)S(1)}, u32[]{:S(2)}, u32[]{:S(2)}) collective-permute-start(bf16[4,8,96,32]{2,3,1,0:T(8,128)(2,1)S(1)} %copy.29), channel_id=1, source_target_pairs={{0,1},{1,0},{2,3},{3,2},{4,5},{5,4},{6,7},{7,6},{8,9},{9,8},{10,11... | collective-permute-start | bytes 589832 | tf_op jit(solution)/shard_map/ppermute | solution.py:470
  172.6 31.2 %copy-start.7 = (bf16[1,3072,32]{1,2,0:T(8,128)(2,1)}, bf16[1,3072,32]{1,2,0:T(8,128)(2,1)S(1)}, u32[]{:S(2)}) copy-start(bf16[1,3072,32]{1,2,0:T(8,128)(2,1)S(1)} %dynamic_update_slice.4) | copy-start | bytes 589828
Sparse Core Ops, SparseCore 0:
  10.1 35.0 all-gather.2
  54.3 59.6 all-gather.4
